TPU v7x, 32 devices: a whole 2x2x4 slice. The times are simulated.
32 devices in a mesh: groups: 2 (over x), cols: 16 (over z, y, core).
Axes of the slice: x: 2, y: 2, z: 4, core: 2. Of those that a mesh axis runs over, the one named last changes fastest.
Arguments:
- clip_tokens: bfloat16 [14, 32, 64, 512], P('groups', None, 'cols'), parts along dimension 0, may hold values from -6 to 6
- cotangent: bfloat16 [14, 32, 64, 512], P('groups', None, 'cols'), parts along dimension 0, may hold values from -6 to 6
- gain_attn: float32 [512], replicated, may hold values from 0.25 to 1.75
- w_query: bfloat16 [512, 512], replicated, may hold values from -0.25 to 0.25
- w_key: bfloat16 [512, 512], replicated, may hold values from -0.25 to 0.25
- w_value: bfloat16 [512, 512], replicated, may hold values from -0.25 to 0.25
- w_out: bfloat16 [512, 512], replicated, may hold values from -0.25 to 0.25
- gain_first: float32 [512], replicated, may hold values from 0.25 to 1.75
- conv_first: bfloat16 [3, 3, 512, 512], replicated, may hold values from -0.09375 to 0.09375
- gain_second: float32 [512], replicated, may hold values from 0.25 to 1.75
- conv_second: bfloat16 [3, 3, 512, 512], replicated, may hold values from -0.09375 to 0.09375
- matching: int32 [7], replicated, may hold values from 0 to 6, as said below
- block_lists: int32 [7, 16, 2], replicated, may hold values from 0 to 15, as said below
- counts: int32 [7, 16], replicated, may hold values from 1 to 2
Outputs:
- result: bfloat16 [14, 32, 64, 512], P('groups', None, 'cols'), parts along dimension 0
- d_clip: bfloat16 [14, 32, 64, 512], P('groups', None, 'cols'), parts along dimension 0
There are 2 independent parts, one for each index of `groups`. A program takes and returns all parts, laid end to end along the dimension named above; an argument that names none is the same for every part. Nothing has to cross between parts.
Inputs may be any that keep to these rules, and one draw needn't show every extreme that they name: `matching`: each camera's partner is another camera, and every camera is the partner of exactly one camera. At one tile column j, the 14 entries block_lists[c, j, s] over all cameras c and slots s are pairwise distinct.
All inputs are finite; a program needn't handle non-finite values.
Results may differ from a plain program's by a relative error of at most 0.0075.
Values may be sent and summed in bfloat16 or wider, within the bound.
No kernel may reach another device: no remote copies, remote signals or barrier semaphores. Data moves between devices by JAX's collectives and lax.ppermute only.
A program may use at most 320 MiB of HBM per device.

v0:
```python
import jax
import jax.numpy as jnp
from jax import lax
from jax.sharding import PartitionSpec as P

HEADS = 8


EPSILON = 1e-06
CONTRACT_LAST = (((1,), (1,)), ((), ()))


def padded_2(shard, sides, width):
    for axis, dim in sides:
        size, length = (lax.axis_size(axis), shard.shape[dim])
        up = [(i, (i + 1) % size) for i in range(size - 1)]
        down = [(j, i) for i, j in up]
        last = lax.slice_in_dim(shard, length - width, length, axis=dim)
        first = lax.slice_in_dim(shard, 0, width, axis=dim)
        before = lax.ppermute(last, axis, up)
        after = lax.ppermute(first, axis, down)
        shard = jnp.concatenate([before, shard, after], axis=dim)
    return shard


def row_norm(values, gain_vec):
    inv_rms = lax.rsqrt(jnp.mean(values * values, axis=-1, keepdims=True) + EPSILON)
    return (values * inv_rms * gain_vec, inv_rms)


def norm_back(gradient, values, inv_rms, gain_vec):
    weighted = gradient * gain_vec
    cubed = inv_rms * inv_rms * inv_rms
    return inv_rms * weighted - values * cubed * jnp.mean(weighted * values, axis=-1, keepdims=True)


def silu_slope(inputs):
    sigmoid = jax.nn.sigmoid(inputs)
    return sigmoid * (1.0 + inputs * (1.0 - sigmoid))


def head_product(tokens, weight):
    product = jnp.dot(tokens, weight, preferred_element_type=jnp.float32)
    return product.reshape(product.shape[0], HEADS, -1)


def transposed_product(tokens, weight):
    return lax.dot_general(tokens, weight, CONTRACT_LAST, preferred_element_type=jnp.float32)


def row_share(grad_pairs, key_pre_rows, key_inv_rows, w_key, w_value):
    model_width = w_key.shape[0]
    head_size = model_width // HEADS
    key_grad = grad_pairs[..., :model_width].astype(jnp.float32).reshape(-1, HEADS, head_size)
    listed_keys = norm_back(
        key_grad,
        key_pre_rows.reshape(-1, HEADS, head_size),
        key_inv_rows.reshape(-1, HEADS, 1),
        1.0,
    )
    share = transposed_product(listed_keys.reshape(-1, model_width).astype(jnp.bfloat16), w_key)
    share = share + transposed_product(
        grad_pairs[..., model_width:].reshape(-1, model_width), w_value
    )
    return share.astype(jnp.bfloat16)


def conv_forward(activation, kernel):
    view_count, row_count, tile_width, model_width = activation.shape
    padded = padded_2(activation, (("cols", 2),), 1)
    padded = jnp.pad(padded, ((0, 0), (1, 1), (0, 0), (0, 0)))
    summed = jnp.zeros((view_count * row_count * tile_width, kernel.shape[3]), jnp.float32)
    for vertical in range(3):
        for across in range(3):
            window = padded[
                :, vertical : vertical + row_count, across : across + tile_width, :
            ].reshape(-1, model_width)
            summed = summed + jnp.dot(
                window, kernel[vertical, across], preferred_element_type=jnp.float32
            )
    return summed


def conv_backward(gradient, kernel):
    view_count, row_count, tile_width, model_width = gradient.shape
    padded = padded_2(gradient, (("cols", 2),), 1)
    padded = jnp.pad(padded, ((0, 0), (1, 1), (0, 0), (0, 0)))
    summed = jnp.zeros((view_count * row_count * tile_width, kernel.shape[2]), jnp.float32)
    for vertical in range(3):
        for across in range(3):
            window = padded[
                :, 2 - vertical : 2 - vertical + row_count, 2 - across : 2 - across + tile_width, :
            ].reshape(-1, model_width)
            summed = summed + transposed_product(window, kernel[vertical, across])
    return summed


def attention_weights(queries, keys, live_mask):
    raw = jnp.einsum(
        "cqhd,ckhd->chqk", queries, keys, preferred_element_type=jnp.float32
    ) * queries.shape[-1] ** (-0.5)
    grown = jnp.exp(raw) * live_mask[:, None, None, :]
    return grown / jnp.sum(grown, axis=-1, keepdims=True)


def local(
    clip_tokens,
    cotangent,
    gain_attn,
    w_query,
    w_key,
    w_value,
    w_out,
    gain_first,
    conv_first,
    gain_second,
    conv_second,
    matching,
    block_lists,
    counts,
):
    view_count, row_count, tile_width, model_width = clip_tokens.shape
    camera_count = matching.shape[0]
    frame_count = view_count // camera_count
    pick_count = block_lists.shape[2]
    block_size = row_count * tile_width
    head_size = model_width // HEADS
    col_count = lax.axis_size("cols")
    own_index = lax.axis_index("cols")
    inputs = clip_tokens.astype(jnp.float32).reshape(-1, model_width)
    normed, inv_in = row_norm(inputs, gain_attn)
    rows_in = normed.astype(jnp.bfloat16)
    query_pre = head_product(rows_in, w_query)
    query_hat, query_inv = row_norm(query_pre, 1.0)
    key_pre = head_product(rows_in, w_key)
    key_hat, key_inv = row_norm(key_pre, 1.0)
    values = jnp.dot(rows_in, w_value, preferred_element_type=jnp.float32).astype(jnp.bfloat16)
    queries = query_hat.astype(jnp.bfloat16).reshape(
        frame_count, camera_count, block_size, HEADS, head_size
    )
    pairs = jnp.concatenate(
        [key_hat.astype(jnp.bfloat16).reshape(-1, model_width), values], axis=-1
    )
    pairs = pairs.reshape(frame_count, camera_count, block_size, 2 * model_width)
    slot_ids = jnp.arange(pick_count, dtype=jnp.int32)
    my_lists = jnp.take(block_lists, own_index, axis=1)
    my_counts = jnp.take(counts, own_index, axis=1)
    wanted = ((block_lists == own_index) & (slot_ids[None, None, :] < counts[:, :, None])).astype(
        jnp.int32
    )
    asked = jnp.sum(wanted, axis=(0, 2))
    source_camera = jnp.sum(wanted * matching[:, None, None], axis=(0, 2))
    request_flat = my_lists.reshape(-1)
    table_rows = rows_in.reshape(frame_count, camera_count, block_size, model_width)
    chosen = jnp.take(table_rows, source_camera, axis=1)
    arrived = lax.all_to_all(
        jnp.where(asked[None, :, None, None] > 0, chosen, jnp.zeros_like(chosen)),
        "cols",
        split_axis=1,
        concat_axis=1,
        tiled=True,
    )
    fetched = jnp.take(arrived, request_flat, axis=1).reshape(-1, model_width)
    far_pre = head_product(fetched, w_key)
    far_hat, far_inv = row_norm(far_pre, 1.0)
    far_values = jnp.dot(fetched, w_value, preferred_element_type=jnp.float32).astype(jnp.bfloat16)
    remote = jnp.concatenate(
        [far_hat.astype(jnp.bfloat16).reshape(-1, model_width), far_values], axis=-1
    )
    remote = remote.reshape(frame_count, camera_count * pick_count, block_size, 2 * model_width)
    remote = remote.reshape(frame_count, camera_count, pick_count, block_size, 2 * model_width)
    all_blocks = jnp.concatenate([pairs[:, :, None], remote], axis=2)
    all_blocks = all_blocks.reshape(
        frame_count, camera_count, (1 + pick_count) * block_size, 2 * model_width
    )
    live_far = (slot_ids[None, :] < my_counts[:, None]).astype(jnp.float32)
    live_mask = jnp.repeat(
        jnp.concatenate([jnp.ones((camera_count, 1), jnp.float32), live_far], axis=1),
        block_size,
        axis=1,
    )

    def split_pairs(pair_set):
        key_part = pair_set[..., :model_width].reshape(camera_count, -1, HEADS, head_size)
        value_part = pair_set[..., model_width:].reshape(camera_count, -1, HEADS, head_size)
        return (key_part, value_part)

    def forward_frame(operands):
        frame_queries, pair_set = operands
        key_part, value_part = split_pairs(pair_set)
        weights = attention_weights(frame_queries, key_part, live_mask)
        mixed_frame = jnp.einsum(
            "chqk,ckhd->cqhd",
            weights.astype(jnp.bfloat16),
            value_part,
            preferred_element_type=jnp.float32,
        )
        return mixed_frame.astype(jnp.bfloat16)

    mixed = lax.map(forward_frame, (queries, all_blocks)).reshape(-1, model_width)
    lifted = (inputs + jnp.dot(mixed, w_out, preferred_element_type=jnp.float32)).astype(
        jnp.bfloat16
    )
    lifted_f = lifted.astype(jnp.float32)
    spatial = (view_count, row_count, tile_width, model_width)
    first_in, inv_two = row_norm(lifted_f, gain_first)
    act_one = jax.nn.silu(first_in).astype(jnp.bfloat16)
    conv_one = conv_forward(act_one.reshape(spatial), conv_first)
    second_in, inv_three = row_norm(conv_one, gain_second)
    act_two = jax.nn.silu(second_in).astype(jnp.bfloat16)
    conv_two = conv_forward(act_two.reshape(spatial), conv_second)
    result = (lifted_f + conv_two).astype(jnp.bfloat16)
    grad_out = cotangent.astype(jnp.float32).reshape(-1, model_width)
    d_act_two = conv_backward(cotangent, conv_second)
    d_conv_one = norm_back(
        d_act_two * silu_slope(second_in), conv_one, inv_three, gain_second
    ).astype(jnp.bfloat16)
    d_act_one = conv_backward(d_conv_one.reshape(spatial), conv_first)
    d_lifted = grad_out + norm_back(d_act_one * silu_slope(first_in), lifted_f, inv_two, gain_first)
    d_mixed = transposed_product(d_lifted.astype(jnp.bfloat16), w_out).astype(jnp.bfloat16)

    def backward_frame(operands):
        frame_queries, pair_set, gradient = operands
        key_part, value_part = split_pairs(pair_set)
        weights = attention_weights(frame_queries, key_part, live_mask)
        rounded = weights.astype(jnp.bfloat16)
        slope = jnp.einsum(
            "cqhd,ckhd->chqk", gradient, value_part, preferred_element_type=jnp.float32
        )
        d_score = weights * (slope - jnp.sum(weights * slope, axis=-1, keepdims=True))
        d_scaled = (d_score * head_size ** (-0.5)).astype(jnp.bfloat16)
        d_query = jnp.einsum(
            "chqk,ckhd->cqhd", d_scaled, key_part, preferred_element_type=jnp.float32
        )
        d_keys = jnp.einsum(
            "chqk,cqhd->ckhd", d_scaled, frame_queries, preferred_element_type=jnp.float32
        )
        d_vals = jnp.einsum(
            "chqk,cqhd->ckhd", rounded, gradient, preferred_element_type=jnp.float32
        )
        both = jnp.concatenate(
            [
                d_keys.reshape(camera_count, -1, model_width),
                d_vals.reshape(camera_count, -1, model_width),
            ],
            axis=-1,
        )
        return (d_query, both.reshape(camera_count, 1 + pick_count, block_size, 2 * model_width))

    d_mixed_frames = d_mixed.reshape(frame_count, camera_count, block_size, HEADS, head_size)
    d_query, d_pairs = lax.map(backward_frame, (queries, all_blocks, d_mixed_frames))
    far_grad = (
        d_pairs[:, :, 1:]
        .astype(jnp.bfloat16)
        .reshape(frame_count, camera_count * pick_count, block_size, 2 * model_width)
    )
    owner_ids = jnp.arange(col_count, dtype=jnp.int32)
    matched = (request_flat[None, :] == owner_ids[:, None]).astype(jnp.int32)
    which_request = jnp.sum(
        matched * jnp.arange(camera_count * pick_count, dtype=jnp.int32)[None, :], axis=1
    )
    present = jnp.sum(matched, axis=1)
    holders = (
        (source_camera[:, None] == jnp.arange(camera_count, dtype=jnp.int32)[None, :])
        & (asked[:, None] > 0)
    ).astype(jnp.bfloat16)
    chosen = jnp.take(far_grad, which_request, axis=1)
    returned = lax.all_to_all(
        jnp.where(present[None, :, None, None] > 0, chosen, jnp.zeros_like(chosen)),
        "cols",
        split_axis=1,
        concat_axis=1,
        tiled=True,
    )
    asked_pre = jnp.take(
        key_pre.reshape(frame_count, camera_count, block_size, model_width), source_camera, axis=1
    )
    asked_inv = jnp.take(
        key_inv.reshape(frame_count, camera_count, block_size, HEADS), source_camera, axis=1
    )
    shares = row_share(returned, asked_pre, asked_inv, w_key, w_value)
    shares = shares.reshape(frame_count, col_count, block_size, model_width)
    gathered = jnp.einsum("fnbx,nc->fcbx", shares, holders, preferred_element_type=jnp.float32)
    own_pairs = d_pairs[:, :, 0].reshape(-1, 2 * model_width)
    d_query_pre = norm_back(d_query.reshape(-1, HEADS, head_size), query_pre, query_inv, 1.0)
    d_key_pre = norm_back(
        own_pairs[:, :model_width].reshape(-1, HEADS, head_size), key_pre, key_inv, 1.0
    )
    d_rows = transposed_product(d_query_pre.reshape(-1, model_width).astype(jnp.bfloat16), w_query)
    d_rows = d_rows + transposed_product(
        d_key_pre.reshape(-1, model_width).astype(jnp.bfloat16), w_key
    )
    d_rows = d_rows + transposed_product(own_pairs[:, model_width:].astype(jnp.bfloat16), w_value)
    d_rows = d_rows + gathered.reshape(-1, model_width)
    d_clip = (d_lifted + norm_back(d_rows, inputs, inv_in, gain_attn)).astype(jnp.bfloat16)
    return (result.reshape(spatial), d_clip.reshape(spatial))


def solution(mesh):
    in_specs = (
        P("groups", None, "cols", None),
        P("groups", None, "cols", None),
        P(),
        P(),
        P(),
        P(),
        P(),
        P(),
        P(),
        P(),
        P(),
        P(),
        P(),
        P(),
    )
    out_specs = (P("groups", None, "cols", None), P("groups", None, "cols", None))
    return jax.shard_map(local, mesh=mesh, in_specs=in_specs, out_specs=out_specs, check_vma=False)
```

profile of v0, /device:TPU:13, one launch (start us, length us, event | category | flops | bytes accessed | tf_op | source)
XLA Modules:
  0.0 729.6 jit_solution(15713617460395423048)
XLA Ops:
  7.2 3.9 collective-permute-start.4
  21.4 5.5 all-to-all-start
  39.1 3.5 fusion.212
  42.6 3.4 copy.123
  51.8 3.4 multiply_reduce_fusion.6
  70.3 5.4 copy.155
  75.8 5.4 copy.153
  81.2 4.9 gather.46
  97.7 4.2 fusion.205
  140.0 3.7 concatenate.72
  143.7 4.4 copy.128
  148.1 4.7 maximum_maximum_fusion
  157.7 4.7 copy.129
  162.4 4.4 fusion.3
  166.8 3.4 fusion.63
  179.7 3.5 collective-permute-start
  188.6 5.4 collective-permute-done.1
  205.4 3.4 fusion.123
  210.3 4.6 fusion.207
  244.5 5.8 multiply_reduce_fusion.5
  271.1 5.1 collective-permute-done.7
  287.6 3.4 fusion.121
  292.6 4.5 fusion.204
  326.7 6.5 fusion.52
  336.3 3.6 reshape.808
  342.9 9.7 %fusion.21 = f32[7,384,8,64]{1,3,2,0:T(8,128)} fusion(bf16[7,128,8,64]{1,3,2,0:T(8,128)(2,1)} %copy.141, f32[7,8,128,384]{3,2,1,0:T(8,128)} %copy-done.28, f32[7,8,128]{2,1,0:T(8,128)S(1)} %get-tuple-element.127, f32[7,384]{1,0:T(8,128)S(1)} %broadcast_bitcast_fusion), kind=kOutput, calls=%fused_computation.41 | convolution fusion | flops 363331584 | bytes 17472000 | tf_op jit(solution)/shard_map/while/body/eval_jaxpr/chqk,cqhd->ckhd/dot_general | solution.py:238
  352.6 5.8 fusion.213
  358.4 9.0 %concatenate.91 = f32[1,7,3,128,512]{3,2,4,1,0:T(4,128)} reshape(f32[7,384,8,64]{1,3,2,0:T(8,128)} %fusion.21) | data formatting | bytes 11010048 | tf_op jit(solution)/shard_map/while/body/eval_jaxpr/concatenate | solution.py:241
  367.4 45.5 %fusion.24 = f32[7,384,8,64]{1,3,2,0:T(8,128)} fusion(f32[7,8,128,384]{3,2,1,0:T(8,128)} %fusion.213, f32[7,8,128,384]{3,2,1,0:T(8,128)} %copy-done.28, f32[7,8,128]{2,1,0:T(8,128)S(1)} %get-tuple-element.127, f32[7,384]{1,0:T(8,128)S(1)} %broadcast_bitcast_fusion, f32[896,8,64]{0,2,1:T(8,128)S(1)} %copy-done.6, f32[896,8]{0,1:T(8,128)S(1)} %get-tuple-element.116), kind=kOutput, calls=%fused_computation.42 | convolution fusion | flops 383524224 | bytes 29428224 | tf_op jit(solution)/shard_map/while/body/eval_jaxpr/chqk,cqhd->ckhd/dot_general | solution.py:235
  412.9 9.1 %concatenate.90 = f32[1,7,3,128,512]{3,2,4,1,0:T(4,128)} reshape(f32[7,384,8,64]{1,3,2,0:T(8,128)} %fusion.24) | data formatting | bytes 11010048 | tf_op jit(solution)/shard_map/while/body/eval_jaxpr/concatenate | solution.py:241
  421.9 7.3 constant_dynamic-update-slice_fusion.1
  429.2 7.3 constant_dynamic-update-slice_fusion
  436.5 8.3 %slice.529 = bf16[1,7,2,128,1024]{3,2,4,1,0:T(2,128)(2,1)} slice(f32[1,7,3,128,1024]{3,2,4,1,0:T(4,128)} %constant_dynamic-update-slice_fusion), slice={[0:1], [0:7], [1:3], [0:128], [0:1024]} | slice | bytes 7340032 | tf_op jit(solution)/shard_map/slice | solution.py:253
  444.8 9.9 %copy.150 = bf16[1,7,2,128,1024]{4,3,2,1,0:T(8,128)(2,1)} copy(bf16[1,7,2,128,1024]{3,2,4,1,0:T(2,128)(2,1)} %slice.529) | data formatting | bytes 7340032 | tf_op jit(solution)/shard_map/slice | solution.py:253
  454.7 4.9 gather_fusion.3
  459.6 4.7 fusion.15
  464.2 7.7 %all-to-all-start.1 = ((bf16[1,16,128,1024]{3,2,0,1:T(8,128)(2,1)}), bf16[1,16,128,1024]{3,2,0,1:T(8,128)(2,1)}, u32[]{:S(2)}, u32[]{:S(2)}) async-start(bf16[1,16,128,1024]{3,2,0,1:T(8,128)(2,1)} %fusion.15), calls=%async_computation.1 | async-start | bytes 8388608 | tf_op jit(solution)/shard_map/all_to_all | solution.py:268
  473.1 3.3 collective-permute-start.2
  481.3 8.1 %slice.372 = f32[1,7,1,128,1024]{3,2,4,1,0:T(1,128)} slice(f32[1,7,3,128,1024]{3,2,4,1,0:T(4,128)} %constant_dynamic-update-slice_fusion), slice={[0:1], [0:7], [0:1], [0:128], [0:1024]} | slice | bytes 7340032 | tf_op jit(solution)/shard_map/slice | solution.py:284
  489.4 78.2 %collective-permute-done.2 = bf16[7,32,1,512]{3,2,1,0:T(2,128)(2,1)S(1)} collective-permute-done((bf16[7,32,1,512]{3,2,1,0:T(2,128)(2,1)S(1)}, bf16[7,32,1,512]{3,2,1,0:T(2,128)(2,1)S(1)}, u32[]{:S(2)}, u32[]{:S(2)}) %collective-permute-start.2) | collective-permute-done | bytes 229408 | tf_op jit(solution)/shard_map/ppermute | solution.py:20
  578.4 4.5 fusion.206
  609.3 9.9 %copy.145 = f32[1,7,1,128,1024]{4,3,1,2,0:T(8,128)} copy(f32[1,7,1,128,1024]{3,2,4,1,0:T(1,128)} %slice.372) | data formatting | bytes 7340032 | tf_op jit(solution)/shard_map/slice | solution.py:284
  630.9 49.0 %fusion.57 = f32[7,8,8,8,128]{4,3,2,1,0:T(8,128)} fusion(bf16[7,384,8,64]{1,3,2,0:T(8,128)(2,1)} %bitcast.320, f32[7,8,128,384]{3,2,1,0:T(8,128)} %fusion.213, f32[7,8,128,384]{3,2,1,0:T(8,128)} %copy-done.28, f32[7,8,128]{2,1,0:T(8,128)S(1)} %get-tuple-element.127, f32[7,384]{1,0:T(8,128)S(1)} %broadcast_bitcast_fusion), kind=kOutput, calls=%fused_computation.109 | convolution fusion | flops 382606720 | bytes 26647040 | tf_op jit(solution)/shard_map/while/body/eval_jaxpr/chqk,ckhd->cqhd/dot_general | solution.py:232
  689.8 5.6 fusion.203
  695.4 5.5 copy.154
  700.9 5.4 copy.158
  706.3 5.2 reshape.675
  711.5 4.7 multiply_reduce_fusion.1
  (387 shorter events, 308.4 us)
Async XLA Ops:
  0.6 36.8 %copy-start = (bf16[512,512]{1,0:T(8,128)(2,1)S(1)}, bf16[512,512]{1,0:T(8,128)(2,1)}, u32[]{:S(2)}) copy-start(bf16[512,512]{1,0:T(8,128)(2,1)} %param.19) | copy-start | bytes 1572868
  0.6 10.4 %copy-start.27 = (bf16[7,32,4,512]{3,2,1,0:T(4,128)(2,1)S(1)}, bf16[7,32,4,512]{3,2,1,0:T(4,128)(2,1)}, u32[]{:S(2)}) copy-start(bf16[7,32,4,512]{3,2,1,0:T(4,128)(2,1)} %param.14) | copy-start | bytes 2752516
  3.9 82.8 %collective-permute-start.5 = (bf16[7,32,1,512]{3,1,2,0:T(8,128)(2,1)}, bf16[7,32,1,512]{3,1,2,0:T(8,128)(2,1)}, u32[]{:S(2)}, u32[]{:S(2)}) collective-permute-start(bf16[7,32,1,512]{3,1,2,0:T(8,128)(2,1)} %copy.162), channel_id=1, source_target_pairs={{1,0},{2,1},{3,2},{4,3},{5,4},{6,5},{7,6},{8,7},{9,8},{10,9},{11,1... | collective-permute-start | bytes 688136 | tf_op jit(solution)/shard_map/ppermute | solution.py:21
  7.2 80.8 %collective-permute-start.4 = (bf16[7,32,1,512]{3,1,2,0:T(8,128)(2,1)}, bf16[7,32,1,512]{3,1,2,0:T(8,128)(2,1)}, u32[]{:S(2)}, u32[]{:S(2)}) collective-permute-start(bf16[7,32,1,512]{3,1,2,0:T(8,128)(2,1)} %copy.161), channel_id=1, source_target_pairs={{0,1},{1,2},{2,3},{3,4},{4,5},{5,6},{6,7},{7,8},{8,9},{9,10},{10,1... | collective-permute-start | bytes 688136 | tf_op jit(solution)/shard_map/ppermute | solution.py:20
  21.4 110.6 %all-to-all-start = ((bf16[1,16,128,512]{3,2,0,1:T(8,128)(2,1)}), bf16[1,16,128,512]{3,2,0,1:T(8,128)(2,1)}, u32[]{:S(2)}, u32[]{:S(2)}) async-start(bf16[1,16,128,512]{3,2,0,1:T(8,128)(2,1)} %fusion.27), calls=%async_computation | async-start | bytes 4194304 | tf_op jit(solution)/shard_map/all_to_all | solution.py:156
  27.3 11.8 %copy-start.82 = (f32[896]{0:T(1024)}, f32[896]{0:T(1024)S(1)}, u32[]{:S(2)}) copy-start(f32[896]{0:T(1024)S(1)} %rsqrt.82) | copy-start | bytes 10756
  31.6 5.9 copy-start.3
  42.6 24.9 %copy-start.1 = (f32[896,512]{1,0:T(8,128)}, f32[896,512]{1,0:T(8,128)S(1)}, u32[]{:S(2)}) copy-start(f32[896,512]{1,0:T(8,128)S(1)} %get-tuple-element.124) | copy-start | bytes 5505028
  106.0 4.9 copy-start.53
  177.2 7.9 %copy-start.33 = (bf16[896,512]{1,0:T(8,128)(2,1)S(1)}, bf16[896,512]{1,0:T(8,128)(2,1)}, u32[]{:S(2)}) copy-start(bf16[896,512]{1,0:T(8,128)(2,1)} %fusion.43) | copy-start | bytes 2752516
  179.7 14.3 %copy-start.23 = (bf16[7,32,4,512]{3,2,1,0:T(4,128)(2,1)S(1)}, bf16[7,32,4,512]{3,2,1,0:T(4,128)(2,1)}, u32[]{:S(2)}) copy-start(bf16[7,32,4,512]{3,2,1,0:T(4,128)(2,1)} %reshape.634) | copy-start | bytes 2752516
  179.7 8.9 %collective-permute-start = (bf16[7,32,1,512]{3,2,1,0:T(2,128)(2,1)S(1)}, bf16[7,32,1,512]{3,2,1,0:T(2,128)(2,1)S(1)}, u32[]{:S(2)}, u32[]{:S(2)}) collective-permute-start(bf16[7,32,1,512]{3,2,1,0:T(2,128)(2,1)S(1)} %get-tuple-element.110), channel_id=1, source_target_pairs={{0,1},{1,2},{2,3},{3,4},{4,5},{5,6},{6,7},{7,8},{8,9},{9,10},{10,1... | collective-permute-start | bytes 688136 | tf_op jit(solution)/shard_map/ppermute | solution.py:20
  183.1 10.8 %collective-permute-start.1 = (bf16[7,32,1,512]{3,2,1,0:T(2,128)(2,1)S(1)}, bf16[7,32,1,512]{3,2,1,0:T(2,128)(2,1)S(1)}, u32[]{:S(2)}, u32[]{:S(2)}) collective-permute-start(bf16[7,32,1,512]{3,2,1,0:T(2,128)(2,1)S(1)} %get-tuple-element.111), channel_id=1, source_target_pairs={{1,0},{2,1},{3,2},{4,3},{5,4},{6,5},{7,6},{8,7},{9,8},{10,9},{11,1... | collective-permute-start | bytes 688136 | tf_op jit(solution)/shard_map/ppermute | solution.py:21
  188.6 8.6 %copy-start.68 = (bf16[7,32,1,512]{3,2,1,0:T(2,128)(2,1)}, bf16[7,32,1,512]{3,2,1,0:T(2,128)(2,1)S(1)}, u32[]{:S(2)}) copy-start(bf16[7,32,1,512]{3,2,1,0:T(2,128)(2,1)S(1)} %collective-permute-done) | copy-start | bytes 688132
  244.4 5.9 copy-start.36
  244.4 5.9 copy-start.37
  244.4 6.0 copy-start.38
  244.4 6.5 copy-start.39
  244.4 7.0 copy-start.40
  244.4 7.5 %copy-start.41 = (f32[896,512]{1,0:T(8,128)S(1)}, f32[896,512]{1,0:T(8,128)}, u32[]{:S(2)}) copy-start(f32[896,512]{1,0:T(8,128)} %fusion.99) | copy-start | bytes 5505028
  244.4 8.0 %copy-start.42 = (f32[896,512]{1,0:T(8,128)S(1)}, f32[896,512]{1,0:T(8,128)}, u32[]{:S(2)}) copy-start(f32[896,512]{1,0:T(8,128)} %fusion.103) | copy-start | bytes 5505028
  244.4 8.6 %copy-start.43 = (f32[896,512]{1,0:T(8,128)S(1)}, f32[896,512]{1,0:T(8,128)}, u32[]{:S(2)}) copy-start(f32[896,512]{1,0:T(8,128)} %fusion.107) | copy-start | bytes 5505028
  244.5 8.7 %copy-start.63 = (bf16[896,512]{1,0:T(8,128)(2,1)S(1)}, bf16[896,512]{1,0:T(8,128)(2,1)}, u32[]{:S(2)}) copy-start(bf16[896,512]{1,0:T(8,128)(2,1)} %reshape.662) | copy-start | bytes 2752516
  244.5 8.7 %copy-start.89 = (f32[512]{0:T(512)S(1)}, f32[512]{0:T(512)}, u32[]{:S(2)}) copy-start(f32[512]{0:T(512)} %param.23) | copy-start | bytes 6148
  260.7 7.4 %copy-start.35 = (bf16[896,512]{1,0:T(8,128)(2,1)S(1)}, bf16[896,512]{1,0:T(8,128)(2,1)}, u32[]{:S(2)}) copy-start(bf16[896,512]{1,0:T(8,128)(2,1)} %get-tuple-element.94) | copy-start | bytes 2752516
  263.2 12.9 %copy-start.25 = (bf16[7,32,4,512]{3,2,1,0:T(4,128)(2,1)S(1)}, bf16[7,32,4,512]{3,2,1,0:T(4,128)(2,1)}, u32[]{:S(2)}) copy-start(bf16[7,32,4,512]{3,2,1,0:T(4,128)(2,1)} %reshape.663) | copy-start | bytes 2752516
  263.2 7.9 %collective-permute-start.6 = (bf16[7,32,1,512]{3,2,1,0:T(2,128)(2,1)S(1)}, bf16[7,32,1,512]{3,2,1,0:T(2,128)(2,1)S(1)}, u32[]{:S(2)}, u32[]{:S(2)}) collective-permute-start(bf16[7,32,1,512]{3,2,1,0:T(2,128)(2,1)S(1)} %get-tuple-element.98), channel_id=1, source_target_pairs={{0,1},{1,2},{2,3},{3,4},{4,5},{5,6},{6,7},{7,8},{8,9},{9,10},{10,1... | collective-permute-start | bytes 688136 | tf_op jit(solution)/shard_map/ppermute | solution.py:20
  265.3 10.9 %collective-permute-start.7 = (bf16[7,32,1,512]{3,2,1,0:T(2,128)(2,1)S(1)}, bf16[7,32,1,512]{3,2,1,0:T(2,128)(2,1)S(1)}, u32[]{:S(2)}, u32[]{:S(2)}) collective-permute-start(bf16[7,32,1,512]{3,2,1,0:T(2,128)(2,1)S(1)} %get-tuple-element.99), channel_id=1, source_target_pairs={{1,0},{2,1},{3,2},{4,3},{5,4},{6,5},{7,6},{8,7},{9,8},{10,9},{11,1... | collective-permute-start | bytes 688136 | tf_op jit(solution)/shard_map/ppermute | solution.py:21
  271.1 8.3 %copy-start.70 = (bf16[7,32,1,512]{3,2,1,0:T(2,128)(2,1)}, bf16[7,32,1,512]{3,2,1,0:T(2,128)(2,1)S(1)}, u32[]{:S(2)}) copy-start(bf16[7,32,1,512]{3,2,1,0:T(2,128)(2,1)S(1)} %collective-permute-done.6) | copy-start | bytes 688132
  326.7 7.8 %copy-start.21 = (bf16[896,512]{1,0:T(8,128)(2,1)S(1)}, bf16[896,512]{1,0:T(8,128)(2,1)}, u32[]{:S(2)}) copy-start(bf16[896,512]{1,0:T(8,128)(2,1)} %reshape.653) | copy-start | bytes 2752516
  326.7 7.8 %copy-start.79 = (bf16[512,512]{1,0:T(8,128)(2,1)S(1)}, bf16[512,512]{1,0:T(8,128)(2,1)}, u32[]{:S(2)}) copy-start(bf16[512,512]{1,0:T(8,128)(2,1)} %param.20) | copy-start | bytes 1572868
  342.9 9.7 %copy-start.11 = (bf16[7,384,512]{1,2,0:T(8,128)(2,1)S(1)}, bf16[7,384,512]{1,2,0:T(8,128)(2,1)}, u32[]{:S(2)}) copy-start(bf16[7,384,512]{1,2,0:T(8,128)(2,1)} %copy.129) | copy-start | bytes 8257540
  342.9 9.7 %copy-start.51 = (bf16[7,128,8,64]{1,3,2,0:T(8,128)(2,1)S(1)}, bf16[7,128,8,64]{1,3,2,0:T(8,128)(2,1)}, u32[]{:S(2)}) copy-start(bf16[7,128,8,64]{1,3,2,0:T(8,128)(2,1)} %copy.141) | copy-start | bytes 2752516
  454.7 4.9 copy-start.97
  454.7 4.9 copy-start.98
  464.2 7.8 %copy-start.96 = (pred[16]{0:T(512)(128)(4,1)S(1)}, pred[16]{0:T(512)(128)(4,1)}, u32[]{:S(2)}) copy-start(pred[16]{0:T(512)(128)(4,1)} %copy-done.95) | copy-start | bytes 52
  464.2 7.8 %copy-start.12 = (f32[16,128,8]{1,2,0:T(8,128)S(1)}, f32[16,128,8]{1,2,0:T(8,128)}, u32[]{:S(2)}) copy-start(f32[16,128,8]{1,2,0:T(8,128)} %gather_fusion.2) | copy-start | bytes 196612
  464.2 7.9 %copy-start.34 = (bf16[896,512]{1,0:T(8,128)(2,1)S(1)}, bf16[896,512]{1,0:T(8,128)(2,1)}, u32[]{:S(2)}) copy-start(bf16[896,512]{1,0:T(8,128)(2,1)} %get-tuple-element.95) | copy-start | bytes 2752516
  464.2 225.6 %all-to-all-start.1 = ((bf16[1,16,128,1024]{3,2,0,1:T(8,128)(2,1)}), bf16[1,16,128,1024]{3,2,0,1:T(8,128)(2,1)}, u32[]{:S(2)}, u32[]{:S(2)}) async-start(bf16[1,16,128,1024]{3,2,0,1:T(8,128)(2,1)} %fusion.15), calls=%async_computation.1 | async-start | bytes 8388608 | tf_op jit(solution)/shard_map/all_to_all | solution.py:268
  473.1 94.4 %collective-permute-start.2 = (bf16[7,32,1,512]{3,2,1,0:T(2,128)(2,1)S(1)}, bf16[7,32,1,512]{3,2,1,0:T(2,128)(2,1)S(1)}, u32[]{:S(2)}, u32[]{:S(2)}) collective-permute-start(bf16[7,32,1,512]{3,2,1,0:T(2,128)(2,1)S(1)} %get-tuple-element.106), channel_id=1, source_target_pairs={{0,1},{1,2},{2,3},{3,4},{4,5},{5,6},{6,7},{7,8},{8,9},{9,10},{10,1... | collective-permute-start | bytes 688136 | tf_op jit(solution)/shard_map/ppermute | solution.py:20
  476.5 92.8 %collective-permute-start.3 = (bf16[7,32,1,512]{3,2,1,0:T(2,128)(2,1)S(1)}, bf16[7,32,1,512]{3,2,1,0:T(2,128)(2,1)S(1)}, u32[]{:S(2)}, u32[]{:S(2)}) collective-permute-start(bf16[7,32,1,512]{3,2,1,0:T(2,128)(2,1)S(1)} %get-tuple-element.107), channel_id=1, source_target_pairs={{1,0},{2,1},{3,2},{4,3},{5,4},{6,5},{7,6},{8,7},{9,8},{10,9},{11,1... | collective-permute-start | bytes 688136 | tf_op jit(solution)/shard_map/ppermute | solution.py:21
  590.0 11.7 %slice-start = ((s8[4718592]{0:T(1024)(128)(4,1)}), s8[524288]{0:T(1024)(128)(4,1)S(1)}, s32[]{:S(2)}) async-start(s8[4718592]{0:T(1024)(128)(4,1)} %bitcast.316), calls=%async_computation.2 | async-start | bytes 1048576
  596.0 5.7 slice-start.1
  609.3 9.9 %copy-start.2 = (f32[896,512]{1,0:T(8,128)S(1)}, f32[896,512]{1,0:T(8,128)}, u32[]{:S(2)}) copy-start(f32[896,512]{1,0:T(8,128)} %copy-done.1) | copy-start | bytes 5505028
  679.9 7.8 %copy-start.49 = (f32[896,512]{1,0:T(8,128)S(1)}, f32[896,512]{1,0:T(8,128)}, u32[]{:S(2)}) copy-start(f32[896,512]{1,0:T(8,128)} %copy.149) | copy-start | bytes 5505028
  682.5 5.2 copy-start.8
  682.5 5.2 copy-start.47
  711.5 5.9 copy-start.14
  (64 other events, 165.9 us)
where the time goes:
time: 737 us; the launch traced here: 730 us
  local copies, waits for them, and re-layouts  288 us (39%)
  matrix products  243 us (33%)
  waiting for transfers between devices  90.9 us (12%)
  other arithmetic  69.7 us (9%)
  starting transfers between devices  35.2 us (5%)
    ppermute x4, waiting for transfers between devices, padded_2(): before = lax.ppermute(last, axis, up)  78.8 us
    dot_general x24, matrix products, transposed_product(): lax.dot_general(tokens, weight, CONTRACT_LAST, preferred_element_type=jnp...  69.2 us
    dot_general x1, matrix products, backward_frame(): jnp.einsum('chqk,ckhd->cqhd', d_scaled, key_part, preferred_element_type=...  49 us
    dot_general x1, matrix products, backward_frame(): jnp.einsum('chqk,cqhd->ckhd', d_scaled, frame_queries, preferred_element_...  45.5 us
    dot_general x18, matrix products, conv_forward(): jnp.dot(window, kernel[vertical, across], preferred_element_type=jnp.floa...  42.3 us
    reshape x16, local copies, waits for them, and re-layouts, conv_forward(): window = padded[:, vertical:vertical + row_count, across:across + tile_wi...  36.3 us
    reshape x16, local copies, waits for them, and re-layouts, conv_backward(): window = padded[:, 2 - vertical:2 - vertical + row_count, 2 - across:2 -...  32.3 us
    concatenate x3, local copies, waits for them, and re-layouts, backward_frame(): jnp.concatenate([d_keys.reshape(camera_count, -1, model_width), d_vals.re...  25.4 us
  transfers between devices with their start and end apart: 10, of which 5 were waited for; matrix products, arithmetic and copies ran while one was open for 34% of the time, Pallas kernels for 0%

commit v1 on v0

v1 whole, which is shorter than its diff:
```python
import functools

import jax
import jax.numpy as jnp
from jax import lax
from jax.experimental import pallas as pl
from jax.experimental.pallas import tpu as pltpu
from jax.sharding import PartitionSpec as P

HEADS = 8
EPSILON = 1e-06
F32 = jnp.float32
BF16 = jnp.bfloat16
VMEM_LIMIT = 56 * 1024 * 1024


def mm(a, b):
    return lax.dot_general(a, b, (((1,), (0,)), ((), ())), preferred_element_type=F32)


def mm_t(a, b):
    return lax.dot_general(a, b, (((1,), (1,)), ((), ())), preferred_element_type=F32)


def params(sems=None):
    return pltpu.CompilerParams(
        dimension_semantics=sems, vmem_limit_bytes=VMEM_LIMIT
    )


def whole(shape):
    zeros = (0,) * len(shape)
    return pl.BlockSpec(shape, lambda *_: zeros)


def rms(values):
    return lax.rsqrt(jnp.mean(values * values, axis=-1, keepdims=True) + EPSILON)


def silu_parts(u):
    sigmoid = jax.nn.sigmoid(u)
    return u * sigmoid, sigmoid * (1.0 + u * (1.0 - sigmoid))


def head_ones(width, head):
    rows = lax.broadcasted_iota(jnp.int32, (width, width), 0) // head
    cols = lax.broadcasted_iota(jnp.int32, (width, width), 1) // head
    return jnp.where(rows == cols, 1.0, 0.0).astype(BF16)


def head_mean(values, ones, head):
    width = ones.shape[0]
    parts = [
        mm(values[:, i : i + width].astype(BF16), ones)
        for i in range(0, values.shape[1], width)
    ]
    return jnp.concatenate(parts, axis=1) * (1.0 / head)


def prep_kernel(n_cols, own_s, match_s, lists_s, counts_s, clip_ref, gain_ref, rows_ref, send_ref, sem):
    cams = match_s.shape[0]
    picks = lists_s.shape[2]
    own = own_s[0]
    tw, _, nr, width = clip_ref.shape
    for c in range(cams):
        x = clip_ref[:, c].reshape(tw * nr, width).astype(F32)
        rows_ref[c] = (x * rms(x) * gain_ref[...]).astype(BF16)

    def copy(i):
        cam = jnp.int32(0)
        for c in range(cams):
            for s in range(picks):
                hit = (lists_s[c, i, s] == own) & (s < counts_s[c, i])
                cam = jnp.where(hit, match_s[c], cam)
        pltpu.make_async_copy(rows_ref.at[cam], send_ref.at[i], sem.at[i]).start()

    def start(i, carry):
        copy(i)
        return carry

    lax.fori_loop(0, n_cols, start, 0)

    def wait(i, carry):
        pltpu.make_async_copy(rows_ref.at[0], send_ref.at[i], sem.at[i]).wait()
        return carry

    lax.fori_loop(0, n_cols, wait, 0)


def prep(n_cols, own, matching, lists, counts, clip_t, gain):
    tw, cams, nr, width = clip_t.shape
    blk = tw * nr
    return pl.pallas_call(
        functools.partial(prep_kernel, n_cols),
        name="prep",
        out_shape=(
            jax.ShapeDtypeStruct((cams, blk, width), BF16),
            jax.ShapeDtypeStruct((n_cols, blk, width), BF16),
        ),
        grid_spec=pltpu.PrefetchScalarGridSpec(
            num_scalar_prefetch=4,
            grid=(1,),
            in_specs=[whole(clip_t.shape), whole((1, width))],
            out_specs=[whole((cams, blk, width)), pl.BlockSpec(memory_space=pl.ANY)],
            scratch_shapes=[pltpu.SemaphoreType.DMA((n_cols,))],
        ),
        compiler_params=params(),
    )(own, matching, lists, counts, clip_t, gain)


def project_kernel(head, rows_ref, wq_ref, wk_ref, wv_ref, q_ref, k_ref, v_ref, rq_ref, rk_ref):
    rows = rows_ref[...]
    width = rows.shape[1]
    half = width // 2
    ones = head_ones(half, head)
    for n in range(2):
        cols = slice(n * half, (n + 1) * half)
        for w_ref, o_ref, r_ref in ((wq_ref, q_ref, rq_ref), (wk_ref, k_ref, rk_ref)):
            pre = mm(rows, w_ref[:, cols])
            r = lax.rsqrt(head_mean(pre * pre, ones, head) + EPSILON)
            o_ref[:, cols] = (pre * r).astype(BF16)
            r_ref[:, cols] = r
        v_ref[:, cols] = mm(rows, wv_ref[:, cols]).astype(BF16)


def project(rows, wq, wk, wv, head):
    total, width = rows.shape
    full = (total, width)
    return pl.pallas_call(
        functools.partial(project_kernel, head),
        name="project",
        out_shape=(
            jax.ShapeDtypeStruct(full, BF16),
            jax.ShapeDtypeStruct(full, BF16),
            jax.ShapeDtypeStruct(full, BF16),
            jax.ShapeDtypeStruct(full, F32),
            jax.ShapeDtypeStruct(full, F32),
        ),
        compiler_params=params(),
        cost_estimate=pl.CostEstimate(
            flops=6 * total * width * width, bytes_accessed=20 * total * width, transcendentals=0
        ),
    )(rows, wq, wk, wv)


def pair_rows(x, low):
    zero = jnp.zeros_like(x)
    return jnp.concatenate([jnp.where(low, x, zero), jnp.where(low, zero, x)], axis=0)


def attend_kernel(head, picks, own_s, lists_s, counts_s, *refs):
    far = refs[:picks]
    (q_ref, k_ref, v_ref, clip_ref, wk_ref, wv_ref, wo_ref, gain_ref,
     lifted_ref, act_ref, near_ref, farther_ref, kf_ref, vf_ref, rf_ref, kcat, vcat) = refs[picks:]
    c = pl.program_id(0)
    own = own_s[0]
    count = counts_s[c, own]
    blk, width = q_ref.shape[1:]
    half = width // 2
    keys = (1 + picks) * blk
    ones_h = head_ones(half, head)
    rows = jnp.concatenate([f[0] for f in far], axis=0)
    kcat[:blk] = k_ref[0]
    vcat[:blk] = v_ref[0]
    for n in range(2):
        cols = slice(n * half, (n + 1) * half)
        pre = mm(rows, wk_ref[:, cols])
        r = lax.rsqrt(head_mean(pre * pre, ones_h, head) + EPSILON)
        k = (pre * r).astype(BF16)
        v = mm(rows, wv_ref[:, cols]).astype(BF16)
        kcat[blk:, cols] = k
        vcat[blk:, cols] = v
        kf_ref[0, :, cols] = k
        vf_ref[0, :, cols] = v
        rf_ref[0, :, cols] = r
    key_block = lax.broadcasted_iota(jnp.int32, (keys, 1), 0) // blk
    live = jnp.where(key_block <= count, 1.0, 0.0)
    live_ones = jnp.broadcast_to(live, (keys, 128)).astype(BF16)
    low = lax.broadcasted_iota(jnp.int32, (blk, 128), 1) < head
    scale = head ** (-0.5)
    mixed = []
    for h in range(0, width, 128):
        q2 = pair_rows(q_ref[0, :, h : h + 128] * jnp.asarray(scale, BF16), low)
        grown = jnp.exp(mm_t(q2, kcat[:, h : h + 128])).astype(BF16)
        ext = jnp.concatenate([vcat[:, h : h + 128] * live_ones, live_ones], axis=1)
        out = mm(grown, ext)
        out = out[:, :128] / out[:, 128:]
        mixed.append(jnp.where(low, out[:blk], out[blk:]).astype(BF16))
    mixed = jnp.concatenate(mixed, axis=1)
    clip = clip_ref[:, 0].reshape(blk, width).astype(F32)
    lifted = (clip + mm(mixed, wo_ref[...])).astype(BF16)
    lifted_f = lifted.astype(F32)
    act, _ = silu_parts(lifted_f * rms(lifted_f) * gain_ref[...])
    slabs = (clip_ref.shape[0], clip_ref.shape[2], width)
    lifted_ref[:, 0] = lifted.reshape(slabs)
    act = act.astype(BF16).reshape(slabs)
    act_ref[:, 0] = act
    even = lax.rem(own, 2) == 0
    near_ref[0] = jnp.where(even, act[-1], act[0])
    farther_ref[0] = jnp.where(even, act[0], act[-1])


def attend(own, lists, counts, arrived, q, k, v, clip_t, wk, wv, wo, gain, head):
    tw, cams, nr, width = clip_t.shape
    blk = tw * nr
    picks = lists.shape[2]
    slab = pl.BlockSpec((tw, 1, nr, width), lambda c, *_: (0, c, 0, 0))
    block = pl.BlockSpec((1, blk, width), lambda c, *_: (c, 0, 0))
    far_block = pl.BlockSpec((1, picks * blk, width), lambda c, *_: (c, 0, 0))
    edge = pl.BlockSpec((1, nr, width), lambda c, *_: (c, 0, 0))

    def listed(s):
        return pl.BlockSpec(
            (1, blk, width), lambda c, own, lists, counts: (lists[c, own[0], s], 0, 0)
        )

    return pl.pallas_call(
        functools.partial(attend_kernel, head, picks),
        name="attend",
        out_shape=(
            jax.ShapeDtypeStruct(clip_t.shape, BF16),
            jax.ShapeDtypeStruct(clip_t.shape, BF16),
            jax.ShapeDtypeStruct((cams, nr, width), BF16),
            jax.ShapeDtypeStruct((cams, nr, width), BF16),
            jax.ShapeDtypeStruct((cams, picks * blk, width), BF16),
            jax.ShapeDtypeStruct((cams, picks * blk, width), BF16),
            jax.ShapeDtypeStruct((cams, picks * blk, width), F32),
        ),
        grid_spec=pltpu.PrefetchScalarGridSpec(
            num_scalar_prefetch=3,
            grid=(cams,),
            in_specs=[listed(s) for s in range(picks)]
            + [block, block, block, slab]
            + [whole((width, width))] * 3
            + [whole((1, width))],
            out_specs=[slab, slab, edge, edge, far_block, far_block, far_block],
            scratch_shapes=[
                pltpu.VMEM(((1 + picks) * blk, width), BF16),
                pltpu.VMEM(((1 + picks) * blk, width), BF16),
            ],
        ),
        compiler_params=params(("arbitrary",)),
    )(own, lists, counts, *([arrived] * picks), q, k, v, clip_t, wk, wv, wo, gain)


def fill_windows(own_s, act_ref, near_ref, farther_ref, x_ref, edge, total):
    width = act_ref.shape[1]
    even = lax.rem(own_s[0], 2) == 0
    near = near_ref[...]
    farther = farther_ref[...]
    x_ref[:edge, :width] = jnp.where(even, farther, near)
    x_ref[edge:, :width] = act_ref[: total - edge]
    x_ref[:, width : 2 * width] = act_ref[...]
    x_ref[: total - edge, 2 * width :] = act_ref[edge:]
    x_ref[total - edge :, 2 * width :] = jnp.where(even, near, farther)


def conv_step(w_ref, x_ref, y_ref, step, transposed):
    width = w_ref.shape[2]
    if transposed:
        total = None
        for q in range(3):
            cols = slice((2 - q) * width, (3 - q) * width)
            part = mm_t(x_ref[:, cols], w_ref[0, q])
            total = part if total is None else total + part
        y_ref[step] = total
    else:
        y_ref[step] = mm(x_ref[...], w_ref[0].reshape(3 * width, width))


def conv_rows(y_ref, start, size, nr, transposed):
    rows = pl.ds(start, size)
    before, centre, after = (2, 1, 0) if transposed else (0, 1, 2)
    place = lax.broadcasted_iota(jnp.int32, (size, 1), 0) % nr
    up = pltpu.roll(y_ref[before, rows, :], 1, 0)
    down = pltpu.roll(y_ref[after, rows, :], size - 1, 0)
    return (
        jnp.where(place == 0, 0.0, up)
        + y_ref[centre, rows, :]
        + jnp.where(place == nr - 1, 0.0, down)
    )


def conv_kernel(body, n_extra, transposed, nr, own_s, act_ref, near_ref, farther_ref, w_ref, *refs):
    extra, outs, (x_ref, y_ref) = refs[:n_extra], refs[n_extra:-2], refs[-2:]
    step = pl.program_id(0)
    total = act_ref.shape[0]
    edge = near_ref.shape[0]

    @pl.when(step == 0)
    def _():
        fill_windows(own_s, act_ref, near_ref, farther_ref, x_ref, edge, total)

    conv_step(w_ref, x_ref, y_ref, step, transposed)

    @pl.when(step == 2)
    def _():
        even = lax.rem(own_s[0], 2) == 0
        body(lambda start, size: conv_rows(y_ref, start, size, nr, transposed), even, edge, extra, outs)


def conv_call(name, body, own, act, near, farther, weights, extra, outs, nr, transposed):
    total, width = act.shape
    edge = near.shape[0]
    return pl.pallas_call(
        functools.partial(conv_kernel, body, len(extra), transposed, nr),
        name=name,
        out_shape=outs,
        grid_spec=pltpu.PrefetchScalarGridSpec(
            num_scalar_prefetch=1,
            grid=(3,),
            in_specs=[
                whole((total, width)),
                whole((edge, width)),
                whole((edge, width)),
                pl.BlockSpec((1, 3, width, width), lambda p, *_: (p, 0, 0, 0)),
            ]
            + [whole(e.shape) for e in extra],
            out_specs=[whole(o.shape) for o in outs],
            scratch_shapes=[
                pltpu.VMEM((total, 3 * width), BF16),
                pltpu.VMEM((3, total, width), F32),
            ],
        ),
        compiler_params=params(("arbitrary",)),
        cost_estimate=pl.CostEstimate(
            flops=18 * total * width * width, bytes_accessed=18 * width * width, transcendentals=0
        ),
    )(own, act, near, farther, weights, *extra)


CHUNK = 32


def chunks(total, fn):
    def step(i, carry):
        fn(pl.multiple_of(i * CHUNK, CHUNK))
        return carry

    lax.fori_loop(0, total // CHUNK, step, 0)


def grad_two_body(rows_of, even, edge, extra, outs):
    (out,) = outs

    def one(start):
        out[pl.ds(start, CHUNK), :] = rows_of(start, CHUNK)

    chunks(out.shape[0], one)


def copy_edges(even, edge, full, near, farther):
    total = full.shape[0]
    first = full[:edge]
    last = full[total - edge :]
    near[...] = jnp.where(even, last, first)
    farther[...] = jnp.where(even, first, last)


def conv_one_body(rows_of, even, edge, extra, outs):
    grad_ref, gain_ref = extra
    act_ref, act_near, act_far, d_ref, d_near, d_far = outs
    total = act_ref.shape[0]
    gain = gain_ref[...]

    def one(start):
        rows = pl.ds(start, CHUNK)
        conv = rows_of(start, CHUNK)
        r = rms(conv)
        hat = conv * r
        act, slope = silu_parts(hat * gain)
        act_ref[rows, :] = act.astype(BF16)
        g = grad_ref[rows, :] * slope * gain
        d_ref[rows, :] = (r * (g - hat * jnp.mean(g * hat, axis=-1, keepdims=True))).astype(BF16)

    chunks(total, one)
    copy_edges(even, edge, act_ref, act_near, act_far)
    copy_edges(even, edge, d_ref, d_near, d_far)


def conv_two_body(rows_of, even, edge, extra, outs):
    (lifted_ref,) = extra
    (out,) = outs

    def one(start):
        rows = pl.ds(start, CHUNK)
        out[rows, :] = (lifted_ref[rows, :].astype(F32) + rows_of(start, CHUNK)).astype(BF16)

    chunks(out.shape[0], one)


def grad_one_body(rows_of, even, edge, extra, outs):
    lifted_ref, cot_ref, gain_ref, wo_ref = extra
    d_lifted_ref, d_mixed_ref = outs
    gain = gain_ref[...]
    total = d_lifted_ref.shape[0]

    def one(start):
        rows = pl.ds(start, CHUNK)
        lifted = lifted_ref[rows, :].astype(F32)
        r = rms(lifted)
        hat = lifted * r
        _, slope = silu_parts(hat * gain)
        g = rows_of(start, CHUNK) * slope * gain
        back = r * (g - hat * jnp.mean(g * hat, axis=-1, keepdims=True))
        d_lifted_ref[rows, :] = cot_ref[rows, :].astype(F32) + back

    chunks(total, one)
    d_mixed_ref[...] = mm_t(d_lifted_ref[...].astype(BF16), wo_ref[...]).astype(BF16)


def head_norm_back(grad, hat, r, ones, head):
    hat = hat.astype(F32)
    return r * (grad - hat * head_mean(grad * hat, ones, head))


def attend_back_kernel(head, picks, own_s, lists_s, counts_s, *refs):
    (q_ref, k_ref, v_ref, kf_ref, vf_ref, rq_ref, rk_ref, rf_ref, dm_ref, wk_ref, wv_ref,
     dq_ref, dk_ref, dv_ref, send_ref, kcat, vcat, kgrad, vgrad) = refs
    c = pl.program_id(0)
    own = own_s[0]
    count = counts_s[c, own]
    blk, width = q_ref.shape[1:]
    half = width // 2
    keys = (1 + picks) * blk
    tw, nr = dm_ref.shape[0], dm_ref.shape[2]
    scale = head ** (-0.5)

    @pl.when(c == 0)
    def _():
        send_ref[...] = jnp.zeros_like(send_ref)

    kcat[:blk] = k_ref[0]
    kcat[blk:] = kf_ref[0]
    vcat[:blk] = v_ref[0]
    vcat[blk:] = vf_ref[0]
    key_block = lax.broadcasted_iota(jnp.int32, (keys, 1), 0) // blk
    live = jnp.where(key_block <= count, 1.0, 0.0)
    low = lax.broadcasted_iota(jnp.int32, (blk, 128), 1) < head
    ones_h = head_ones(half, head)
    dq = []
    for h in range(0, width, 128):
        cols = slice(h, h + 128)
        kp = kcat[:, cols]
        q2 = pair_rows(q_ref[0, :, cols] * jnp.asarray(scale, BF16), low)
        dm2 = pair_rows(dm_ref[:, 0, :, cols].reshape(blk, 128), low)
        grown = jnp.exp(mm_t(kp, q2)) * live
        inverse = 1.0 / jnp.sum(grown, axis=0, keepdims=True)
        weights = grown * inverse
        slope = mm_t(vcat[:, cols], dm2)
        drift = jnp.sum(weights * slope, axis=0, keepdims=True)
        d_scaled = (weights * (slope - drift)).astype(BF16)
        kgrad[:, cols] = mm(d_scaled, q2)
        vgrad[:, cols] = mm(weights.astype(BF16), dm2)
        dq_t = mm(jnp.transpose(kp), d_scaled) * scale
        dq_t = jnp.concatenate([dq_t[:head, :blk], dq_t[head:, blk:]], axis=0)
        dq.append(jnp.transpose(dq_t))
    dq = jnp.concatenate(dq, axis=1)
    dq_ref[0] = head_norm_back(dq, q_ref[0], rq_ref[0], ones_h, head).astype(BF16)
    dk_ref[0] = head_norm_back(kgrad[:blk], kcat[:blk], rk_ref[0], ones_h, head).astype(BF16)
    dv_ref[0] = vgrad[:blk].astype(BF16)
    far_k = head_norm_back(kgrad[blk:], kcat[blk:], rf_ref[0], ones_h, head).astype(BF16)
    share = mm_t(far_k, wk_ref[...]) + mm_t(vgrad[blk:].astype(BF16), wv_ref[...])
    share = share.astype(BF16)
    for s in range(picks):
        send_ref[lists_s[c, own, s]] = share[s * blk : (s + 1) * blk]


def attend_back(own, lists, counts, n_cols, q, k, v, kf, vf, rq, rk, rf, dm_t, wk, wv, head):
    tw, cams, nr, width = dm_t.shape
    blk = tw * nr
    picks = lists.shape[2]
    slab = pl.BlockSpec((tw, 1, nr, width), lambda c, *_: (0, c, 0, 0))
    block = pl.BlockSpec((1, blk, width), lambda c, *_: (c, 0, 0))
    far_block = pl.BlockSpec((1, picks * blk, width), lambda c, *_: (c, 0, 0))
    keys = (1 + picks) * blk
    return pl.pallas_call(
        functools.partial(attend_back_kernel, head, picks),
        name="attend_back",
        out_shape=(
            jax.ShapeDtypeStruct((cams, blk, width), BF16),
            jax.ShapeDtypeStruct((cams, blk, width), BF16),
            jax.ShapeDtypeStruct((cams, blk, width), BF16),
            jax.ShapeDtypeStruct((n_cols, blk, width), BF16),
        ),
        grid_spec=pltpu.PrefetchScalarGridSpec(
            num_scalar_prefetch=3,
            grid=(cams,),
            in_specs=[block, block, block, far_block, far_block, block, block, far_block, slab]
            + [whole((width, width))] * 2,
            out_specs=[block, block, block, whole((n_cols, blk, width))],
            scratch_shapes=[
                pltpu.VMEM((keys, width), BF16),
                pltpu.VMEM((keys, width), BF16),
                pltpu.VMEM((keys, width), F32),
                pltpu.VMEM((keys, width), F32),
            ],
        ),
        compiler_params=params(("arbitrary",)),
    )(own, lists, counts, q, k, v, kf, vf, rq, rk, rf, dm_t, wk, wv)


def row_grad_kernel(dq_ref, dk_ref, dv_ref, wq_ref, wk_ref, wv_ref, out_ref):
    out_ref[...] = mm_t(dq_ref[...], wq_ref[...])
    out_ref[...] += mm_t(dk_ref[...], wk_ref[...])
    out_ref[...] += mm_t(dv_ref[...], wv_ref[...])


def row_grad(dq, dk, dv, wq, wk, wv):
    total, width = dq.shape
    return pl.pallas_call(
        row_grad_kernel,
        name="row_grad",
        out_shape=jax.ShapeDtypeStruct((total, width), F32),
        compiler_params=params(),
        cost_estimate=pl.CostEstimate(
            flops=6 * total * width * width, bytes_accessed=10 * total * width, transcendentals=0
        ),
    )(dq, dk, dv, wq, wk, wv)


def final_kernel(n_cols, own_s, match_s, lists_s, counts_s, back_ref, rows_ref, clip_ref, dl_ref, gain_ref, out_ref, acc):
    cams = match_s.shape[0]
    picks = lists_s.shape[2]
    own = own_s[0]
    tw, _, nr, width = clip_ref.shape
    blk = tw * nr
    acc[...] = rows_ref[...]

    def add(i, carry):
        cam = jnp.int32(-1)
        for c in range(cams):
            for s in range(picks):
                hit = (lists_s[c, i, s] == own) & (s < counts_s[c, i])
                cam = jnp.where(hit, match_s[c], cam)

        @pl.when(cam >= 0)
        def _():
            acc[cam] += back_ref[i].astype(F32)

        return carry

    lax.fori_loop(0, n_cols, add, 0)
    gain = gain_ref[...]

    def one(c, carry):
        x = clip_ref[:, c].reshape(blk, width).astype(F32)
        r = rms(x)
        hat = x * r
        g = acc[c] * gain
        d = dl_ref[:, c].reshape(blk, width) + r * (
            g - hat * jnp.mean(g * hat, axis=-1, keepdims=True)
        )
        out_ref[:, c] = d.astype(BF16).reshape(tw, nr, width)
        return carry

    lax.fori_loop(0, cams, one, 0)


def final(own, matching, lists, counts, back, rows, clip_t, d_lifted, gain):
    n_cols = back.shape[0]
    return pl.pallas_call(
        functools.partial(final_kernel, n_cols),
        name="final",
        out_shape=jax.ShapeDtypeStruct(clip_t.shape, BF16),
        grid_spec=pltpu.PrefetchScalarGridSpec(
            num_scalar_prefetch=4,
            grid=(1,),
            in_specs=[whole(a.shape) for a in (back, rows, clip_t, d_lifted, gain)],
            out_specs=whole(clip_t.shape),
            scratch_shapes=[pltpu.VMEM(rows.shape, F32)],
        ),
        compiler_params=params(),
    )(own, matching, lists, counts, back, rows, clip_t, d_lifted, gain)


def exchange_edges(near, farther):
    size = lax.axis_size("cols")
    inner = [(i, i ^ 1) for i in range(size)]
    outer = [(i, i + 1 if i % 2 else i - 1) for i in range(1, size - 1)]
    return lax.ppermute(near, "cols", inner), lax.ppermute(farther, "cols", outer)


def local(
    clip_tokens,
    cotangent,
    gain_attn,
    w_query,
    w_key,
    w_value,
    w_out,
    gain_first,
    conv_first,
    gain_second,
    conv_second,
    matching,
    block_lists,
    counts,
):
    views, nr, tw, width = clip_tokens.shape
    head = width // HEADS
    n_cols = lax.axis_size("cols")
    own_index = lax.axis_index("cols").astype(jnp.int32)
    own = own_index.reshape(1)
    total = views * nr * tw
    blk = nr * tw
    flat = (total, width)
    slabs = (tw, views, nr, width)
    gain_attn = gain_attn.reshape(1, width)
    gain_first = gain_first.reshape(1, width)
    gain_second = gain_second.reshape(1, width)

    clip_t = jnp.transpose(clip_tokens, (2, 0, 1, 3))
    cot_t = jnp.transpose(cotangent, (2, 0, 1, 3))
    odd = own_index % 2
    last = (tw - 1) * (1 - odd)
    cot_near = lax.dynamic_index_in_dim(cot_t, last, 0, keepdims=False).reshape(-1, width)
    cot_far = lax.dynamic_index_in_dim(cot_t, tw - 1 - last, 0, keepdims=False).reshape(-1, width)
    cot_near, cot_far = exchange_edges(cot_near, cot_far)

    rows, send = prep(n_cols, own, matching, block_lists, counts, clip_t, gain_attn)
    arrived = lax.all_to_all(send, "cols", split_axis=0, concat_axis=0, tiled=True)

    (d_act_two,) = conv_call(
        "grad_two", grad_two_body, own, cot_t.reshape(flat), cot_near, cot_far, conv_second,
        (), (jax.ShapeDtypeStruct(flat, F32),), nr, True,
    )
    q, k, v, rq, rk = (
        a.reshape(views, blk, width)
        for a in project(rows.reshape(flat), w_query, w_key, w_value, head)
    )
    lifted, act_one, near, farther, kf, vf, rf = attend(
        own, block_lists, counts, arrived, q, k, v, clip_t, w_key, w_value, w_out, gain_first, head
    )
    edge = (views * nr, width)
    near, farther = exchange_edges(near.reshape(edge), farther.reshape(edge))
    flat_bf = jax.ShapeDtypeStruct(flat, BF16)
    edge_bf = jax.ShapeDtypeStruct(edge, BF16)
    act_two, act_near, act_far, d_conv, d_near, d_far = conv_call(
        "conv_one", conv_one_body, own, act_one.reshape(flat), near, farther, conv_first,
        (d_act_two, gain_second),
        (flat_bf, edge_bf, edge_bf, flat_bf, edge_bf, edge_bf), nr, False,
    )
    d_near, d_far = exchange_edges(d_near, d_far)
    d_lifted, d_mixed = conv_call(
        "grad_one", grad_one_body, own, d_conv, d_near, d_far, conv_first,
        (lifted.reshape(flat), cot_t.reshape(flat), gain_first, w_out),
        (jax.ShapeDtypeStruct(flat, F32), flat_bf), nr, True,
    )
    dq, dk, dv, send_back = attend_back(
        own, block_lists, counts, n_cols, q, k, v, kf, vf, rq, rk, rf,
        d_mixed.reshape(slabs), w_key, w_value, head,
    )
    back = lax.all_to_all(send_back, "cols", split_axis=0, concat_axis=0, tiled=True)
    act_near, act_far = exchange_edges(act_near, act_far)
    (result,) = conv_call(
        "conv_two", conv_two_body, own, act_two, act_near, act_far, conv_second,
        (lifted.reshape(flat),), (flat_bf,), nr, False,
    )
    d_rows = row_grad(
        dq.reshape(flat), dk.reshape(flat), dv.reshape(flat), w_query, w_key, w_value
    ).reshape(views, blk, width)
    d_clip = final(own, matching, block_lists, counts, back, d_rows, clip_t, d_lifted.reshape(slabs), gain_attn)
    return (
        jnp.transpose(result.reshape(slabs), (1, 2, 0, 3)),
        jnp.transpose(d_clip, (1, 2, 0, 3)),
    )


def solution(mesh):
    tiles = P("groups", None, "cols", None)
    in_specs = (tiles, tiles) + (P(),) * 12
    return jax.shard_map(
        local, mesh=mesh, in_specs=in_specs, out_specs=(tiles, tiles), check_vma=False
    )
```

time: 737 us -> 245 us (0.33)
  local copies, waits for them, and re-layouts: 288 us -> 16.4 us
  matrix products: 243 us -> 0 us
  Pallas kernels: 0 us -> 112 us
  other arithmetic: 69.7 us -> 0 us
  starting transfers between devices: 35.2 us -> 26.6 us
    dot_general x55 -> x0, matrix products: 243 us -> none  [the longest x24 69.2 us: transposed_product(): lax.dot_general(tokens, weight, CONTRACT_LAST, preferred_element_type=jnp...]
    pallas_call x0 -> x10, Pallas kernels: none -> 112 us  [the longest x4 47.9 us: conv_call(): pl.pallas_call(functools.partial(conv_kernel, body, len(extra), transpose...]
    reshape x42 -> x1, local copies, waits for them, and re-layouts: 90.7 us -> 2.81 us  [local(): result.reshape(slabs)]
    slice x15 -> x0, local copies, waits for them, and re-layouts: 71.8 us -> none  [the longest x2 18.2 us: local(): d_pairs[:, :, 1:].astype(jnp.bfloat16)]
    ppermute x8, waiting for transfers between devices: 90.9 us -> 52 us  [the longest x4 52 us: exchange_edges(): lax.ppermute(farther, 'cols', outer)]
    all_to_all x2, waiting for transfers between devices: 0.01 us -> 35.3 us  [the longest x1 35.3 us: local(): lax.all_to_all(send, 'cols', split_axis=0, concat_axis=0, tiled=True)]
    concatenate x5 -> x0, local copies, waits for them, and re-layouts: 33.4 us -> none  [the longest x3 25.4 us: backward_frame(): jnp.concatenate([d_keys.reshape(camera_count, -1, model_width), d_vals.re...]
    gather x8 -> x0, local copies, waits for them, and re-layouts: 29.1 us -> none  [the longest x4 18.6 us: local(): jnp.take(key_pre.reshape(frame_count, camera_count, block_size, model_wid...]
  transfers between devices with their start and end apart: 10 -> 10, of which waited for: 5 -> 3; matrix products, arithmetic and copies ran while one was open for 34% -> 2% of each run, Pallas kernels for 0% -> 18%
where the time goes in v1:
time: 245 us; the launch traced here: 243 us
  Pallas kernels  112 us (46%)
  waiting for transfers between devices  87.3 us (36%)
  starting transfers between devices  26.6 us (11%)
  local copies, waits for them, and re-layouts  16.4 us (7%)
    ppermute x4, waiting for transfers between devices, exchange_edges(): lax.ppermute(farther, 'cols', outer)  52 us
    pallas_call x4, Pallas kernels, conv_call(): pl.pallas_call(functools.partial(conv_kernel, body, len(extra), transpose...  47.9 us
    all_to_all x1, waiting for transfers between devices, local(): lax.all_to_all(send, 'cols', split_axis=0, concat_axis=0, tiled=True)  35.3 us
    pallas_call x1, Pallas kernels, attend_back(): pl.pallas_call(functools.partial(attend_back_kernel, head, picks), name='...  23.5 us
    pallas_call x1, Pallas kernels, attend(): pl.pallas_call(functools.partial(attend_kernel, head, picks), name='atten...  15.9 us
    ppermute x4, starting transfers between devices, exchange_edges(): lax.ppermute(farther, 'cols', outer)  12.9 us
    unnamed x27, local copies, waits for them, and re-layouts  11.4 us
    pallas_call x1, Pallas kernels, final(): pl.pallas_call(functools.partial(final_kernel, n_cols), name='final', out...  8.02 us
  transfers between devices with their start and end apart: 10, of which 3 were waited for; matrix products, arithmetic and copies ran while one was open for 2% of the time, Pallas kernels for 18%

profile of v1, /device:TPU:13, one launch (start us, length us, event | category | flops | bytes accessed | tf_op | source)
XLA Modules:
  0.0 243.4 jit_solution(13270488494290653040)
XLA Ops:
  0.6 1.4 copy.26.lists_s
  2.1 2.3 copy.39
  4.4 5.6 %prep.1 = (bf16[7,128,512]{2,1,0:T(8,128)(2,1)}, bf16[16,128,512]{2,1,0:T(8,128)(2,1)}) custom-call(s32[1]{0:T(128)} %bitcast.own_s, s32[7]{0:T(128)} %match_s.3, s32[7,16,2]{2,1,0:T(8,128)} %copy.26.lists_s, s32[7,16]{1,0:T(8,128)} %counts_s.7, bf16[4,7,32,512]{3,2,1,0:T(8,128)(2,1)} %bitcast.32, f32[1,512]{1,0:T(1,128)} %bitcast.57), custom_call_target="tpu_custom_call" | custom-call | tf_op jit(solution)/shard_map/prep/pallas_call | solution.py:93
  10.0 0.0 copy-start.2
  10.0 6.7 %all-to-all-start = ((bf16[16,128,512]{2,1,0:T(8,128)(2,1)}), bf16[16,128,512]{2,1,0:T(8,128)(2,1)S(1)}, u32[]{:S(2)}, u32[]{:S(2)}) async-start(bf16[16,128,512]{2,1,0:T(8,128)(2,1)} %get-tuple-element.28), calls=%async_computation | async-start | bytes 4194304 | tf_op jit(solution)/shard_map/all_to_all | solution.py:622
  16.7 0.0 copy-done.2
  16.7 1.1 constant_dynamic-slice_fusion
  17.8 0.4 collective-permute-start.2
  18.3 3.1 %collective-permute-start.3 = (bf16[224,512]{1,0:T(8,128)(2,1)S(1)}, bf16[224,512]{1,0:T(8,128)(2,1)}, u32[]{:S(2)}, u32[]{:S(2)}) collective-permute-start(bf16[224,512]{1,0:T(8,128)(2,1)S(1)} %bitcast.56), channel_id=1, source_target_pairs={{1,2},{2,1},{3,4},{4,3},{5,6},{6,5},{7,8},{8,7},{9,10},{10,9},{11,... | collective-permute-start | bytes 688136 | tf_op jit(solution)/shard_map/ppermute | solution.py:581
  21.4 1.1 copy.27
  22.6 6.3 %project.1 = (bf16[896,512]{1,0:T(8,128)(2,1)}, bf16[896,512]{1,0:T(8,128)(2,1)}, bf16[896,512]{1,0:T(8,128)(2,1)}, f32[896,512]{1,0:T(8,128)}, f32[896,512]{1,0:T(8,128)}) custom-call(bf16[896,512]{1,0:T(8,128)(2,1)} %bitcast.63, bf16[512,512]{1,0:T(8,128)(2,1)} %wq_ref.3, bf16[512,512]{1,0:T(8,128)(2,1)} %wk_ref.3, bf16[512,512]{1,0:T(8,128)(2,1)} %wv_ref.3), custom_call_target="tpu_custom_call" | custom-call | flops 1409286144 | bytes 9175040 | tf_op jit(solution)/shard_map/project/pallas_call | solution.py:129
  28.8 35.3 %all-to-all-done.refs_0_.refs_1_ = bf16[16,128,512]{2,1,0:T(8,128)(2,1)S(1)} async-done(((bf16[16,128,512]{2,1,0:T(8,128)(2,1)}), bf16[16,128,512]{2,1,0:T(8,128)(2,1)S(1)}, u32[]{:S(2)}, u32[]{:S(2)}) %all-to-all-start) | async-done | bytes 2097184 | tf_op jit(solution)/shard_map/all_to_all | solution.py:622
  64.2 1.3 copy-done
  65.5 15.9 %attend.1 = (bf16[4,7,32,512]{3,2,1,0:T(8,128)(2,1)}, bf16[4,7,32,512]{3,2,1,0:T(8,128)(2,1)}, bf16[7,32,512]{2,1,0:T(8,128)(2,1)}, bf16[7,32,512]{2,1,0:T(8,128...) custom-call(s32[1]{0:T(128)} %bitcast.own_s, ...), custom_call_target="tpu_custom_call" | custom-call | tf_op jit(solution)/shard_map/attend/pallas_call | solution.py:217
  81.4 0.3 collective-permute-start
  81.7 3.8 %collective-permute-start.1 = (bf16[224,512]{1,0:T(8,128)(2,1)}, bf16[224,512]{1,0:T(8,128)(2,1)S(1)}, u32[]{:S(2)}, u32[]{:S(2)}) collective-permute-start(bf16[224,512]{1,0:T(8,128)(2,1)} %bitcast.65), channel_id=1, source_target_pairs={{1,2},{2,1},{3,4},{4,3},{5,6},{6,5},{7,8},{8,7},{9,10},{10,9},{11,... | collective-permute-start | bytes 688136 | tf_op jit(solution)/shard_map/ppermute | solution.py:581
  85.5 0.0 collective-permute-done.2.near_ref
  85.5 0.0 collective-permute-done.3.farther_ref
  85.5 8.7 %grad_two.1.refs_0_ = f32[896,512]{1,0:T(8,128)} custom-call(s32[1]{0:T(128)} %bitcast.own_s, bf16[896,512]{1,0:T(8,128)(2,1)} %bitcast.47, bf16[224,512]{1,0:T(8,128)(2,1)} %collective-permute-done.2.near_ref, bf16[224,512]{1,0:T(8,128)(2,1)} %collective-permute-done.3.farther_ref, bf16[3,3,512,512]{3,2,1,0:T(8,128)(2,1)} %w_ref.6), custom_call_target="tpu_custom_call" | custom-call | flops 4227858432 | bytes 4718592 | tf_op jit(solution)/shard_map/grad_two/pallas_call | solution.py:305
  94.2 0.0 collective-permute-done.near_ref
  94.2 0.0 collective-permute-done.1.farther_ref
  94.2 0.0 copy-start.6
  94.2 0.7 copy-done.5
  94.9 0.1 copy-done.6
  94.9 15.0 %conv_one.1 = (bf16[896,512]{1,0:T(8,128)(2,1)}, bf16[224,512]{1,0:T(8,128)(2,1)}, bf16[224,512]{1,0:T(8,128)(2,1)}, bf16[896,512]{1,0:T(8,128)(2,1)}, bf16[224,...) custom-call(s32[1]{0:T(128)} %bitcast.own_s, bf16[896,512]{1,0:T(8,128)(2,1)} %bitcast.64, bf16[224,512]{1,0:T(8,128)(2,1)} %copy-done.5, ...), custom_call_target="tpu_custom_call" | custom-call | flops 4227858432 | bytes 4718592 | tf_op jit(solution)/shard_map/conv_one/pallas_call | solution.py:305
  109.9 0.0 collective-permute-start.6
  109.9 2.8 %collective-permute-start.7 = (bf16[224,512]{1,0:T(8,128)(2,1)}, bf16[224,512]{1,0:T(8,128)(2,1)S(1)}, u32[]{:S(2)}, u32[]{:S(2)}) collective-permute-start(bf16[224,512]{1,0:T(8,128)(2,1)} %get-tuple-element.47), channel_id=1, source_target_pairs={{1,2},{2,1},{3,4},{4,3},{5,6},{6,5},{7,8},{8,7},{9,10},{10,9},{11,... | collective-permute-start | bytes 688136 | tf_op jit(solution)/shard_map/ppermute | solution.py:581
  112.8 0.0 collective-permute-done.6.near_ref
  112.8 0.0 copy-start.7
  112.8 5.7 %collective-permute-done.7.farther_ref = bf16[224,512]{1,0:T(8,128)(2,1)S(1)} collective-permute-done((bf16[224,512]{1,0:T(8,128)(2,1)}, bf16[224,512]{1,0:T(8,128)(2,1)S(1)}, u32[]{:S(2)}, u32[]{:S(2)}) %collective-permute-start.7) | collective-permute-done | bytes 229408 | tf_op jit(solution)/shard_map/ppermute | solution.py:581
  118.5 0.7 copy-done.9
  119.2 15.6 %grad_one.1 = (f32[896,512]{1,0:T(8,128)}, bf16[896,512]{1,0:T(8,128)(2,1)}) custom-call(s32[1]{0:T(128)} %bitcast.own_s, bf16[896,512]{1,0:T(8,128)(2,1)} %get-tuple-element.45.act_ref, bf16[224,512]{1,0:T(8,128)(2,1)} %copy-done.7, bf16[224,512]{1,0:T(8,128)(2,1)} %copy-done.9, bf16[3,3,512,512]{3,2,1,0:T(8,128)(2,1)} %w_ref.7, bf16[896,512]{1,0:T(8,128)(2,1)} %bitcast.61, ...), custom_call_target="tpu_custom_call" | custom-call | flops 4227858432 | bytes 4718592 | tf_op jit(solution)/shard_map/grad_one/pallas_call | solution.py:305
  134.7 23.5 %attend_back.1 = (bf16[7,128,512]{2,1,0:T(8,128)(2,1)}, bf16[7,128,512]{2,1,0:T(8,128)(2,1)}, bf16[7,128,512]{2,1,0:T(8,128)(2,1)}, bf16[16,128,512]{2,1,0:T(8,128)(2,1)}) custom-call(s32[1]{0:T(128)} %bitcast.own_s, s32[7,16,2]{2,1,0:T(8,128)} %copy.26.lists_s, s32[7,16]{1,0:T(8,128)} %counts_s.7, bf16[7,128,512]{2,1,0:T(8,128)(2,1)} %bitcast.38, ...), custom_call_target="tpu_custom_call" | custom-call | tf_op jit(solution)/shard_map/attend_back/pallas_call | solution.py:477
  158.2 0.0 copy-start.4
  158.2 0.0 copy-start.3
  158.2 6.0 %all-to-all-start.1 = ((bf16[16,128,512]{2,1,0:T(8,128)(2,1)}), bf16[16,128,512]{2,1,0:T(8,128)(2,1)S(1)}, u32[]{:S(2)}, u32[]{:S(2)}) async-start(bf16[16,128,512]{2,1,0:T(8,128)(2,1)} %get-tuple-element.49), calls=%async_computation.1 | async-start | bytes 4194304 | tf_op jit(solution)/shard_map/all_to_all | solution.py:654
  164.2 0.4 collective-permute-start.4
  164.6 3.1 %collective-permute-start.5 = (bf16[224,512]{1,0:T(8,128)(2,1)S(1)}, bf16[224,512]{1,0:T(8,128)(2,1)S(1)}, u32[]{:S(2)}, u32[]{:S(2)}) collective-permute-start(bf16[224,512]{1,0:T(8,128)(2,1)S(1)} %copy-done.3), channel_id=1, source_target_pairs={{1,2},{2,1},{3,4},{4,3},{5,6},{6,5},{7,8},{8,7},{9,10},{10,9},{11,... | collective-permute-start | bytes 688136 | tf_op jit(solution)/shard_map/ppermute | solution.py:581
  167.7 0.0 collective-permute-done.4.near_ref
  167.8 46.2 %collective-permute-done.5.farther_ref = bf16[224,512]{1,0:T(8,128)(2,1)S(1)} collective-permute-done((bf16[224,512]{1,0:T(8,128)(2,1)S(1)}, bf16[224,512]{1,0:T(8,128)(2,1)S(1)}, u32[]{:S(2)}, u32[]{:S(2)}) %collective-permute-start.5) | collective-permute-done | bytes 229408 | tf_op jit(solution)/shard_map/ppermute | solution.py:581
  214.0 0.7 copy-done.10
  214.7 8.7 %conv_two.1 = bf16[896,512]{1,0:T(8,128)(2,1)} custom-call(s32[1]{0:T(128)} %bitcast.own_s, bf16[896,512]{1,0:T(8,128)(2,1)} %get-tuple-element.36.act_ref, bf16[224,512]{1,0:T(8,128)(2,1)} %copy-done.8, bf16[224,512]{1,0:T(8,128)(2,1)} %copy-done.10, bf16[3,3,512,512]{3,2,1,0:T(8,128)(2,1)} %w_ref.6, bf16[896,512]{1,0:T(8,128)(2,1)} %bitcast.62), custom_call_target="tpu_custom_call" | custom-call | flops 4227858432 | bytes 4718592 | tf_op jit(solution)/shard_map/conv_two/pallas_call | solution.py:305
  223.4 2.8 %copy.38 = bf16[4,7,32,512]{3,0,2,1:T(4,128)(2,1)} copy(bf16[4,7,32,512]{3,2,1,0:T(8,128)(2,1)} %bitcast.50) | data formatting | bytes 1835008 | tf_op jit(solution)/shard_map/reshape | solution.py:665
  226.2 5.0 %row_grad.1 = f32[896,512]{1,0:T(8,128)} custom-call(bf16[896,512]{1,0:T(8,128)(2,1)} %bitcast.51, bf16[896,512]{1,0:T(8,128)(2,1)} %bitcast.52, bf16[896,512]{1,0:T(8,128)(2,1)} %bitcast.53, bf16[512,512]{1,0:T(8,128)(2,1)} %wq_ref.3, bf16[512,512]{1,0:T(8,128)(2,1)} %wk_ref.3, bf16[512,512]{1,0:T(8,128)(2,1)} %wv_ref.3), custom_call_target="tpu_custom_call" | custom-call | flops 1409286144 | bytes 4587520 | tf_op jit(solution)/shard_map/row_grad/pallas_call | solution.py:511
  231.2 0.0 all-to-all-done.1.back_ref
  231.3 1.3 copy-done.1
  232.6 8.0 %final.1 = bf16[4,7,32,512]{3,2,1,0:T(8,128)(2,1)} custom-call(s32[1]{0:T(128)} %bitcast.own_s, s32[7]{0:T(128)} %match_s.3, s32[7,16,2]{2,1,0:T(8,128)} %copy.26.lists_s, s32[7,16]{1,0:T(8,128)} %counts_s.7, bf16[16,128,512]{2,1,0:T(8,128)(2,1)} %copy-done.1, f32[7,128,512]{2,1,0:T(8,128)} %bitcast.35, bf16[4,7,32,512]{3,2,1,0:T(8,128)(2,1)} %bitcast.34, ...), custom_call_target="tpu_custom_call" | custom-call | tf_op jit(solution)/shard_map/final/pallas_call | solution.py:562
  240.6 2.8 %copy.33 = bf16[7,32,4,512]{3,2,1,0:T(4,128)(2,1)} copy(bf16[7,32,4,512]{3,1,0,2:T(8,128)(2,1)} %bitcast.36) | data formatting | bytes 1835008
  (12 shorter events, 0.1 us)
Async XLA Ops:
  10.0 6.7 %copy-start.2 = (bf16[7,32,4,512]{3,2,1,0:T(4,128)(2,1)S(1)}, bf16[7,32,4,512]{3,2,1,0:T(4,128)(2,1)}, u32[]{:S(2)}) copy-start(bf16[7,32,4,512]{3,2,1,0:T(4,128)(2,1)} %param.15) | copy-start | bytes 2752516
  10.0 54.2 %all-to-all-start = ((bf16[16,128,512]{2,1,0:T(8,128)(2,1)}), bf16[16,128,512]{2,1,0:T(8,128)(2,1)S(1)}, u32[]{:S(2)}, u32[]{:S(2)}) async-start(bf16[16,128,512]{2,1,0:T(8,128)(2,1)} %get-tuple-element.28), calls=%async_computation | async-start | bytes 4194304 | tf_op jit(solution)/shard_map/all_to_all | solution.py:622
  17.8 67.6 %collective-permute-start.2 = (bf16[224,512]{1,0:T(8,128)(2,1)S(1)}, bf16[224,512]{1,0:T(8,128)(2,1)}, u32[]{:S(2)}, u32[]{:S(2)}) collective-permute-start(bf16[224,512]{1,0:T(8,128)(2,1)S(1)} %bitcast.55), channel_id=1, source_target_pairs={{0,1},{1,0},{2,3},{3,2},{4,5},{5,4},{6,7},{7,6},{8,9},{9,8},{10,11... | collective-permute-start | bytes 688136 | tf_op jit(solution)/shard_map/ppermute | solution.py:581
  18.3 67.2 %collective-permute-start.3 = (bf16[224,512]{1,0:T(8,128)(2,1)S(1)}, bf16[224,512]{1,0:T(8,128)(2,1)}, u32[]{:S(2)}, u32[]{:S(2)}) collective-permute-start(bf16[224,512]{1,0:T(8,128)(2,1)S(1)} %bitcast.56), channel_id=1, source_target_pairs={{1,2},{2,1},{3,4},{4,3},{5,6},{6,5},{7,8},{8,7},{9,10},{10,9},{11,... | collective-permute-start | bytes 688136 | tf_op jit(solution)/shard_map/ppermute | solution.py:581
  64.2 1.3 copy-start
  81.4 12.8 %collective-permute-start = (bf16[224,512]{1,0:T(8,128)(2,1)}, bf16[224,512]{1,0:T(8,128)(2,1)S(1)}, u32[]{:S(2)}, u32[]{:S(2)}) collective-permute-start(bf16[224,512]{1,0:T(8,128)(2,1)} %bitcast.66), channel_id=1, source_target_pairs={{0,1},{1,0},{2,3},{3,2},{4,5},{5,4},{6,7},{7,6},{8,9},{9,8},{10,11... | collective-permute-start | bytes 688136 | tf_op jit(solution)/shard_map/ppermute | solution.py:581
  81.7 12.5 %collective-permute-start.1 = (bf16[224,512]{1,0:T(8,128)(2,1)}, bf16[224,512]{1,0:T(8,128)(2,1)S(1)}, u32[]{:S(2)}, u32[]{:S(2)}) collective-permute-start(bf16[224,512]{1,0:T(8,128)(2,1)} %bitcast.65), channel_id=1, source_target_pairs={{1,2},{2,1},{3,4},{4,3},{5,6},{6,5},{7,8},{8,7},{9,10},{10,9},{11,... | collective-permute-start | bytes 688136 | tf_op jit(solution)/shard_map/ppermute | solution.py:581
  94.2 0.7 copy-start.5
  94.2 0.8 copy-start.6
  109.9 2.8 %collective-permute-start.6 = (bf16[224,512]{1,0:T(8,128)(2,1)}, bf16[224,512]{1,0:T(8,128)(2,1)S(1)}, u32[]{:S(2)}, u32[]{:S(2)}) collective-permute-start(bf16[224,512]{1,0:T(8,128)(2,1)} %get-tuple-element.46), channel_id=1, source_target_pairs={{0,1},{1,0},{2,3},{3,2},{4,5},{5,4},{6,7},{7,6},{8,9},{9,8},{10,11... | collective-permute-start | bytes 688136 | tf_op jit(solution)/shard_map/ppermute | solution.py:581
  109.9 8.5 %collective-permute-start.7 = (bf16[224,512]{1,0:T(8,128)(2,1)}, bf16[224,512]{1,0:T(8,128)(2,1)S(1)}, u32[]{:S(2)}, u32[]{:S(2)}) collective-permute-start(bf16[224,512]{1,0:T(8,128)(2,1)} %get-tuple-element.47), channel_id=1, source_target_pairs={{1,2},{2,1},{3,4},{4,3},{5,6},{6,5},{7,8},{8,7},{9,10},{10,9},{11,... | collective-permute-start | bytes 688136 | tf_op jit(solution)/shard_map/ppermute | solution.py:581
  112.8 5.7 %copy-start.7 = (bf16[224,512]{1,0:T(8,128)(2,1)}, bf16[224,512]{1,0:T(8,128)(2,1)S(1)}, u32[]{:S(2)}) copy-start(bf16[224,512]{1,0:T(8,128)(2,1)S(1)} %collective-permute-done.6.near_ref) | copy-start | bytes 688132
  118.5 0.7 copy-start.9
  158.2 6.0 %copy-start.4 = (bf16[224,512]{1,0:T(8,128)(2,1)S(1)}, bf16[224,512]{1,0:T(8,128)(2,1)}, u32[]{:S(2)}) copy-start(bf16[224,512]{1,0:T(8,128)(2,1)} %get-tuple-element.37) | copy-start | bytes 688132
  158.2 6.4 %copy-start.3 = (bf16[224,512]{1,0:T(8,128)(2,1)S(1)}, bf16[224,512]{1,0:T(8,128)(2,1)}, u32[]{:S(2)}) copy-start(bf16[224,512]{1,0:T(8,128)(2,1)} %get-tuple-element.38) | copy-start | bytes 688132
  158.2 73.0 %all-to-all-start.1 = ((bf16[16,128,512]{2,1,0:T(8,128)(2,1)}), bf16[16,128,512]{2,1,0:T(8,128)(2,1)S(1)}, u32[]{:S(2)}, u32[]{:S(2)}) async-start(bf16[16,128,512]{2,1,0:T(8,128)(2,1)} %get-tuple-element.49), calls=%async_computation.1 | async-start | bytes 4194304 | tf_op jit(solution)/shard_map/all_to_all | solution.py:654
  164.2 3.6 %collective-permute-start.4 = (bf16[224,512]{1,0:T(8,128)(2,1)S(1)}, bf16[224,512]{1,0:T(8,128)(2,1)S(1)}, u32[]{:S(2)}, u32[]{:S(2)}) collective-permute-start(bf16[224,512]{1,0:T(8,128)(2,1)S(1)} %copy-done.4), channel_id=1, source_target_pairs={{0,1},{1,0},{2,3},{3,2},{4,5},{5,4},{6,7},{7,6},{8,9},{9,8},{10,11... | collective-permute-start | bytes 688136 | tf_op jit(solution)/shard_map/ppermute | solution.py:581
  164.6 49.4 %collective-permute-start.5 = (bf16[224,512]{1,0:T(8,128)(2,1)S(1)}, bf16[224,512]{1,0:T(8,128)(2,1)S(1)}, u32[]{:S(2)}, u32[]{:S(2)}) collective-permute-start(bf16[224,512]{1,0:T(8,128)(2,1)S(1)} %copy-done.3), channel_id=1, source_target_pairs={{1,2},{2,1},{3,4},{4,3},{5,6},{6,5},{7,8},{8,7},{9,10},{10,9},{11,... | collective-permute-start | bytes 688136 | tf_op jit(solution)/shard_map/ppermute | solution.py:581
  167.7 46.3 %copy-start.8 = (bf16[224,512]{1,0:T(8,128)(2,1)}, bf16[224,512]{1,0:T(8,128)(2,1)S(1)}, u32[]{:S(2)}) copy-start(bf16[224,512]{1,0:T(8,128)(2,1)S(1)} %collective-permute-done.4.near_ref) | copy-start | bytes 688132
  214.0 0.7 copy-start.10
  231.3 1.3 copy-start.1

commit v2 on v1

v2 whole, which is shorter than its diff:
```python
import functools

import jax
import jax.numpy as jnp
from jax import lax
from jax.experimental import pallas as pl
from jax.experimental.pallas import tpu as pltpu
from jax.sharding import PartitionSpec as P

HEADS = 8
EPSILON = 1e-06
F32 = jnp.float32
BF16 = jnp.bfloat16


def mm(a, b):
    return lax.dot_general(a, b, (((1,), (0,)), ((), ())), preferred_element_type=F32)


def mm_t(a, b):
    return lax.dot_general(a, b, (((1,), (1,)), ((), ())), preferred_element_type=F32)


def params(mib):
    return pltpu.CompilerParams(vmem_limit_bytes=mib * 1024 * 1024)


def hbm(x):
    return pltpu.with_memory_space_constraint(x, pltpu.HBM)


def vmem(x):
    return pltpu.with_memory_space_constraint(x, pltpu.VMEM)


def whole(shape):
    zeros = (0,) * len(shape)
    return pl.BlockSpec(shape, lambda *_: zeros)


def rms(values):
    return lax.rsqrt(jnp.mean(values * values, axis=-1, keepdims=True) + EPSILON)


def silu_parts(u):
    sigmoid = 0.5 + 0.5 * jnp.tanh(0.5 * u)
    return u * sigmoid, sigmoid * (1.0 + u * (1.0 - sigmoid))


def head_ones(width, head):
    rows = lax.broadcasted_iota(jnp.int32, (width, width), 0) // head
    cols = lax.broadcasted_iota(jnp.int32, (width, width), 1) // head
    return jnp.where(rows == cols, 1.0, 0.0).astype(BF16)


def head_mean(values, ones, head):
    width = ones.shape[0]
    parts = [
        mm(values[:, i : i + width].astype(BF16), ones)
        for i in range(0, values.shape[1], width)
    ]
    return jnp.concatenate(parts, axis=1) * (1.0 / head)


def prep_kernel(n_cols, own_s, match_s, lists_s, counts_s, clip_ref, gain_ref, rows_ref, send_ref, sem):
    cams = match_s.shape[0]
    picks = lists_s.shape[2]
    own = own_s[0]
    tw, _, nr, width = clip_ref.shape
    for c in range(cams):
        x = clip_ref[:, c].reshape(tw * nr, width).astype(F32)
        rows_ref[c] = (x * rms(x) * gain_ref[...]).astype(BF16)

    def copy(i):
        cam = jnp.int32(0)
        for c in range(cams):
            for s in range(picks):
                hit = (lists_s[c, i, s] == own) & (s < counts_s[c, i])
                cam = jnp.where(hit, match_s[c], cam)
        pltpu.make_async_copy(rows_ref.at[cam], send_ref.at[i], sem.at[i]).start()

    def start(i, carry):
        copy(i)
        return carry

    lax.fori_loop(0, n_cols, start, 0)

    def wait(i, carry):
        pltpu.make_async_copy(rows_ref.at[0], send_ref.at[i], sem.at[i]).wait()
        return carry

    lax.fori_loop(0, n_cols, wait, 0)


def prep(n_cols, own, matching, lists, counts, clip_t, gain):
    tw, cams, nr, width = clip_t.shape
    blk = tw * nr
    return pl.pallas_call(
        functools.partial(prep_kernel, n_cols),
        name="prep",
        out_shape=(
            jax.ShapeDtypeStruct((cams, blk, width), BF16),
            pltpu.HBM((n_cols, blk, width), BF16),
        ),
        grid_spec=pltpu.PrefetchScalarGridSpec(
            num_scalar_prefetch=4,
            grid=(1,),
            in_specs=[whole(clip_t.shape), whole((1, width))],
            out_specs=[whole((cams, blk, width)), pl.BlockSpec(memory_space=pltpu.HBM)],
            scratch_shapes=[pltpu.SemaphoreType.DMA((n_cols,))],
        ),
        compiler_params=params(8),
    )(own, matching, lists, counts, clip_t, gain)


def project_kernel(head, blk, rows_ref, wq_ref, wk_ref, wv_ref, wvt_ref, q_ref, k_ref, v_ref, vt_ref, rq_ref, rk_ref):
    rows = rows_ref[...]
    total, width = rows.shape
    half = width // 2
    ones = head_ones(half, head)
    for n in range(2):
        cols = slice(n * half, (n + 1) * half)
        for w_ref, o_ref, r_ref, scale in (
            (wq_ref, q_ref, rq_ref, head ** (-0.5)),
            (wk_ref, k_ref, rk_ref, 1.0),
        ):
            pre = mm(rows, w_ref[:, cols])
            r = lax.rsqrt(head_mean(pre * pre, ones, head) + EPSILON)
            o_ref[:, cols] = (pre * r * scale).astype(BF16)
            r_ref[:, cols] = r
        v_ref[:, cols] = mm(rows, wv_ref[:, cols]).astype(BF16)
    for c in range(total // blk):
        vt_ref[c] = mm_t(wvt_ref[...], rows_ref[c * blk : (c + 1) * blk]).astype(BF16)


def project(rows, wq, wk, wv, wvt, head, blk):
    total, width = rows.shape
    full = (total, width)
    return pl.pallas_call(
        functools.partial(project_kernel, head, blk),
        name="project",
        out_shape=(
            pltpu.VMEM(full, BF16),
            pltpu.VMEM(full, BF16),
            pltpu.VMEM(full, BF16),
            pltpu.VMEM((total // blk, width, blk), BF16),
            pltpu.VMEM(full, F32),
            pltpu.VMEM(full, F32),
        ),
        compiler_params=params(8),
        cost_estimate=pl.CostEstimate(
            flops=8 * total * width * width, bytes_accessed=20 * total * width, transcendentals=0
        ),
    )(rows, wq, wk, wv, wvt)


def pair_rows(x, low):
    zero = jnp.zeros_like(x)
    return jnp.concatenate([jnp.where(low, x, zero), jnp.where(low, zero, x)], axis=0)


PAD = 16


def attend_kernel(head, picks, own_s, lists_s, counts_s, *refs):
    (arrived_ref, q_ref, k_ref, vt_ref, clip_ref, wk_ref, wvt_ref, wo_ref, gain_ref,
     lifted_ref, act_ref, near_ref, farther_ref, kf_ref, rf_ref, e_ref, row_ref, col_ref,
     kcat, vcat) = refs
    c = pl.program_id(0)
    q_ref, k_ref, vt_ref, near_ref, farther_ref, kf_ref, rf_ref, e_ref, row_ref, col_ref = (
        camera(r, c)
        for r in (q_ref, k_ref, vt_ref, near_ref, farther_ref, kf_ref, rf_ref, e_ref, row_ref, col_ref)
    )
    clip_ref, lifted_ref, act_ref = (camera_slabs(r, c) for r in (clip_ref, lifted_ref, act_ref))
    own = own_s[0]
    count = counts_s[c, own]
    blk, width = q_ref.shape[1:]
    half = width // 2
    keys = (1 + picks) * blk
    pairs = width // 128

    @pl.when(c == 0)
    def _():
        vcat[:, 128:] = jnp.ones((pairs, PAD, keys), BF16)

    ones_h = head_ones(half, head)
    rows = jnp.concatenate([arrived_ref[lists_s[c, own, s]] for s in range(picks)], axis=0)
    kcat[:blk] = k_ref[0]
    vcat[:, :128, :blk] = vt_ref[0].reshape(pairs, 128, blk)
    vcat[:, :128, blk:] = mm_t(wvt_ref[...], rows).astype(BF16).reshape(pairs, 128, keys - blk)
    for n in range(2):
        cols = slice(n * half, (n + 1) * half)
        pre = mm(rows, wk_ref[:, cols])
        r = lax.rsqrt(head_mean(pre * pre, ones_h, head) + EPSILON)
        k = (pre * r).astype(BF16)
        kcat[blk:, cols] = k
        kf_ref[0, :, cols] = k
        rf_ref[0, :, cols] = r
    low = lax.broadcasted_iota(jnp.int32, (blk, 128), 1) < head
    live = [jnp.where(s < count, 1.0, 0.0) for s in range(picks)]
    mixed = []
    inverses = []
    for p in range(pairs):
        cols = slice(128 * p, 128 * (p + 1))
        q2 = pair_rows(q_ref[0, :, cols], low)
        grown = jnp.exp(mm_t(kcat[:, cols], q2))
        e_ref[0, p, :blk] = grown[:blk].astype(BF16)
        for s in range(picks):
            part = slice((1 + s) * blk, (2 + s) * blk)
            e_ref[0, p, part] = (grown[part] * live[s]).astype(BF16)
        out = mm(vcat[p], e_ref[0, p])
        inverse = 1.0 / out[128:129]
        inverses += [inverse[:, :blk], inverse[:, blk:]]
        out = out[:128] * inverse
        out = jnp.concatenate([out[:head, :blk], out[head:, blk:]], axis=0)
        mixed.append(jnp.transpose(out).astype(BF16))
    inverses = jnp.concatenate(inverses, axis=0)
    row_ref[0] = inverses
    spread = jnp.concatenate([inverses, jnp.zeros((128 - HEADS, blk), F32)], axis=0)
    col_ref[0] = jnp.transpose(spread)
    mixed = jnp.concatenate(mixed, axis=1)
    clip = clip_ref[:, 0].reshape(blk, width).astype(F32)
    lifted = (clip + mm(mixed, wo_ref[...])).astype(BF16)
    lifted_f = lifted.astype(F32)
    act, _ = silu_parts(lifted_f * rms(lifted_f) * gain_ref[...])
    slabs = (clip_ref.shape[0], clip_ref.shape[2], width)
    lifted_ref[:, 0] = lifted.reshape(slabs)
    act = act.astype(BF16).reshape(slabs)
    act_ref[:, 0] = act
    even = lax.rem(own, 2) == 0
    near_ref[0] = jnp.where(even, act[-1], act[0])
    farther_ref[0] = jnp.where(even, act[0], act[-1])


def camera(ref, c):
    return ref.at[pl.ds(c, 1)]


def camera_slabs(ref, c):
    return ref.at[:, pl.ds(c, 1)]


def attend(own, lists, counts, arrived, q, k, vt, clip_t, wk, wvt, wo, gain, head):
    tw, cams, nr, width = clip_t.shape
    blk = tw * nr
    picks = lists.shape[2]
    keys = (1 + picks) * blk
    pairs = width // 128
    args = (arrived, q, k, vt, clip_t, wk, wvt, wo, gain)
    outs = (
            pltpu.VMEM(clip_t.shape, BF16),
            pltpu.VMEM(clip_t.shape, BF16),
            jax.ShapeDtypeStruct((cams, nr, width), BF16),
            jax.ShapeDtypeStruct((cams, nr, width), BF16),
            pltpu.VMEM((cams, picks * blk, width), BF16),
            pltpu.VMEM((cams, picks * blk, width), F32),
            pltpu.VMEM((cams, pairs, keys, 2 * blk), BF16),
            pltpu.VMEM((cams, HEADS, blk), F32),
            pltpu.VMEM((cams, blk, 128), F32),
        )
    return pl.pallas_call(
        functools.partial(attend_kernel, head, picks),
        name="attend",
        out_shape=outs,
        grid_spec=pltpu.PrefetchScalarGridSpec(
            num_scalar_prefetch=3,
            grid=(cams,),
            in_specs=[whole(x.shape) for x in args],
            out_specs=[whole(x.shape) for x in outs],
            scratch_shapes=[
                pltpu.VMEM((keys, width), BF16),
                pltpu.VMEM((pairs, 128 + PAD, keys), BF16),
            ],
        ),
        compiler_params=params(6 + 2 * picks),
    )(own, lists, counts, *args)


def far_values_kernel(picks, own_s, lists_s, arrived_ref, w_ref, out_ref):
    cams = lists_s.shape[0]
    blk = arrived_ref.shape[1]
    for c in range(cams):
        rows = jnp.concatenate([arrived_ref[lists_s[c, own_s[0], s]] for s in range(picks)], axis=0)
        out_ref[c] = mm(rows, w_ref[...]).astype(BF16)


def far_values(own, lists, arrived, w):
    _, blk, width = arrived.shape
    cams, _, picks = lists.shape
    return pl.pallas_call(
        functools.partial(far_values_kernel, picks),
        name="far_values",
        out_shape=pltpu.VMEM((cams, picks * blk, width), BF16),
        grid_spec=pltpu.PrefetchScalarGridSpec(
            num_scalar_prefetch=2,
            grid=(1,),
            in_specs=[whole(arrived.shape), whole(w.shape)],
            out_specs=whole((cams, picks * blk, width)),
        ),
        compiler_params=params(4 + 2 * picks),
        cost_estimate=pl.CostEstimate(
            flops=2 * cams * picks * blk * width * width,
            bytes_accessed=4 * cams * picks * blk * width,
            transcendentals=0,
        ),
    )(own, lists, arrived, w)


def fill_windows(own_s, act_ref, near_ref, farther_ref, x_ref, edge, total):
    width = act_ref.shape[1]
    even = lax.rem(own_s[0], 2) == 0
    near = near_ref[...]
    farther = farther_ref[...]
    x_ref[:edge, :width] = jnp.where(even, farther, near)
    x_ref[edge:, :width] = act_ref[: total - edge]
    x_ref[:, width : 2 * width] = act_ref[...]
    x_ref[: total - edge, 2 * width :] = act_ref[edge:]
    x_ref[total - edge :, 2 * width :] = jnp.where(even, near, farther)


def conv_step(w_ref, x_ref, y_ref, step, transposed):
    width = w_ref.shape[2]
    if transposed:
        total = None
        for q in range(3):
            cols = slice((2 - q) * width, (3 - q) * width)
            part = mm_t(x_ref[:, cols], w_ref[0, q])
            total = part if total is None else total + part
        y_ref[step] = total
    else:
        y_ref[step] = mm(x_ref[...], w_ref[0].reshape(3 * width, width))


def conv_rows(y_ref, start, size, nr, transposed):
    rows = pl.ds(start, size)
    before, centre, after = (2, 1, 0) if transposed else (0, 1, 2)
    place = lax.broadcasted_iota(jnp.int32, (size, 1), 0) % nr
    up = pltpu.roll(y_ref[before, rows, :], 1, 0)
    down = pltpu.roll(y_ref[after, rows, :], size - 1, 0)
    return (
        jnp.where(place == 0, 0.0, up)
        + y_ref[centre, rows, :]
        + jnp.where(place == nr - 1, 0.0, down)
    )


def conv_kernel(body, n_extra, transposed, nr, own_s, act_ref, near_ref, farther_ref, w_ref, *refs):
    extra, outs, (x_ref, y_ref) = refs[:n_extra], refs[n_extra:-2], refs[-2:]
    step = pl.program_id(0)
    total = act_ref.shape[0]
    edge = near_ref.shape[0]

    @pl.when(step == 0)
    def _():
        fill_windows(own_s, act_ref, near_ref, farther_ref, x_ref, edge, total)

    conv_step(w_ref, x_ref, y_ref, step, transposed)

    @pl.when(step == 2)
    def _():
        even = lax.rem(own_s[0], 2) == 0
        body(lambda start, size: conv_rows(y_ref, start, size, nr, transposed), even, edge, extra, outs)


def conv_call(name, body, own, act, near, farther, weights, extra, outs, nr, transposed):
    total, width = act.shape
    edge = near.shape[0]
    return pl.pallas_call(
        functools.partial(conv_kernel, body, len(extra), transposed, nr),
        name=name,
        out_shape=outs,
        grid_spec=pltpu.PrefetchScalarGridSpec(
            num_scalar_prefetch=1,
            grid=(3,),
            in_specs=[
                whole((total, width)),
                whole((edge, width)),
                whole((edge, width)),
                pl.BlockSpec((1, 3, width, width), lambda p, *_: (p, 0, 0, 0)),
            ]
            + [whole(e.shape) for e in extra],
            out_specs=[whole(o.shape) for o in outs],
            scratch_shapes=[
                pltpu.VMEM((total, 3 * width), BF16),
                pltpu.VMEM((3, total, width), F32),
            ],
        ),
        compiler_params=params(14),
        cost_estimate=pl.CostEstimate(
            flops=18 * total * width * width, bytes_accessed=18 * width * width, transcendentals=0
        ),
    )(own, act, near, farther, weights, *extra)


CHUNK = 128


def chunks(total, fn):
    def step(i, carry):
        fn(pl.multiple_of(i * CHUNK, CHUNK))
        return carry

    lax.fori_loop(0, total // CHUNK, step, 0)


def grad_two_body(rows_of, even, edge, extra, outs):
    (out,) = outs

    def one(start):
        out[pl.ds(start, CHUNK), :] = rows_of(start, CHUNK)

    chunks(out.shape[0], one)


def copy_edges(even, edge, full, near, farther):
    total = full.shape[0]
    first = full[:edge]
    last = full[total - edge :]
    near[...] = jnp.where(even, last, first)
    farther[...] = jnp.where(even, first, last)


def conv_one_body(rows_of, even, edge, extra, outs):
    grad_ref, gain_ref = extra
    act_ref, act_near, act_far, d_ref, d_near, d_far = outs
    total = act_ref.shape[0]
    gain = gain_ref[...]

    def one(start):
        rows = pl.ds(start, CHUNK)
        conv = rows_of(start, CHUNK)
        r = rms(conv)
        hat = conv * r
        act, slope = silu_parts(hat * gain)
        act_ref[rows, :] = act.astype(BF16)
        g = grad_ref[rows, :] * slope * gain
        d_ref[rows, :] = (r * (g - hat * jnp.mean(g * hat, axis=-1, keepdims=True))).astype(BF16)

    chunks(total, one)
    copy_edges(even, edge, act_ref, act_near, act_far)
    copy_edges(even, edge, d_ref, d_near, d_far)


def conv_two_body(rows_of, even, edge, extra, outs):
    (lifted_ref,) = extra
    (out,) = outs

    def one(start):
        rows = pl.ds(start, CHUNK)
        out[rows, :] = (lifted_ref[rows, :].astype(F32) + rows_of(start, CHUNK)).astype(BF16)

    chunks(out.shape[0], one)


def grad_one_body(rows_of, even, edge, extra, outs):
    lifted_ref, cot_ref, gain_ref, wo_ref = extra
    d_lifted_ref, d_mixed_ref = outs
    gain = gain_ref[...]
    total = d_lifted_ref.shape[0]

    def one(start):
        rows = pl.ds(start, CHUNK)
        lifted = lifted_ref[rows, :].astype(F32)
        r = rms(lifted)
        hat = lifted * r
        _, slope = silu_parts(hat * gain)
        g = rows_of(start, CHUNK) * slope * gain
        back = r * (g - hat * jnp.mean(g * hat, axis=-1, keepdims=True))
        d_lifted_ref[rows, :] = cot_ref[rows, :].astype(F32) + back

    chunks(total, one)
    d_mixed_ref[...] = mm_t(d_lifted_ref[...].astype(BF16), wo_ref[...]).astype(BF16)


def head_norm_back(grad, hat, r, ones, head):
    hat = hat.astype(F32)
    return r * (grad - hat * head_mean(grad * hat, ones, head))


def pair_grads(p, head, q_ref, v_ref, vf_ref, e_ref, dm_ref, row_ref, col_ref, low):
    blk = q_ref.shape[1]
    cols = slice(128 * p, 128 * (p + 1))
    row = jnp.concatenate([row_ref[0, 2 * p : 2 * p + 1], row_ref[0, 2 * p + 1 : 2 * p + 2]], axis=1)
    col = jnp.where(low, col_ref[0, :, 2 * p : 2 * p + 1], col_ref[0, :, 2 * p + 1 : 2 * p + 2])
    dm = dm_ref[:, 0, :, cols].reshape(blk, 128).astype(F32)
    q2 = pair_rows(q_ref[0, :, cols], low)
    dm2 = pair_rows((dm * col).astype(BF16), low)
    e = e_ref[0, p].astype(F32)
    slope = jnp.concatenate([mm_t(v_ref[0, :, cols], dm2), mm_t(vf_ref[0, :, cols], dm2)], axis=0)
    drift = jnp.sum(e * slope, axis=0, keepdims=True) * row
    return q2, dm2, (e * (slope - drift)).astype(BF16)


def far_grads_kernel(head, picks, own_s, lists_s, counts_s, q_ref, v_ref, vf_ref, e_ref, dm_ref,
                     row_ref, col_ref, kf_ref, rf_ref, wk_ref, wv_ref, send_ref, kgrad, vgrad, shares, sems):
    c = pl.program_id(0)
    q_ref, v_ref, vf_ref, e_ref, row_ref, col_ref, kf_ref, rf_ref = (
        camera(r, c) for r in (q_ref, v_ref, vf_ref, e_ref, row_ref, col_ref, kf_ref, rf_ref)
    )
    dm_ref = camera_slabs(dm_ref, c)
    own = own_s[0]
    blk, width = q_ref.shape[1:]
    low = lax.broadcasted_iota(jnp.int32, (blk, 128), 1) < head
    ones_h = head_ones(width // 2, head)
    for p in range(width // 128):
        cols = slice(128 * p, 128 * (p + 1))
        q2, dm2, d_scaled = pair_grads(
            p, head, q_ref, v_ref, vf_ref, e_ref, dm_ref, row_ref, col_ref, low
        )
        kgrad[:, cols] = mm(d_scaled[blk:], q2)
        vgrad[:, cols] = mm(e_ref[0, p, blk:], dm2).astype(BF16)
    far_k = head_norm_back(kgrad[...], kf_ref[0], rf_ref[0], ones_h, head).astype(BF16)
    share = mm_t(far_k, wk_ref[...]) + mm_t(vgrad[...], wv_ref[...])
    share = share.astype(BF16)
    for s in range(picks):
        shares[c, s] = share[s * blk : (s + 1) * blk]
        pltpu.make_async_copy(
            shares.at[c, s], send_ref.at[lists_s[c, own, s]], sems.at[c, s]
        ).start()

    @pl.when(c == pl.num_programs(0) - 1)
    def _():
        for i in range(shares.shape[0]):
            for s in range(picks):
                pltpu.make_async_copy(shares.at[i, s], send_ref.at[0], sems.at[i, s]).wait()


def far_grads(own, lists, counts, n_cols, q, v, vf, e, dm_t, row, col, kf, rf, wk, wv, head):
    tw, cams, nr, width = dm_t.shape
    blk = tw * nr
    picks = lists.shape[2]
    args = (q, v, vf, e, dm_t, row, col, kf, rf, wk, wv)
    return pl.pallas_call(
        functools.partial(far_grads_kernel, head, picks),
        name="far_grads",
        out_shape=pltpu.HBM((n_cols, blk, width), BF16),
        grid_spec=pltpu.PrefetchScalarGridSpec(
            num_scalar_prefetch=3,
            grid=(cams,),
            in_specs=[whole(x.shape) for x in args],
            out_specs=pl.BlockSpec(memory_space=pltpu.HBM),
            scratch_shapes=[
                pltpu.VMEM((picks * blk, width), F32),
                pltpu.VMEM((picks * blk, width), BF16),
                pltpu.VMEM((cams, picks, blk, width), BF16),
                pltpu.SemaphoreType.DMA((cams, picks)),
            ],
        ),
        compiler_params=params(6 + 5 * picks),
    )(own, lists, counts, *args)


def own_grads_kernel(head, q_ref, v_ref, vf_ref, e_ref, dm_ref, row_ref, col_ref, k_ref, kf_ref,
                     rq_ref, rk_ref, wq_ref, wk_ref, wv_ref, out_ref):
    c = pl.program_id(0)
    q_ref, v_ref, vf_ref, e_ref, row_ref, col_ref, k_ref, kf_ref, rq_ref, rk_ref, out_ref = (
        camera(r, c)
        for r in (q_ref, v_ref, vf_ref, e_ref, row_ref, col_ref, k_ref, kf_ref, rq_ref, rk_ref, out_ref)
    )
    dm_ref = camera_slabs(dm_ref, c)
    blk, width = q_ref.shape[1:]
    low = lax.broadcasted_iota(jnp.int32, (blk, 128), 1) < head
    ones_h = head_ones(width // 2, head)
    scale = head ** (-0.5)
    dq, dk, dv = [], [], []
    for p in range(width // 128):
        cols = slice(128 * p, 128 * (p + 1))
        q2, dm2, d_scaled = pair_grads(
            p, head, q_ref, v_ref, vf_ref, e_ref, dm_ref, row_ref, col_ref, low
        )
        dk.append(mm(d_scaled[:blk], q2))
        dv.append(mm(e_ref[0, p, :blk], dm2).astype(BF16))
        flipped = jnp.transpose(d_scaled)
        both = mm(flipped[:, :blk], k_ref[0, :, cols]) + mm(flipped[:, blk:], kf_ref[0, :, cols])
        dq.append(jnp.where(low, both[:blk], both[blk:]) * scale)
    dq, dk, dv = (jnp.concatenate(parts, axis=1) for parts in (dq, dk, dv))
    q_hat = q_ref[0].astype(F32) * (1.0 / scale)
    dq = head_norm_back(dq, q_hat, rq_ref[0], ones_h, head).astype(BF16)
    dk = head_norm_back(dk, k_ref[0], rk_ref[0], ones_h, head).astype(BF16)
    out_ref[0] = mm_t(dq, wq_ref[...]) + mm_t(dk, wk_ref[...]) + mm_t(dv, wv_ref[...])


def own_grads(q, v, vf, e, dm_t, row, col, k, kf, rq, rk, wq, wk, wv, head):
    tw, cams, nr, width = dm_t.shape
    blk = tw * nr
    args = (q, v, vf, e, dm_t, row, col, k, kf, rq, rk, wq, wk, wv)
    return pl.pallas_call(
        functools.partial(own_grads_kernel, head),
        name="own_grads",
        out_shape=pltpu.VMEM((cams, blk, width), F32),
        grid_spec=pltpu.PrefetchScalarGridSpec(
            num_scalar_prefetch=0,
            grid=(cams,),
            in_specs=[whole(x.shape) for x in args],
            out_specs=whole((cams, blk, width)),
        ),
        compiler_params=params(12 + e.shape[2] * 8 // 256),
        cost_estimate=pl.CostEstimate(
            flops=20 * cams * blk * width * width, bytes_accessed=4 * e.size, transcendentals=0
        ),
    )(*args)


def final_kernel(own_s, match_s, lists_s, counts_s, back_ref, rows_ref, clip_ref, dl_ref, gain_ref, out_ref, acc):
    cams, n_cols, picks = lists_s.shape
    own = own_s[0]
    me = pl.program_id(0)
    rows_ref = camera(rows_ref, me)
    clip_ref, dl_ref, out_ref = (camera_slabs(r, me) for r in (clip_ref, dl_ref, out_ref))
    tw, _, nr, width = clip_ref.shape
    blk = tw * nr
    source = jnp.int32(0)
    for c in range(cams):
        source = jnp.where(match_s[c] == me, c, source)
    acc[...] = rows_ref[0]
    for i in range(n_cols):
        hit = jnp.bool_(False)
        for s in range(picks):
            hit = hit | ((lists_s[source, i, s] == own) & (s < counts_s[source, i]))

        @pl.when(hit)
        def _():
            acc[...] += back_ref[i].astype(F32)

    x = clip_ref[:, 0].reshape(blk, width).astype(F32)
    r = rms(x)
    hat = x * r
    g = acc[...] * gain_ref[...]
    d = dl_ref[:, 0].reshape(blk, width) + r * (
        g - hat * jnp.mean(g * hat, axis=-1, keepdims=True)
    )
    out_ref[:, 0] = d.astype(BF16).reshape(tw, nr, width)


def final(own, matching, lists, counts, back, rows, clip_t, d_lifted, gain):
    tw, cams, nr, width = clip_t.shape
    blk = tw * nr
    slab = pl.BlockSpec((tw, 1, nr, width), lambda c, *_: (0, c, 0, 0))
    return pl.pallas_call(
        final_kernel,
        name="final",
        out_shape=jax.ShapeDtypeStruct(clip_t.shape, BF16),
        grid_spec=pltpu.PrefetchScalarGridSpec(
            num_scalar_prefetch=4,
            grid=(cams,),
            in_specs=[whole(a.shape) for a in (back, rows, clip_t, d_lifted, gain)],
            out_specs=whole(clip_t.shape),
            scratch_shapes=[pltpu.VMEM((blk, width), F32)],
        ),
        compiler_params=params(8),
    )(own, matching, lists, counts, back, rows, clip_t, d_lifted, gain)


def exchange_edges(near, farther):
    size = lax.axis_size("cols")
    inner = [(i, i ^ 1) for i in range(size)]
    outer = [(i, i + 1 if i % 2 else i - 1) for i in range(1, size - 1)]
    return lax.ppermute(near, "cols", inner), lax.ppermute(farther, "cols", outer)


def local(
    clip_tokens,
    cotangent,
    gain_attn,
    w_query,
    w_key,
    w_value,
    w_out,
    gain_first,
    conv_first,
    gain_second,
    conv_second,
    matching,
    block_lists,
    counts,
):
    views, nr, tw, width = clip_tokens.shape
    head = width // HEADS
    n_cols = lax.axis_size("cols")
    own_index = lax.axis_index("cols").astype(jnp.int32)
    own = own_index.reshape(1)
    total = views * nr * tw
    blk = nr * tw
    flat = (total, width)
    slabs = (tw, views, nr, width)
    gain_attn = gain_attn.reshape(1, width)
    gain_first = gain_first.reshape(1, width)
    gain_second = gain_second.reshape(1, width)

    clip_t = jnp.transpose(clip_tokens, (2, 0, 1, 3))
    cot_t = jnp.transpose(cotangent, (2, 0, 1, 3))
    odd = own_index % 2
    last = (tw - 1) * (1 - odd)
    cot_near = lax.dynamic_index_in_dim(cot_t, last, 0, keepdims=False).reshape(-1, width)
    cot_far = lax.dynamic_index_in_dim(cot_t, tw - 1 - last, 0, keepdims=False).reshape(-1, width)

    rows, send = prep(n_cols, own, matching, block_lists, counts, clip_t, gain_attn)
    arrived = lax.all_to_all(send, "cols", split_axis=0, concat_axis=0, tiled=True)
    w_value_t = w_value.T
    q, k, v, vt, rq, rk = project(rows.reshape(flat), w_query, w_key, w_value, w_value_t, head, blk)
    q, k, v, rq, rk = (a.reshape(views, blk, width) for a in (q, k, v, rq, rk))
    arrived, q, k, v, vt, rq, rk, cot_t, cot_near, cot_far = lax.optimization_barrier(
        (arrived, q, k, v, vt, rq, rk, cot_t, cot_near, cot_far)
    )
    cot_near, cot_far = exchange_edges(cot_near, cot_far)
    lifted, act_one, near, farther, kf, rf, e, row, col = attend(
        own, block_lists, counts, arrived, q, k, vt, clip_t, w_key, w_value_t, w_out, gain_first, head
    )
    edge = (views * nr, width)
    near, farther = exchange_edges(near.reshape(edge), farther.reshape(edge))
    (d_act_two,) = conv_call(
        "grad_two", grad_two_body, own, cot_t.reshape(flat), cot_near, cot_far, conv_second,
        (), (pltpu.VMEM(flat, F32),), nr, True,
    )
    flat_bf = pltpu.VMEM(flat, BF16)
    edge_bf = jax.ShapeDtypeStruct(edge, BF16)
    act_two, act_near, act_far, d_conv, d_near, d_far = conv_call(
        "conv_one", conv_one_body, own, act_one.reshape(flat), near, farther, conv_first,
        (d_act_two, gain_second),
        (flat_bf, edge_bf, edge_bf, flat_bf, edge_bf, edge_bf), nr, False,
    )
    d_near, d_far = exchange_edges(d_near, d_far)
    vf = far_values(own, block_lists, arrived, w_value)
    d_near, d_far, vf = lax.optimization_barrier((d_near, d_far, vf))
    d_lifted, d_mixed = conv_call(
        "grad_one", grad_one_body, own, d_conv, d_near, d_far, conv_first,
        (lifted.reshape(flat), cot_t.reshape(flat), gain_first, w_out),
        (pltpu.VMEM(flat, F32), flat_bf), nr, True,
    )
    d_mixed, act_near, act_far = lax.optimization_barrier((d_mixed, act_near, act_far))
    d_mixed = d_mixed.reshape(slabs)
    act_near, act_far = exchange_edges(act_near, act_far)
    send_back = far_grads(
        own, block_lists, counts, n_cols, q, v, vf, e, d_mixed, row, col, kf, rf, w_key, w_value, head
    )
    send_back, act_near, act_far = lax.optimization_barrier((send_back, act_near, act_far))
    back = lax.all_to_all(send_back, "cols", split_axis=0, concat_axis=0, tiled=True)
    (result,) = conv_call(
        "conv_two", conv_two_body, own, act_two, act_near, act_far, conv_second,
        (lifted.reshape(flat),), (jax.ShapeDtypeStruct(flat, BF16),), nr, False,
    )
    d_rows = own_grads(
        q, v, vf, e, d_mixed, row, col, k, kf, rq, rk, w_query, w_key, w_value, head
    )
    d_clip = final(own, matching, block_lists, counts, back, d_rows, clip_t, d_lifted.reshape(slabs), gain_attn)
    return (
        jnp.transpose(result.reshape(slabs), (1, 2, 0, 3)),
        jnp.transpose(d_clip, (1, 2, 0, 3)),
    )


def solution(mesh):
    tiles = P("groups", None, "cols", None)
    in_specs = (tiles, tiles) + (P(),) * 12
    return jax.shard_map(
        local, mesh=mesh, in_specs=in_specs, out_specs=(tiles, tiles), check_vma=False
    )
```

time: 245 us -> 208 us (0.85)
  waiting for transfers between devices: 87.3 us -> 36 us
  local copies, waits for them, and re-layouts: 16.4 us -> 53.1 us
  Pallas kernels: 112 us -> 89.8 us
    ppermute x4, waiting for transfers between devices: 52 us -> 2.16 us  [exchange_edges(): lax.ppermute(farther, 'cols', outer)]
    unnamed x27 -> x138, local copies, waits for them, and re-layouts: 11.4 us -> 47.5 us
    pallas_call x4, Pallas kernels: 47.9 us -> 26.5 us  [conv_call(): pl.pallas_call(functools.partial(conv_kernel, body, len(extra), transpose...]
    all_to_all x1, waiting for transfers between devices: 35.3 us -> 28.3 us  [local(): lax.all_to_all(send, 'cols', split_axis=0, concat_axis=0, tiled=True)]
    all_to_all x1, waiting for transfers between devices: 0.01 us -> 5.5 us  [local(): lax.all_to_all(send_back, 'cols', split_axis=0, concat_axis=0, tiled=True)]
    pallas_call x4 -> x5, Pallas kernels: 42.8 us -> 45.2 us  [the longest x1 16.8 us: own_grads(): pl.pallas_call(functools.partial(own_grads_kernel, head), name='own_grads...]
  transfers between devices with their start and end apart: 10 -> 10, of which waited for: 3 -> 3; matrix products, arithmetic and copies ran while one was open for 2% -> 4% of each run, Pallas kernels for 18% -> 31%
where the time goes in v2:
time: 208 us; the launch traced here: 207 us
  Pallas kernels  89.8 us (43%)
  local copies, waits for them, and re-layouts  53.1 us (26%)
  waiting for transfers between devices  36 us (17%)
  starting transfers between devices  26.7 us (13%)
    unnamed x138, local copies, waits for them, and re-layouts  47.5 us
    all_to_all x1, waiting for transfers between devices, local(): lax.all_to_all(send, 'cols', split_axis=0, concat_axis=0, tiled=True)  28.3 us
    pallas_call x4, Pallas kernels, conv_call(): pl.pallas_call(functools.partial(conv_kernel, body, len(extra), transpose...  26.5 us
    pallas_call x1, Pallas kernels, own_grads(): pl.pallas_call(functools.partial(own_grads_kernel, head), name='own_grads...  16.8 us
    pallas_call x1, Pallas kernels, far_grads(): pl.pallas_call(functools.partial(far_grads_kernel, head, picks), name='fa...  16 us
    pallas_call x1, Pallas kernels, attend(): pl.pallas_call(functools.partial(attend_kernel, head, picks), name='atten...  14.8 us
    ppermute x4, starting transfers between devices, exchange_edges(): lax.ppermute(farther, 'cols', outer)  13.5 us
    all_to_all x1, starting transfers between devices, local(): lax.all_to_all(send, 'cols', split_axis=0, concat_axis=0, tiled=True)  6.56 us
  transfers between devices with their start and end apart: 10, of which 3 were waited for; matrix products, arithmetic and copies ran while one was open for 4% of the time, Pallas kernels for 31%

profile of v2, /device:TPU:13, one launch (start us, length us, event | category | flops | bytes accessed | tf_op | source)
XLA Modules:
  0.0 207.0 jit_solution(4260797097168519372)
XLA Ops:
  1.4 1.4 copy.43
  4.9 3.4 %prep.1 = (bf16[7,128,512]{2,1,0:T(8,128)(2,1)S(1)}, bf16[16,128,512]{2,1,0:T(8,128)(2,1)}) custom-call(s32[1]{0:T(128)} %bitcast.own_s, s32[7]{0:T(128)S(1)} %copy-done.49, s32[7,16,2]{2,1,0:T(8,128)S(1)} %copy.31.lists_s, s32[7,16]{1,0:T(8,128)S(1)} %copy-done.44, bf16[4,7,32,512]{3,2,1,0:T(8,128)(2,1)S(1)} %bitcast.29, f32[1,512]{1,0:T(1,128)S(1)} %bitcast.50), custom_call_target="tpu_custom_call" | custom-call | tf_op jit(solution)/shard_map/prep/pallas_call | solution.py:98
  9.2 6.6 %all-to-all-start = ((bf16[16,128,512]{2,1,0:T(8,128)(2,1)}), bf16[16,128,512]{2,1,0:T(8,128)(2,1)S(1)}, u32[]{:S(2)}, u32[]{:S(2)}) async-start(bf16[16,128,512]{2,1,0:T(8,128)(2,1)} %get-tuple-element.46), calls=%async_computation | async-start | bytes 4194304 | tf_op jit(solution)/shard_map/all_to_all | solution.py:698
  15.8 2.6 %constant_dynamic-slice_fusion = (bf16[7,32,1,512]{3,2,1,0:T(2,128)(2,1)S(1)}, bf16[7,32,1,512]{3,2,1,0:T(2,128)(2,1)S(1)}) fusion(bf16[7,32,4,512]{3,2,1,0:T(4,128)(2,1)} %param.15, s32[]{:T(128)S(6)} %select_n.16, s32[]{:T(128)S(6)} %select_n.15), kind=kLoop, calls=%fused_computation.2 | loop fusion | bytes 917512 | tf_op jit(solution)/shard_map/dynamic-slice.1
  20.8 1.0 copy-done.12
  21.9 1.0 copy-done.23
  22.9 1.0 copy-done.40
  23.9 1.2 copy-done.56
  25.1 3.5 %project.1 = (bf16[896,512]{1,0:T(8,128)(2,1)S(1)}, bf16[896,512]{1,0:T(8,128)(2,1)S(1)}, bf16[896,512]{1,0:T(8,128)(2,1)S(1)}, bf16[7,512,128]{2,1,0:T(8,128)(2...) custom-call(bf16[896,512]{1,0:T(8,128)(2,1)S(1)} %bitcast.58, bf16[512,512]{1,0:T(8,128)(2,1)S(1)} %copy-done.40, ...), custom_call_target="tpu_custom_call" | custom-call | flops 1879048192 | bytes 9175040 | tf_op jit(solution)/shard_map/project/pallas_call | solution.py:139
  31.4 1.2 copy-done.29
  32.7 1.2 copy-done.31
  34.9 28.3 %all-to-all-done.refs_0_.arrived_ref = bf16[16,128,512]{2,1,0:T(8,128)(2,1)S(1)} async-done(((bf16[16,128,512]{2,1,0:T(8,128)(2,1)}), bf16[16,128,512]{2,1,0:T(8,128)(2,1)S(1)}, u32[]{:S(2)}, u32[]{:S(2)}) %all-to-all-start) | async-done | bytes 2097184 | tf_op jit(solution)/shard_map/all_to_all | solution.py:698
  63.4 3.5 %collective-permute-start.3 = (bf16[224,512]{1,0:T(8,128)(2,1)}, bf16[224,512]{1,0:T(8,128)(2,1)S(1)}, u32[]{:S(2)}, u32[]{:S(2)}) collective-permute-start(bf16[224,512]{1,0:T(8,128)(2,1)} %bitcast.65), channel_id=1, source_target_pairs={{1,2},{2,1},{3,4},{4,3},{5,6},{6,5},{7,8},{8,7},{9,10},{10,9},{11,... | collective-permute-start | bytes 688136 | tf_op jit(solution)/shard_map/ppermute | solution.py:658
  66.9 1.4 copy.32
  68.3 1.2 copy-done.16
  69.5 1.0 copy-done.24
  71.3 1.2 copy-done.38
  72.5 1.0 copy-done.39
  73.6 14.8 %attend.1 = (bf16[4,7,32,512]{3,2,1,0:T(8,128)(2,1)S(1)}, bf16[4,7,32,512]{3,2,1,0:T(8,128)(2,1)S(1)}, bf16[7,32,512]{2,1,0:T(8,128)(2,1)S(1)}, bf16[7,32,512]{2...) custom-call(s32[1]{0:T(128)} %bitcast.own_s, ...), custom_call_target="tpu_custom_call" | custom-call | tf_op jit(solution)/shard_map/attend/pallas_call | solution.py:261
  88.5 3.1 %collective-permute-start.1 = (bf16[224,512]{1,0:T(8,128)(2,1)S(1)}, bf16[224,512]{1,0:T(8,128)(2,1)S(1)}, u32[]{:S(2)}, u32[]{:S(2)}) collective-permute-start(bf16[224,512]{1,0:T(8,128)(2,1)S(1)} %bitcast.60), channel_id=1, source_target_pairs={{1,2},{2,1},{3,4},{4,3},{5,6},{6,5},{7,8},{8,7},{9,10},{10,9},{11,... | collective-permute-start | bytes 688136 | tf_op jit(solution)/shard_map/ppermute | solution.py:658
  91.6 2.3 %copy-done.51 = bf16[3,3,512,512]{3,2,1,0:T(8,128)(2,1)S(1)} copy-done((bf16[3,3,512,512]{3,2,1,0:T(8,128)(2,1)S(1)}, bf16[3,3,512,512]{3,2,1,0:T(8,128)(2,1)}, u32[]{:S(2)}) %copy-start.51) | copy-done | bytes 4718616
  94.0 5.5 %grad_two.1.refs_0_ = f32[896,512]{1,0:T(8,128)S(1)} custom-call(s32[1]{0:T(128)} %bitcast.own_s, bf16[896,512]{1,0:T(8,128)(2,1)S(1)} %bitcast.47, bf16[224,512]{1,0:T(8,128)(2,1)S(1)} %collective-permute-done.2.near_ref, bf16[224,512]{1,0:T(8,128)(2,1)S(1)} %collective-permute-done.3.farther_ref, bf16[3,3,512,512]{3,2,1,0:T(8,128)(2,1)S(1)} %copy-done.51), custom_call_target="tpu_custom_call" | custom-call | flops 4227858432 | bytes 4718592 | tf_op jit(solution)/shard_map/grad_two/pallas_call | solution.py:368
  99.5 7.3 %conv_one.1 = (bf16[896,512]{1,0:T(8,128)(2,1)S(1)}, bf16[224,512]{1,0:T(8,128)(2,1)S(1)}, bf16[224,512]{1,0:T(8,128)(2,1)S(1)}, bf16[896,512]{1,0:T(8,128)(2,1)...) custom-call(s32[1]{0:T(128)} %bitcast.own_s, bf16[896,512]{1,0:T(8,128)(2,1)S(1)} %bitcast.59, ...), custom_call_target="tpu_custom_call" | custom-call | flops 4227858432 | bytes 4718592 | tf_op jit(solution)/shard_map/conv_one/pallas_call | solution.py:368
  107.0 3.6 %collective-permute-start.5 = (bf16[224,512]{1,0:T(8,128)(2,1)S(1)}, bf16[224,512]{1,0:T(8,128)(2,1)S(1)}, u32[]{:S(2)}, u32[]{:S(2)}) collective-permute-start(bf16[224,512]{1,0:T(8,128)(2,1)S(1)} %get-tuple-element.67), channel_id=1, source_target_pairs={{1,2},{2,1},{3,4},{4,3},{5,6},{6,5},{7,8},{8,7},{9,10},{10,9},{11,... | collective-permute-start | bytes 688136 | tf_op jit(solution)/shard_map/ppermute | solution.py:658
  110.5 2.6 %far_values.1.vf_ref = bf16[7,256,512]{2,1,0:T(8,128)(2,1)S(1)} custom-call(s32[1]{0:T(128)} %bitcast.own_s, s32[7,16,2]{2,1,0:T(8,128)S(1)} %copy-done.27, bf16[16,128,512]{2,1,0:T(8,128)(2,1)S(1)} %all-to-all-done.refs_0_.arrived_ref, bf16[512,512]{1,0:T(8,128)(2,1)S(1)} %copy-done.4), custom_call_target="tpu_custom_call" | custom-call | flops 939524096 | bytes 3670016 | tf_op jit(solution)/shard_map/far_values/pallas_call | solution.py:290
  113.2 2.1 %collective-permute-done.5.farther_ref = bf16[224,512]{1,0:T(8,128)(2,1)S(1)} collective-permute-done((bf16[224,512]{1,0:T(8,128)(2,1)S(1)}, bf16[224,512]{1,0:T(8,128)(2,1)S(1)}, u32[]{:S(2)}, u32[]{:S(2)}) %collective-permute-start.5) | collective-permute-done | bytes 229408 | tf_op jit(solution)/shard_map/ppermute | solution.py:658
  115.3 8.0 %grad_one.1 = (f32[896,512]{1,0:T(8,128)S(1)}, bf16[896,512]{1,0:T(8,128)(2,1)S(1)}) custom-call(s32[1]{0:T(128)} %bitcast.own_s, bf16[896,512]{1,0:T(8,128)(2,1)S(1)} %get-tuple-element.70.act_ref, bf16[224,512]{1,0:T(8,128)(2,1)S(1)} %collective-permute-done.4.near_ref, bf16[224,512]{1,0:T(8,128)(2,1)S(1)} %collective-permute-done.5.farther_ref, ...), custom_call_target="tpu_custom_call" | custom-call | flops 4227858432 | bytes 4718592 | tf_op jit(solution)/shard_map/grad_one/pallas_call | solution.py:368
  123.4 2.0 collective-permute-start.6
  125.4 3.4 %collective-permute-start.7 = (bf16[224,512]{1,0:T(8,128)(2,1)S(1)}, bf16[224,512]{1,0:T(8,128)(2,1)S(1)}, u32[]{:S(2)}, u32[]{:S(2)}) collective-permute-start(bf16[224,512]{1,0:T(8,128)(2,1)S(1)} %get-tuple-element.83), channel_id=1, source_target_pairs={{1,2},{2,1},{3,4},{4,3},{5,6},{6,5},{7,8},{8,7},{9,10},{10,9},{11,... | collective-permute-start | bytes 688136 | tf_op jit(solution)/shard_map/ppermute | solution.py:658
  128.8 16.0 %far_grads.1 = bf16[16,128,512]{2,1,0:T(8,128)(2,1)} custom-call(s32[1]{0:T(128)} %bitcast.own_s, s32[7,16,2]{2,1,0:T(8,128)S(1)} %copy-done.27, s32[7,16]{1,0:T(8,128)S(1)} %copy-done.45, bf16[7,128,512]{2,1,0:T(8,128)(2,1)S(1)} %bitcast.33, bf16[7,128,512]{2,1,0:T(8,128)(2,1)S(1)} %bitcast.38, bf16[7,256,512]{2,1,0:T(8,128)(2,1)S(1)} %far_values.1.vf_ref, ...), custom_call_target="tpu_custom_call" | custom-call | tf_op jit(solution)/shard_map/far_grads/pallas_call | solution.py:533
  145.6 4.3 %all-to-all-start.1 = ((bf16[16,128,512]{2,1,0:T(8,128)(2,1)}), bf16[16,128,512]{2,1,0:T(8,128)(2,1)}, u32[]{:S(2)}, u32[]{:S(2)}) async-start(bf16[16,128,512]{2,1,0:T(8,128)(2,1)} %far_grads.1), calls=%async_computation.1 | async-start | bytes 4194304 | tf_op jit(solution)/shard_map/all_to_all | solution.py:737
  150.0 2.6 %copy-done.1 = bf16[7,4,384,256]{3,2,1,0:T(8,128)(2,1)S(1)} copy-done((bf16[7,4,384,256]{3,2,1,0:T(8,128)(2,1)S(1)}, bf16[7,4,384,256]{3,2,1,0:T(8,128)(2,1)}, u32[]{:S(2)}) %copy-start.1) | copy-done | bytes 5505048
  152.5 1.2 copy-done.7
  153.7 1.5 copy-done.9
  155.2 1.0 copy-done.14
  156.2 1.2 copy-done.17
  157.4 1.2 copy-done.20
  158.6 1.2 copy-done.22
  159.8 1.5 copy-done.30
  161.3 1.5 copy-done.32
  164.8 16.8 %own_grads.1.rows_ref = f32[7,128,512]{2,1,0:T(8,128)S(1)} custom-call(bf16[7,128,512]{2,1,0:T(8,128)(2,1)S(1)} %bitcast.34, bf16[7,128,512]{2,1,0:T(8,128)(2,1)S(1)} %bitcast.39, bf16[7,256,512]{2,1,0:T(8,128)(2,1)S(1)} %copy-done.3, bf16[7,4,384,256]{3,2,1,0:T(8,128)(2,1)S(1)} %copy-done.1, bf16[4,7,32,512]{3,2,1,0:T(8,128)(2,1)S(1)} %bitcast.41, ...), custom_call_target="tpu_custom_call" | custom-call | flops 4697620480 | bytes 11010048 | tf_op jit(solution)/shard_map/own_grads/pallas_call | solution.py:587
  181.7 3.0 %copy-done.52 = bf16[3,3,512,512]{3,2,1,0:T(8,128)(2,1)S(1)} copy-done((bf16[3,3,512,512]{3,2,1,0:T(8,128)(2,1)S(1)}, bf16[3,3,512,512]{3,2,1,0:T(8,128)(2,1)}, u32[]{:S(2)}) %copy-start.52) | copy-done | bytes 4718616
  184.6 5.6 %conv_two.1 = bf16[896,512]{1,0:T(8,128)(2,1)S(1)} custom-call(s32[1]{0:T(128)} %bitcast.own_s, bf16[896,512]{1,0:T(8,128)(2,1)S(1)} %copy-done.63, bf16[224,512]{1,0:T(8,128)(2,1)S(1)} %copy-done.58, bf16[224,512]{1,0:T(8,128)(2,1)S(1)} %copy-done.60, bf16[3,3,512,512]{3,2,1,0:T(8,128)(2,1)S(1)} %copy-done.52, bf16[896,512]{1,0:T(8,128)(2,1)S(1)} %bitcast.57), custom_call_target="tpu_custom_call" | custom-call | flops 4227858432 | bytes 4718592 | tf_op jit(solution)/shard_map/conv_two/pallas_call | solution.py:368
  190.3 1.6 copy.42
  191.9 5.5 %all-to-all-done.1.back_ref = bf16[16,128,512]{2,1,0:T(8,128)(2,1)} async-done(((bf16[16,128,512]{2,1,0:T(8,128)(2,1)}), bf16[16,128,512]{2,1,0:T(8,128)(2,1)}, u32[]{:S(2)}, u32[]{:S(2)}) %all-to-all-start.1) | async-done | bytes 2097184 | tf_op jit(solution)/shard_map/all_to_all | solution.py:737
  197.4 1.5 copy-done.34
  198.9 6.4 %final.1 = bf16[4,7,32,512]{3,2,1,0:T(8,128)(2,1)S(1)} custom-call(s32[1]{0:T(128)} %bitcast.own_s, s32[7]{0:T(128)S(1)} %copy-done.50, s32[7,16,2]{2,1,0:T(8,128)S(1)} %copy-done.28, s32[7,16]{1,0:T(8,128)S(1)} %copy-done.45, bf16[16,128,512]{2,1,0:T(8,128)(2,1)} %all-to-all-done.1.back_ref, f32[7,128,512]{2,1,0:T(8,128)S(1)} %copy-done.11, ...), custom_call_target="tpu_custom_call" | custom-call | tf_op jit(solution)/shard_map/final/pallas_call | solution.py:639
  205.3 1.6 copy.37
  (125 shorter events, 14.1 us)
Async XLA Ops:
  1.4 7.7 %copy-start.25 = (s32[7,16,2]{2,1,0:T(8,128)}, s32[7,16,2]{2,1,0:T(8,128)S(1)}, u32[]{:S(2)}) copy-start(s32[7,16,2]{2,1,0:T(8,128)S(1)} %copy.31.lists_s) | copy-start | bytes 2692
  9.2 54.0 %all-to-all-start = ((bf16[16,128,512]{2,1,0:T(8,128)(2,1)}), bf16[16,128,512]{2,1,0:T(8,128)(2,1)S(1)}, u32[]{:S(2)}, u32[]{:S(2)}) async-start(bf16[16,128,512]{2,1,0:T(8,128)(2,1)} %get-tuple-element.46), calls=%async_computation | async-start | bytes 4194304 | tf_op jit(solution)/shard_map/all_to_all | solution.py:698
  15.7 4.1 %copy-start.4 = (bf16[512,512]{1,0:T(8,128)(2,1)S(1)}, bf16[512,512]{1,0:T(8,128)(2,1)}, u32[]{:S(2)}) copy-start(bf16[512,512]{1,0:T(8,128)(2,1)} %wv_ref.5) | copy-start | bytes 1572868
  25.1 43.1 %copy-start.45 = (s32[7,16]{1,0:T(8,128)S(1)}, s32[7,16]{1,0:T(8,128)}, u32[]{:S(2)}) copy-start(s32[7,16]{1,0:T(8,128)} %counts_s.7) | copy-start | bytes 1348
  25.1 43.1 %copy-start.48 = (f32[512]{0:T(512)S(1)}, f32[512]{0:T(512)}, u32[]{:S(2)}) copy-start(f32[512]{0:T(512)} %param.21) | copy-start | bytes 6148
  63.2 5.1 %copy-start.6 = (bf16[896,512]{1,0:T(8,128)(2,1)S(1)}, bf16[896,512]{1,0:T(8,128)(2,1)}, u32[]{:S(2)}) copy-start(bf16[896,512]{1,0:T(8,128)(2,1)} %copy-done.5) | copy-start | bytes 2752516
  63.2 5.1 %copy-start.13 = (bf16[512,512]{1,0:T(8,128)(2,1)S(1)}, bf16[512,512]{1,0:T(8,128)(2,1)}, u32[]{:S(2)}) copy-start(bf16[512,512]{1,0:T(8,128)(2,1)} %wk_ref.5) | copy-start | bytes 1572868
  63.2 28.4 %collective-permute-start.2 = (bf16[224,512]{1,0:T(8,128)(2,1)}, bf16[224,512]{1,0:T(8,128)(2,1)S(1)}, u32[]{:S(2)}, u32[]{:S(2)}) collective-permute-start(bf16[224,512]{1,0:T(8,128)(2,1)} %bitcast.66), channel_id=1, source_target_pairs={{0,1},{1,0},{2,3},{3,2},{4,5},{5,4},{6,7},{7,6},{8,9},{9,8},{10,11... | collective-permute-start | bytes 688136 | tf_op jit(solution)/shard_map/ppermute | solution.py:658
  63.4 28.2 %collective-permute-start.3 = (bf16[224,512]{1,0:T(8,128)(2,1)}, bf16[224,512]{1,0:T(8,128)(2,1)S(1)}, u32[]{:S(2)}, u32[]{:S(2)}) collective-permute-start(bf16[224,512]{1,0:T(8,128)(2,1)} %bitcast.65), channel_id=1, source_target_pairs={{1,2},{2,1},{3,4},{4,3},{5,6},{6,5},{7,8},{8,7},{9,10},{10,9},{11,... | collective-permute-start | bytes 688136 | tf_op jit(solution)/shard_map/ppermute | solution.py:658
  73.6 25.9 %slice-start = ((s8[4718592]{0:T(1024)(128)(4,1)}), s8[4194304]{0:T(1024)(128)(4,1)S(1)}, s32[]{:S(2)}) async-start(s8[4718592]{0:T(1024)(128)(4,1)} %bitcast.54), calls=%async_computation.2 | async-start | bytes 8388608
  88.4 27.0 %copy-start.53 = (bf16[4,7,32,512]{3,2,1,0:T(8,128)(2,1)}, bf16[4,7,32,512]{3,2,1,0:T(8,128)(2,1)S(1)}, u32[]{:S(2)}) copy-start(bf16[4,7,32,512]{3,2,1,0:T(8,128)(2,1)S(1)} %get-tuple-element.73) | copy-start | bytes 2752516
  88.4 40.4 %copy-start = (bf16[7,4,384,256]{3,2,1,0:T(8,128)(2,1)}, bf16[7,4,384,256]{3,2,1,0:T(8,128)(2,1)S(1)}, u32[]{:S(2)}) copy-start(bf16[7,4,384,256]{3,2,1,0:T(8,128)(2,1)S(1)} %get-tuple-element.69.e_ref) | copy-start | bytes 16515076
  88.4 40.4 %copy-start.8 = (bf16[7,256,512]{2,1,0:T(8,128)(2,1)}, bf16[7,256,512]{2,1,0:T(8,128)(2,1)S(1)}, u32[]{:S(2)}) copy-start(bf16[7,256,512]{2,1,0:T(8,128)(2,1)S(1)} %get-tuple-element.80.kf_ref) | copy-start | bytes 5505028
  88.4 40.4 %copy-start.35 = (f32[7,128,128]{2,1,0:T(8,128)}, f32[7,128,128]{2,1,0:T(8,128)S(1)}, u32[]{:S(2)}) copy-start(f32[7,128,128]{2,1,0:T(8,128)S(1)} %get-tuple-element.79.col_ref) | copy-start | bytes 1376260
  88.4 40.4 %copy-start.42 = (f32[7,8,128]{2,1,0:T(8,128)}, f32[7,8,128]{2,1,0:T(8,128)S(1)}, u32[]{:S(2)}) copy-start(f32[7,8,128]{2,1,0:T(8,128)S(1)} %get-tuple-element.78.row_ref) | copy-start | bytes 86020
  88.4 11.1 %collective-permute-start = (bf16[224,512]{1,0:T(8,128)(2,1)S(1)}, bf16[224,512]{1,0:T(8,128)(2,1)S(1)}, u32[]{:S(2)}, u32[]{:S(2)}) collective-permute-start(bf16[224,512]{1,0:T(8,128)(2,1)S(1)} %bitcast.61), channel_id=1, source_target_pairs={{0,1},{1,0},{2,3},{3,2},{4,5},{5,4},{6,7},{7,6},{8,9},{9,8},{10,11... | collective-permute-start | bytes 688136 | tf_op jit(solution)/shard_map/ppermute | solution.py:658
  88.5 11.0 %collective-permute-start.1 = (bf16[224,512]{1,0:T(8,128)(2,1)S(1)}, bf16[224,512]{1,0:T(8,128)(2,1)S(1)}, u32[]{:S(2)}, u32[]{:S(2)}) collective-permute-start(bf16[224,512]{1,0:T(8,128)(2,1)S(1)} %bitcast.60), channel_id=1, source_target_pairs={{1,2},{2,1},{3,4},{4,3},{5,6},{6,5},{7,8},{8,7},{9,10},{10,9},{11,... | collective-permute-start | bytes 688136 | tf_op jit(solution)/shard_map/ppermute | solution.py:658
  91.6 2.3 %copy-start.51 = (bf16[3,3,512,512]{3,2,1,0:T(8,128)(2,1)S(1)}, bf16[3,3,512,512]{3,2,1,0:T(8,128)(2,1)}, u32[]{:S(2)}) copy-start(bf16[3,3,512,512]{3,2,1,0:T(8,128)(2,1)} %w_ref.9) | copy-start | bytes 14155780
  94.0 5.5 %slice-start.1 = ((s8[4718592]{0:T(1024)(128)(4,1)}), s8[524288]{0:T(1024)(128)(4,1)S(1)}, s32[]{:S(2)}) async-start(s8[4718592]{0:T(1024)(128)(4,1)} %bitcast.54), calls=%async_computation.3 | async-start | bytes 1048576
  94.0 5.6 %copy-start.61 = (f32[512]{0:T(512)S(1)}, f32[512]{0:T(512)}, u32[]{:S(2)}) copy-start(f32[512]{0:T(512)} %param.23) | copy-start | bytes 6148
  99.5 11.0 %copy-start.27 = (s32[7,16,2]{2,1,0:T(8,128)S(1)}, s32[7,16,2]{2,1,0:T(8,128)}, u32[]{:S(2)}) copy-start(s32[7,16,2]{2,1,0:T(8,128)} %copy-done.25) | copy-start | bytes 2692
  106.9 6.3 %copy-start.62 = (bf16[896,512]{1,0:T(8,128)(2,1)}, bf16[896,512]{1,0:T(8,128)(2,1)S(1)}, u32[]{:S(2)}) copy-start(bf16[896,512]{1,0:T(8,128)(2,1)S(1)} %get-tuple-element.64.act_ref) | copy-start | bytes 2752516
  106.9 6.3 %collective-permute-start.4 = (bf16[224,512]{1,0:T(8,128)(2,1)S(1)}, bf16[224,512]{1,0:T(8,128)(2,1)S(1)}, u32[]{:S(2)}, u32[]{:S(2)}) collective-permute-start(bf16[224,512]{1,0:T(8,128)(2,1)S(1)} %get-tuple-element.66), channel_id=1, source_target_pairs={{0,1},{1,0},{2,3},{3,2},{4,5},{5,4},{6,7},{7,6},{8,9},{9,8},{10,11... | collective-permute-start | bytes 688136 | tf_op jit(solution)/shard_map/ppermute | solution.py:658
  107.0 8.3 %collective-permute-start.5 = (bf16[224,512]{1,0:T(8,128)(2,1)S(1)}, bf16[224,512]{1,0:T(8,128)(2,1)S(1)}, u32[]{:S(2)}, u32[]{:S(2)}) collective-permute-start(bf16[224,512]{1,0:T(8,128)(2,1)S(1)} %get-tuple-element.67), channel_id=1, source_target_pairs={{1,2},{2,1},{3,4},{4,3},{5,6},{6,5},{7,8},{8,7},{9,10},{10,9},{11,... | collective-permute-start | bytes 688136 | tf_op jit(solution)/shard_map/ppermute | solution.py:658
  113.2 15.7 %copy-start.2 = (bf16[7,256,512]{2,1,0:T(8,128)(2,1)}, bf16[7,256,512]{2,1,0:T(8,128)(2,1)S(1)}, u32[]{:S(2)}) copy-start(bf16[7,256,512]{2,1,0:T(8,128)(2,1)S(1)} %far_values.1.vf_ref) | copy-start | bytes 5505028
  115.3 13.5 %copy-start.19 = (bf16[896,512]{1,0:T(8,128)(2,1)S(1)}, bf16[896,512]{1,0:T(8,128)(2,1)}, u32[]{:S(2)}) copy-start(bf16[896,512]{1,0:T(8,128)(2,1)} %copy-done.18) | copy-start | bytes 2752516
  123.4 21.4 %copy-start.21 = (bf16[896,512]{1,0:T(8,128)(2,1)}, bf16[896,512]{1,0:T(8,128)(2,1)S(1)}, u32[]{:S(2)}) copy-start(bf16[896,512]{1,0:T(8,128)(2,1)S(1)} %get-tuple-element.77) | copy-start | bytes 2752516
  123.4 21.4 %copy-start.33 = (f32[896,512]{1,0:T(8,128)}, f32[896,512]{1,0:T(8,128)S(1)}, u32[]{:S(2)}) copy-start(f32[896,512]{1,0:T(8,128)S(1)} %get-tuple-element.89) | copy-start | bytes 5505028
  123.4 21.4 %collective-permute-start.6 = (bf16[224,512]{1,0:T(8,128)(2,1)S(1)}, bf16[224,512]{1,0:T(8,128)(2,1)S(1)}, u32[]{:S(2)}, u32[]{:S(2)}) collective-permute-start(bf16[224,512]{1,0:T(8,128)(2,1)S(1)} %get-tuple-element.82), channel_id=1, source_target_pairs={{0,1},{1,0},{2,3},{3,2},{4,5},{5,4},{6,7},{7,6},{8,9},{9,8},{10,11... | collective-permute-start | bytes 688136 | tf_op jit(solution)/shard_map/ppermute | solution.py:658
  125.4 19.5 %collective-permute-start.7 = (bf16[224,512]{1,0:T(8,128)(2,1)S(1)}, bf16[224,512]{1,0:T(8,128)(2,1)S(1)}, u32[]{:S(2)}, u32[]{:S(2)}) collective-permute-start(bf16[224,512]{1,0:T(8,128)(2,1)S(1)} %get-tuple-element.83), channel_id=1, source_target_pairs={{1,2},{2,1},{3,4},{4,3},{5,6},{6,5},{7,8},{8,7},{9,10},{10,9},{11,... | collective-permute-start | bytes 688136 | tf_op jit(solution)/shard_map/ppermute | solution.py:658
  144.8 5.1 %copy-start.3 = (bf16[7,256,512]{2,1,0:T(8,128)(2,1)S(1)}, bf16[7,256,512]{2,1,0:T(8,128)(2,1)}, u32[]{:S(2)}) copy-start(bf16[7,256,512]{2,1,0:T(8,128)(2,1)} %copy-done.2) | copy-start | bytes 5505028
  144.8 5.1 %copy-start.43 = (f32[7,8,128]{2,1,0:T(8,128)S(1)}, f32[7,8,128]{2,1,0:T(8,128)}, u32[]{:S(2)}) copy-start(f32[7,8,128]{2,1,0:T(8,128)} %copy-done.42) | copy-start | bytes 86020
  145.6 51.8 %all-to-all-start.1 = ((bf16[16,128,512]{2,1,0:T(8,128)(2,1)}), bf16[16,128,512]{2,1,0:T(8,128)(2,1)}, u32[]{:S(2)}, u32[]{:S(2)}) async-start(bf16[16,128,512]{2,1,0:T(8,128)(2,1)} %far_grads.1), calls=%async_computation.1 | async-start | bytes 4194304 | tf_op jit(solution)/shard_map/all_to_all | solution.py:737
  149.9 2.6 %copy-start.1 = (bf16[7,4,384,256]{3,2,1,0:T(8,128)(2,1)S(1)}, bf16[7,4,384,256]{3,2,1,0:T(8,128)(2,1)}, u32[]{:S(2)}) copy-start(bf16[7,4,384,256]{3,2,1,0:T(8,128)(2,1)} %copy-done) | copy-start | bytes 16515076
  153.7 1.5 copy-start.9
  159.8 1.5 copy-start.30
  161.3 1.5 copy-start.32
  164.8 16.8 %copy-start.54 = (bf16[4,7,32,512]{3,2,1,0:T(8,128)(2,1)S(1)}, bf16[4,7,32,512]{3,2,1,0:T(8,128)(2,1)}, u32[]{:S(2)}) copy-start(bf16[4,7,32,512]{3,2,1,0:T(8,128)(2,1)} %copy-done.53) | copy-start | bytes 2752516
  164.8 16.8 %copy-start.58 = (bf16[224,512]{1,0:T(8,128)(2,1)S(1)}, bf16[224,512]{1,0:T(8,128)(2,1)}, u32[]{:S(2)}) copy-start(bf16[224,512]{1,0:T(8,128)(2,1)} %copy-done.57) | copy-start | bytes 688132
  164.8 16.8 %copy-start.60 = (bf16[224,512]{1,0:T(8,128)(2,1)S(1)}, bf16[224,512]{1,0:T(8,128)(2,1)}, u32[]{:S(2)}) copy-start(bf16[224,512]{1,0:T(8,128)(2,1)} %copy-done.59) | copy-start | bytes 688132
  164.8 16.8 %copy-start.63 = (bf16[896,512]{1,0:T(8,128)(2,1)S(1)}, bf16[896,512]{1,0:T(8,128)(2,1)}, u32[]{:S(2)}) copy-start(bf16[896,512]{1,0:T(8,128)(2,1)} %copy-done.62) | copy-start | bytes 2752516
  181.6 8.6 %copy-start.10 = (f32[7,128,512]{2,1,0:T(8,128)}, f32[7,128,512]{2,1,0:T(8,128)S(1)}, u32[]{:S(2)}) copy-start(f32[7,128,512]{2,1,0:T(8,128)S(1)} %own_grads.1.rows_ref) | copy-start | bytes 5505028
  181.7 3.0 %copy-start.52 = (bf16[3,3,512,512]{3,2,1,0:T(8,128)(2,1)S(1)}, bf16[3,3,512,512]{3,2,1,0:T(8,128)(2,1)}, u32[]{:S(2)}) copy-start(bf16[3,3,512,512]{3,2,1,0:T(8,128)(2,1)} %w_ref.9) | copy-start | bytes 14155780
  184.6 12.8 %copy-start.28 = (s32[7,16,2]{2,1,0:T(8,128)S(1)}, s32[7,16,2]{2,1,0:T(8,128)}, u32[]{:S(2)}) copy-start(s32[7,16,2]{2,1,0:T(8,128)} %copy-done.25) | copy-start | bytes 2692
  184.6 12.8 %copy-start.47 = (f32[512]{0:T(512)S(1)}, f32[512]{0:T(512)}, u32[]{:S(2)}) copy-start(f32[512]{0:T(512)} %param.16) | copy-start | bytes 6148
  184.6 12.8 %copy-start.50 = (s32[7]{0:T(128)S(1)}, s32[7]{0:T(128)}, u32[]{:S(2)}) copy-start(s32[7]{0:T(128)} %match_s.3) | copy-start | bytes 88
  190.3 7.2 %copy-start.11 = (f32[7,128,512]{2,1,0:T(8,128)S(1)}, f32[7,128,512]{2,1,0:T(8,128)}, u32[]{:S(2)}) copy-start(f32[7,128,512]{2,1,0:T(8,128)} %copy-done.10) | copy-start | bytes 5505028
  197.4 1.5 copy-start.34
  (28 other events, 28.0 us)

commit v3 on v2

--- a/solution.py
+++ b/solution.py
@@ -140,14 +140,14 @@
         functools.partial(project_kernel, head, blk),
         name="project",
         out_shape=(
-            pltpu.VMEM(full, BF16),
-            pltpu.VMEM(full, BF16),
-            pltpu.VMEM(full, BF16),
-            pltpu.VMEM((total // blk, width, blk), BF16),
-            pltpu.VMEM(full, F32),
-            pltpu.VMEM(full, F32),
-        ),
-        compiler_params=params(8),
+            pltpu.HBM(full, BF16),
+            pltpu.HBM(full, BF16),
+            pltpu.HBM(full, BF16),
+            pltpu.HBM((total // blk, width, blk), BF16),
+            pltpu.HBM(full, F32),
+            pltpu.HBM(full, F32),
+        ),
+        compiler_params=params(12),
         cost_estimate=pl.CostEstimate(
             flops=8 * total * width * width, bytes_accessed=20 * total * width, transcendentals=0
         ),
@@ -165,13 +165,12 @@
 def attend_kernel(head, picks, own_s, lists_s, counts_s, *refs):
     (arrived_ref, q_ref, k_ref, vt_ref, clip_ref, wk_ref, wvt_ref, wo_ref, gain_ref,
      lifted_ref, act_ref, near_ref, farther_ref, kf_ref, rf_ref, e_ref, row_ref, col_ref,
-     kcat, vcat) = refs
+     mixed_ref, kcat, vcat) = refs
     c = pl.program_id(0)
-    q_ref, k_ref, vt_ref, near_ref, farther_ref, kf_ref, rf_ref, e_ref, row_ref, col_ref = (
-        camera(r, c)
-        for r in (q_ref, k_ref, vt_ref, near_ref, farther_ref, kf_ref, rf_ref, e_ref, row_ref, col_ref)
-    )
-    clip_ref, lifted_ref, act_ref = (camera_slabs(r, c) for r in (clip_ref, lifted_ref, act_ref))
+    near_ref, farther_ref, kf_ref, rf_ref, e_ref, row_ref, col_ref = (
+        r.at[pl.ds(c, 1)] for r in (near_ref, farther_ref, kf_ref, rf_ref, e_ref, row_ref, col_ref)
+    )
+    lifted_ref, act_ref = (r.at[:, pl.ds(c, 1)] for r in (lifted_ref, act_ref))
     own = own_s[0]
     count = counts_s[c, own]
     blk, width = q_ref.shape[1:]
@@ -219,6 +218,7 @@
     spread = jnp.concatenate([inverses, jnp.zeros((128 - HEADS, blk), F32)], axis=0)
     col_ref[0] = jnp.transpose(spread)
     mixed = jnp.concatenate(mixed, axis=1)
+    mixed_ref[c] = mixed
     clip = clip_ref[:, 0].reshape(blk, width).astype(F32)
     lifted = (clip + mm(mixed, wo_ref[...])).astype(BF16)
     lifted_f = lifted.astype(F32)
@@ -232,12 +232,9 @@
     farther_ref[0] = jnp.where(even, act[0], act[-1])
 
 
-def camera(ref, c):
-    return ref.at[pl.ds(c, 1)]
-
-
-def camera_slabs(ref, c):
-    return ref.at[:, pl.ds(c, 1)]
+def per_camera(x):
+    zeros = (0,) * (x.ndim - 1)
+    return pl.BlockSpec((1,) + x.shape[1:], lambda c, *_: (c,) + zeros)
 
 
 def attend(own, lists, counts, arrived, q, k, vt, clip_t, wk, wvt, wo, gain, head):
@@ -246,18 +243,20 @@
     picks = lists.shape[2]
     keys = (1 + picks) * blk
     pairs = width // 128
-    args = (arrived, q, k, vt, clip_t, wk, wvt, wo, gain)
+    slab = pl.BlockSpec((tw, 1, nr, width), lambda c, *_: (0, c, 0, 0))
     outs = (
-            pltpu.VMEM(clip_t.shape, BF16),
-            pltpu.VMEM(clip_t.shape, BF16),
-            jax.ShapeDtypeStruct((cams, nr, width), BF16),
-            jax.ShapeDtypeStruct((cams, nr, width), BF16),
-            pltpu.VMEM((cams, picks * blk, width), BF16),
-            pltpu.VMEM((cams, picks * blk, width), F32),
-            pltpu.VMEM((cams, pairs, keys, 2 * blk), BF16),
-            pltpu.VMEM((cams, HEADS, blk), F32),
-            pltpu.VMEM((cams, blk, 128), F32),
-        )
+        pltpu.VMEM(clip_t.shape, BF16),
+        pltpu.VMEM(clip_t.shape, BF16),
+        jax.ShapeDtypeStruct((cams, nr, width), BF16),
+        jax.ShapeDtypeStruct((cams, nr, width), BF16),
+        pltpu.VMEM((cams, picks * blk, width), BF16),
+        pltpu.VMEM((cams, picks * blk, width), F32),
+        pltpu.VMEM((cams, pairs, keys, 2 * blk), BF16),
+        pltpu.VMEM((cams, HEADS, blk), F32),
+        pltpu.VMEM((cams, blk, 128), F32),
+        pltpu.VMEM((cams, blk, width), BF16),
+    )
+    weights = (wk, wvt, wo, gain)
     return pl.pallas_call(
         functools.partial(attend_kernel, head, picks),
         name="attend",
@@ -265,45 +264,36 @@
         grid_spec=pltpu.PrefetchScalarGridSpec(
             num_scalar_prefetch=3,
             grid=(cams,),
-            in_specs=[whole(x.shape) for x in args],
+            in_specs=[whole(arrived.shape), per_camera(q), per_camera(k), per_camera(vt), slab]
+            + [whole(x.shape) for x in weights],
             out_specs=[whole(x.shape) for x in outs],
             scratch_shapes=[
                 pltpu.VMEM((keys, width), BF16),
                 pltpu.VMEM((pairs, 128 + PAD, keys), BF16),
             ],
         ),
-        compiler_params=params(6 + 2 * picks),
-    )(own, lists, counts, *args)
-
-
-def far_values_kernel(picks, own_s, lists_s, arrived_ref, w_ref, out_ref):
-    cams = lists_s.shape[0]
-    blk = arrived_ref.shape[1]
-    for c in range(cams):
-        rows = jnp.concatenate([arrived_ref[lists_s[c, own_s[0], s]] for s in range(picks)], axis=0)
-        out_ref[c] = mm(rows, w_ref[...]).astype(BF16)
-
-
-def far_values(own, lists, arrived, w):
-    _, blk, width = arrived.shape
-    cams, _, picks = lists.shape
+        compiler_params=params(10 + picks),
+    )(own, lists, counts, arrived, hbm(q), hbm(k), hbm(vt), hbm(clip_t), *weights)
+
+
+def far_values_kernel(arrived_ref, w_ref, out_ref):
+    out_ref[...] = mm(arrived_ref[...], w_ref[...]).astype(BF16)
+
+
+def far_values(arrived, w):
+    total, width = arrived.shape
     return pl.pallas_call(
-        functools.partial(far_values_kernel, picks),
+        far_values_kernel,
         name="far_values",
-        out_shape=pltpu.VMEM((cams, picks * blk, width), BF16),
-        grid_spec=pltpu.PrefetchScalarGridSpec(
-            num_scalar_prefetch=2,
-            grid=(1,),
-            in_specs=[whole(arrived.shape), whole(w.shape)],
-            out_specs=whole((cams, picks * blk, width)),
-        ),
-        compiler_params=params(4 + 2 * picks),
+        out_shape=pltpu.VMEM((total, width), BF16),
+        grid=(total // 512,),
+        in_specs=[pl.BlockSpec((512, width), lambda i: (i, 0)), whole(w.shape)],
+        out_specs=pl.BlockSpec((512, width), lambda i: (i, 0)),
+        compiler_params=params(6),
         cost_estimate=pl.CostEstimate(
-            flops=2 * cams * picks * blk * width * width,
-            bytes_accessed=4 * cams * picks * blk * width,
-            transcendentals=0,
-        ),
-    )(own, lists, arrived, w)
+            flops=2 * total * width * width, bytes_accessed=4 * total * width, transcendentals=0
+        ),
+    )(arrived, w)
 
 
 def fill_windows(own_s, act_ref, near_ref, farther_ref, x_ref, edge, total):
@@ -477,59 +467,76 @@
     return r * (grad - hat * head_mean(grad * hat, ones, head))
 
 
-def pair_grads(p, head, q_ref, v_ref, vf_ref, e_ref, dm_ref, row_ref, col_ref, low):
-    blk = q_ref.shape[1]
+def drift_rows(head, dm, mixed, row):
+    width = dm.shape[1]
+    lanes = lax.broadcasted_iota(jnp.int32, (PAD, width), 1) // head
+    picked = (lanes == lax.broadcasted_iota(jnp.int32, (PAD, width), 0)).astype(BF16)
+    product = (dm.astype(F32) * mixed.astype(F32)).astype(BF16)
+    return mm_t(picked, product)[:HEADS] * row
+
+
+def pair_queries(p, q, dm, col, drift, low):
     cols = slice(128 * p, 128 * (p + 1))
-    row = jnp.concatenate([row_ref[0, 2 * p : 2 * p + 1], row_ref[0, 2 * p + 1 : 2 * p + 2]], axis=1)
-    col = jnp.where(low, col_ref[0, :, 2 * p : 2 * p + 1], col_ref[0, :, 2 * p + 1 : 2 * p + 2])
-    dm = dm_ref[:, 0, :, cols].reshape(blk, 128).astype(F32)
-    q2 = pair_rows(q_ref[0, :, cols], low)
-    dm2 = pair_rows((dm * col).astype(BF16), low)
-    e = e_ref[0, p].astype(F32)
-    slope = jnp.concatenate([mm_t(v_ref[0, :, cols], dm2), mm_t(vf_ref[0, :, cols], dm2)], axis=0)
-    drift = jnp.sum(e * slope, axis=0, keepdims=True) * row
-    return q2, dm2, (e * (slope - drift)).astype(BF16)
-
-
-def far_grads_kernel(head, picks, own_s, lists_s, counts_s, q_ref, v_ref, vf_ref, e_ref, dm_ref,
+    spread = jnp.where(low, col[:, 2 * p : 2 * p + 1], col[:, 2 * p + 1 : 2 * p + 2])
+    q2 = pair_rows(q[:, cols], low)
+    dm2 = pair_rows((dm[:, cols].astype(F32) * spread).astype(BF16), low)
+    shift = jnp.concatenate([drift[2 * p : 2 * p + 1], drift[2 * p + 1 : 2 * p + 2]], axis=1)
+    return q2, dm2, shift
+
+
+def far_grads_kernel(head, picks, own_s, lists_s, counts_s, q_ref, vf_ref, e_ref, dm_ref, mixed_ref,
                      row_ref, col_ref, kf_ref, rf_ref, wk_ref, wv_ref, send_ref, kgrad, vgrad, shares, sems):
     c = pl.program_id(0)
-    q_ref, v_ref, vf_ref, e_ref, row_ref, col_ref, kf_ref, rf_ref = (
-        camera(r, c) for r in (q_ref, v_ref, vf_ref, e_ref, row_ref, col_ref, kf_ref, rf_ref)
-    )
-    dm_ref = camera_slabs(dm_ref, c)
     own = own_s[0]
-    blk, width = q_ref.shape[1:]
+    cams, blk, width = mixed_ref.shape
     low = lax.broadcasted_iota(jnp.int32, (blk, 128), 1) < head
-    ones_h = head_ones(width // 2, head)
+    q = q_ref[0]
+    dm = dm_ref[:, c].reshape(blk, width)
+    drift = drift_rows(head, dm, mixed_ref[c], row_ref[c])
+    col = col_ref[c]
     for p in range(width // 128):
         cols = slice(128 * p, 128 * (p + 1))
-        q2, dm2, d_scaled = pair_grads(
-            p, head, q_ref, v_ref, vf_ref, e_ref, dm_ref, row_ref, col_ref, low
-        )
-        kgrad[:, cols] = mm(d_scaled[blk:], q2)
-        vgrad[:, cols] = mm(e_ref[0, p, blk:], dm2).astype(BF16)
-    far_k = head_norm_back(kgrad[...], kf_ref[0], rf_ref[0], ones_h, head).astype(BF16)
-    share = mm_t(far_k, wk_ref[...]) + mm_t(vgrad[...], wv_ref[...])
-    share = share.astype(BF16)
-    for s in range(picks):
-        shares[c, s] = share[s * blk : (s + 1) * blk]
-        pltpu.make_async_copy(
-            shares.at[c, s], send_ref.at[lists_s[c, own, s]], sems.at[c, s]
-        ).start()
-
-    @pl.when(c == pl.num_programs(0) - 1)
+        q2, dm2, shift = pair_queries(p, q, dm, col, drift, low)
+        far_v = jnp.concatenate([vf_ref[lists_s[c, own, s], :, cols] for s in range(picks)], axis=0)
+        e = e_ref[c, p, blk:]
+        d_scaled = (e.astype(F32) * (mm_t(far_v, dm2) - shift)).astype(BF16)
+        kgrad[c, :, cols] = mm(d_scaled, q2)
+        vgrad[c, :, cols] = mm(e, dm2).astype(BF16)
+
+    @pl.when(c == cams - 1)
     def _():
-        for i in range(shares.shape[0]):
+        ones_h = head_ones(width // 2, head)
+
+        def back(i, carry):
+            grad = head_norm_back(kgrad[i], kf_ref[i], rf_ref[i], ones_h, head)
+            shares[i] = grad.astype(BF16)
+            return carry
+
+        lax.fori_loop(0, cams, back, 0)
+        shape = (picks * blk, width)
+        for first, last in ((0, (cams + 1) // 2), ((cams + 1) // 2, cams)):
+            count = last - first
+            share = mm_t(shares[first:last].reshape(count * shape[0], width), wk_ref[...])
+            share = share + mm_t(vgrad[first:last].reshape(count * shape[0], width), wv_ref[...])
+            shares[first:last] = share.astype(BF16).reshape((count,) + shape)
+            for i in range(first, last):
+                for s in range(picks):
+                    pltpu.make_async_copy(
+                        shares.at[i, pl.ds(s * blk, blk)],
+                        send_ref.at[lists_s[i, own, s]],
+                        sems.at[i, s],
+                    ).start()
+        for i in range(cams):
             for s in range(picks):
-                pltpu.make_async_copy(shares.at[i, s], send_ref.at[0], sems.at[i, s]).wait()
-
-
-def far_grads(own, lists, counts, n_cols, q, v, vf, e, dm_t, row, col, kf, rf, wk, wv, head):
-    tw, cams, nr, width = dm_t.shape
-    blk = tw * nr
+                pltpu.make_async_copy(
+                    shares.at[i, pl.ds(s * blk, blk)], send_ref.at[0], sems.at[i, s]
+                ).wait()
+
+
+def far_grads(own, lists, counts, n_cols, q, vf, e, dm_t, mixed, row, col, kf, rf, wk, wv, head):
+    cams, blk, width = mixed.shape
     picks = lists.shape[2]
-    args = (q, v, vf, e, dm_t, row, col, kf, rf, wk, wv)
+    args = (vf, e, dm_t, mixed, row, col, kf, rf, wk, wv)
     return pl.pallas_call(
         functools.partial(far_grads_kernel, head, picks),
         name="far_grads",
@@ -537,118 +544,119 @@
         grid_spec=pltpu.PrefetchScalarGridSpec(
             num_scalar_prefetch=3,
             grid=(cams,),
-            in_specs=[whole(x.shape) for x in args],
+            in_specs=[per_camera(q)] + [whole(x.shape) for x in args],
             out_specs=pl.BlockSpec(memory_space=pltpu.HBM),
             scratch_shapes=[
-                pltpu.VMEM((picks * blk, width), F32),
-                pltpu.VMEM((picks * blk, width), BF16),
-                pltpu.VMEM((cams, picks, blk, width), BF16),
+                pltpu.VMEM((cams, picks * blk, width), F32),
+                pltpu.VMEM((cams, picks * blk, width), BF16),
+                pltpu.VMEM((cams, picks * blk, width), BF16),
                 pltpu.SemaphoreType.DMA((cams, picks)),
             ],
         ),
-        compiler_params=params(6 + 5 * picks),
-    )(own, lists, counts, *args)
-
-
-def own_grads_kernel(head, q_ref, v_ref, vf_ref, e_ref, dm_ref, row_ref, col_ref, k_ref, kf_ref,
-                     rq_ref, rk_ref, wq_ref, wk_ref, wv_ref, out_ref):
+        compiler_params=params(4 + 6 * picks),
+    )(own, lists, counts, hbm(q), *args)
+
+
+def own_grads_kernel(head, picks, own_s, lists_s, q_ref, k_ref, v_ref, rq_ref, rk_ref, vf_ref, e_ref, dm_ref,
+                     mixed_ref, row_ref, col_ref, kf_ref, wq_ref, wk_ref, wv_ref, out_ref):
     c = pl.program_id(0)
-    q_ref, v_ref, vf_ref, e_ref, row_ref, col_ref, k_ref, kf_ref, rq_ref, rk_ref, out_ref = (
-        camera(r, c)
-        for r in (q_ref, v_ref, vf_ref, e_ref, row_ref, col_ref, k_ref, kf_ref, rq_ref, rk_ref, out_ref)
-    )
-    dm_ref = camera_slabs(dm_ref, c)
-    blk, width = q_ref.shape[1:]
+    own = own_s[0]
+    cams, blk, width = mixed_ref.shape
     low = lax.broadcasted_iota(jnp.int32, (blk, 128), 1) < head
     ones_h = head_ones(width // 2, head)
     scale = head ** (-0.5)
+    q = q_ref[0]
+    dm = dm_ref[:, c].reshape(blk, width)
+    drift = drift_rows(head, dm, mixed_ref[c], row_ref[c])
+    col = col_ref[c]
+    listed = [lists_s[c, own, s] for s in range(picks)]
     dq, dk, dv = [], [], []
     for p in range(width // 128):
         cols = slice(128 * p, 128 * (p + 1))
-        q2, dm2, d_scaled = pair_grads(
-            p, head, q_ref, v_ref, vf_ref, e_ref, dm_ref, row_ref, col_ref, low
-        )
+        q2, dm2, shift = pair_queries(p, q, dm, col, drift, low)
+        all_v = jnp.concatenate([v_ref[0, :, cols]] + [vf_ref[i, :, cols] for i in listed], axis=0)
+        all_k = jnp.concatenate([k_ref[0, :, cols], kf_ref[c, :, cols]], axis=0)
+        e = e_ref[c, p]
+        d_scaled = (e.astype(F32) * (mm_t(all_v, dm2) - shift)).astype(BF16)
         dk.append(mm(d_scaled[:blk], q2))
-        dv.append(mm(e_ref[0, p, :blk], dm2).astype(BF16))
-        flipped = jnp.transpose(d_scaled)
-        both = mm(flipped[:, :blk], k_ref[0, :, cols]) + mm(flipped[:, blk:], kf_ref[0, :, cols])
+        dv.append(mm(e[:blk], dm2).astype(BF16))
+        both = mm(jnp.transpose(d_scaled), all_k)
         dq.append(jnp.where(low, both[:blk], both[blk:]) * scale)
     dq, dk, dv = (jnp.concatenate(parts, axis=1) for parts in (dq, dk, dv))
-    q_hat = q_ref[0].astype(F32) * (1.0 / scale)
+    q_hat = q.astype(F32) * (1.0 / scale)
     dq = head_norm_back(dq, q_hat, rq_ref[0], ones_h, head).astype(BF16)
     dk = head_norm_back(dk, k_ref[0], rk_ref[0], ones_h, head).astype(BF16)
     out_ref[0] = mm_t(dq, wq_ref[...]) + mm_t(dk, wk_ref[...]) + mm_t(dv, wv_ref[...])
 
 
-def own_grads(q, v, vf, e, dm_t, row, col, k, kf, rq, rk, wq, wk, wv, head):
-    tw, cams, nr, width = dm_t.shape
-    blk = tw * nr
-    args = (q, v, vf, e, dm_t, row, col, k, kf, rq, rk, wq, wk, wv)
+def own_grads(own, lists, q, k, v, rq, rk, vf, e, dm_t, mixed, row, col, kf, wq, wk, wv, head):
+    cams, blk, width = mixed.shape
+    picks = lists.shape[2]
+    windows = (q, k, v, rq, rk)
+    args = (vf, e, dm_t, mixed, row, col, kf, wq, wk, wv)
     return pl.pallas_call(
-        functools.partial(own_grads_kernel, head),
+        functools.partial(own_grads_kernel, head, picks),
         name="own_grads",
-        out_shape=pltpu.VMEM((cams, blk, width), F32),
+        out_shape=pltpu.HBM((cams, blk, width), F32),
         grid_spec=pltpu.PrefetchScalarGridSpec(
-            num_scalar_prefetch=0,
+            num_scalar_prefetch=2,
             grid=(cams,),
-            in_specs=[whole(x.shape) for x in args],
-            out_specs=whole((cams, blk, width)),
-        ),
-        compiler_params=params(12 + e.shape[2] * 8 // 256),
+            in_specs=[per_camera(x) for x in windows] + [whole(x.shape) for x in args],
+            out_specs=per_camera(mixed),
+        ),
+        compiler_params=params(6 + picks),
         cost_estimate=pl.CostEstimate(
             flops=20 * cams * blk * width * width, bytes_accessed=4 * e.size, transcendentals=0
         ),
-    )(*args)
-
-
-def final_kernel(own_s, match_s, lists_s, counts_s, back_ref, rows_ref, clip_ref, dl_ref, gain_ref, out_ref, acc):
-    cams, n_cols, picks = lists_s.shape
-    own = own_s[0]
-    me = pl.program_id(0)
-    rows_ref = camera(rows_ref, me)
-    clip_ref, dl_ref, out_ref = (camera_slabs(r, me) for r in (clip_ref, dl_ref, out_ref))
-    tw, _, nr, width = clip_ref.shape
+    )(own, lists, *map(hbm, windows), *args)
+
+
+def final_kernel(table_s, back_ref, rows_ref, clip_ref, dl_ref, gain_ref, out_ref, acc):
+    tw, cams, nr, width = clip_ref.shape
     blk = tw * nr
-    source = jnp.int32(0)
-    for c in range(cams):
-        source = jnp.where(match_s[c] == me, c, source)
-    acc[...] = rows_ref[0]
-    for i in range(n_cols):
-        hit = jnp.bool_(False)
-        for s in range(picks):
-            hit = hit | ((lists_s[source, i, s] == own) & (s < counts_s[source, i]))
-
-        @pl.when(hit)
+    acc[...] = rows_ref[...]
+
+    def add(i, carry):
+        cam = table_s[i]
+
+        @pl.when(cam >= 0)
         def _():
-            acc[...] += back_ref[i].astype(F32)
-
-    x = clip_ref[:, 0].reshape(blk, width).astype(F32)
-    r = rms(x)
-    hat = x * r
-    g = acc[...] * gain_ref[...]
-    d = dl_ref[:, 0].reshape(blk, width) + r * (
-        g - hat * jnp.mean(g * hat, axis=-1, keepdims=True)
-    )
-    out_ref[:, 0] = d.astype(BF16).reshape(tw, nr, width)
-
-
-def final(own, matching, lists, counts, back, rows, clip_t, d_lifted, gain):
-    tw, cams, nr, width = clip_t.shape
-    blk = tw * nr
-    slab = pl.BlockSpec((tw, 1, nr, width), lambda c, *_: (0, c, 0, 0))
+            acc[cam] += back_ref[i].astype(F32)
+
+        return carry
+
+    lax.fori_loop(0, back_ref.shape[0], add, 0)
+    gain = gain_ref[...]
+
+    def one(c, carry):
+        x = clip_ref[:, c].reshape(blk, width).astype(F32)
+        r = rms(x)
+        hat = x * r
+        g = acc[c] * gain
+        d = dl_ref[:, c].reshape(blk, width) + r * (
+            g - hat * jnp.mean(g * hat, axis=-1, keepdims=True)
+        )
+        out_ref[:, c] = d.astype(BF16).reshape(tw, nr, width)
+        return carry
+
+    lax.fori_loop(0, cams, one, 0)
+
+
+def final(table, back, rows, clip_t, d_lifted, gain):
+    args = (back, rows, clip_t, d_lifted, gain)
     return pl.pallas_call(
         final_kernel,
         name="final",
         out_shape=jax.ShapeDtypeStruct(clip_t.shape, BF16),
         grid_spec=pltpu.PrefetchScalarGridSpec(
-            num_scalar_prefetch=4,
-            grid=(cams,),
-            in_specs=[whole(a.shape) for a in (back, rows, clip_t, d_lifted, gain)],
+            num_scalar_prefetch=1,
+            grid=(1,),
+            in_specs=[whole(x.shape) for x in args],
             out_specs=whole(clip_t.shape),
-            scratch_shapes=[pltpu.VMEM((blk, width), F32)],
+            scratch_shapes=[pltpu.VMEM(rows.shape, F32)],
         ),
         compiler_params=params(8),
-    )(own, matching, lists, counts, back, rows, clip_t, d_lifted, gain)
+    )(table, *args)
 
 
 def exchange_edges(near, farther):
@@ -695,15 +703,17 @@
     cot_far = lax.dynamic_index_in_dim(cot_t, tw - 1 - last, 0, keepdims=False).reshape(-1, width)
 
     rows, send = prep(n_cols, own, matching, block_lists, counts, clip_t, gain_attn)
+    cot_near, cot_far = exchange_edges(cot_near, cot_far)
     arrived = lax.all_to_all(send, "cols", split_axis=0, concat_axis=0, tiled=True)
+    rows, w_value, lists, live = lax.optimization_barrier((rows, w_value, block_lists, counts))
     w_value_t = w_value.T
+    slots = jnp.arange(lists.shape[2], dtype=jnp.int32)
+    asks = (lists == own_index) & (slots[None, None, :] < live[:, :, None])
+    table = jnp.sum(jnp.where(asks, matching[:, None, None] + 1, 0), axis=(0, 2)) - 1
     q, k, v, vt, rq, rk = project(rows.reshape(flat), w_query, w_key, w_value, w_value_t, head, blk)
     q, k, v, rq, rk = (a.reshape(views, blk, width) for a in (q, k, v, rq, rk))
-    arrived, q, k, v, vt, rq, rk, cot_t, cot_near, cot_far = lax.optimization_barrier(
-        (arrived, q, k, v, vt, rq, rk, cot_t, cot_near, cot_far)
-    )
-    cot_near, cot_far = exchange_edges(cot_near, cot_far)
-    lifted, act_one, near, farther, kf, rf, e, row, col = attend(
+    arrived, q, k, v, vt, rq, rk = lax.optimization_barrier((arrived, q, k, v, vt, rq, rk))
+    lifted, act_one, near, farther, kf, rf, e, row, col, mixed = attend(
         own, block_lists, counts, arrived, q, k, vt, clip_t, w_key, w_value_t, w_out, gain_first, head
     )
     edge = (views * nr, width)
@@ -720,8 +730,9 @@
         (flat_bf, edge_bf, edge_bf, flat_bf, edge_bf, edge_bf), nr, False,
     )
     d_near, d_far = exchange_edges(d_near, d_far)
-    vf = far_values(own, block_lists, arrived, w_value)
+    vf = far_values(arrived.reshape(-1, width), w_value)
     d_near, d_far, vf = lax.optimization_barrier((d_near, d_far, vf))
+    vf = vf.reshape(arrived.shape)
     d_lifted, d_mixed = conv_call(
         "grad_one", grad_one_body, own, d_conv, d_near, d_far, conv_first,
         (lifted.reshape(flat), cot_t.reshape(flat), gain_first, w_out),
@@ -731,7 +742,7 @@
     d_mixed = d_mixed.reshape(slabs)
     act_near, act_far = exchange_edges(act_near, act_far)
     send_back = far_grads(
-        own, block_lists, counts, n_cols, q, v, vf, e, d_mixed, row, col, kf, rf, w_key, w_value, head
+        own, block_lists, counts, n_cols, q, vf, e, d_mixed, mixed, row, col, kf, rf, w_key, w_value, head
     )
     send_back, act_near, act_far = lax.optimization_barrier((send_back, act_near, act_far))
     back = lax.all_to_all(send_back, "cols", split_axis=0, concat_axis=0, tiled=True)
@@ -740,9 +751,9 @@
         (lifted.reshape(flat),), (jax.ShapeDtypeStruct(flat, BF16),), nr, False,
     )
     d_rows = own_grads(
-        q, v, vf, e, d_mixed, row, col, k, kf, rq, rk, w_query, w_key, w_value, head
-    )
-    d_clip = final(own, matching, block_lists, counts, back, d_rows, clip_t, d_lifted.reshape(slabs), gain_attn)
+        own, block_lists, q, k, v, rq, rk, vf, e, d_mixed, mixed, row, col, kf, w_query, w_key, w_value, head
+    )
+    d_clip = final(table, back, d_rows, clip_t, d_lifted.reshape(slabs), gain_attn)
     return (
         jnp.transpose(result.reshape(slabs), (1, 2, 0, 3)),
         jnp.transpose(d_clip, (1, 2, 0, 3)),

time: 208 us -> 200 us (0.962)
  local copies, waits for them, and re-layouts: 53.1 us -> 37.8 us
  waiting for transfers between devices: 36 us -> 42.1 us
    unnamed x138 -> x97, local copies, waits for them, and re-layouts: 47.5 us -> 30.3 us
    all_to_all x1, waiting for transfers between devices: 5.5 us -> 11.4 us  [local(): lax.all_to_all(send_back, 'cols', split_axis=0, concat_axis=0, tiled=True)]
    pallas_call x1, Pallas kernels: 3.5 us -> 6.01 us  [project(): pl.pallas_call(functools.partial(project_kernel, head, blk), name='projec...]
    transpose x0 -> x1, local copies, waits for them, and re-layouts: none -> 2.31 us  [local(): cot_t = jnp.transpose(cotangent, (2, 0, 1, 3))]
    pallas_call x1, Pallas kernels: 6.38 us -> 4.29 us  [final(): pl.pallas_call(final_kernel, name='final', out_shape=jax.ShapeDtypeStruct...]
  transfers between devices with their start and end apart: 10 -> 10, of which waited for: 3 -> 3; matrix products, arithmetic and copies ran while one was open for 4% -> 5% of each run, Pallas kernels for 31% -> 34%
where the time goes in v3:
time: 200 us; the launch traced here: 199 us
  Pallas kernels  91.3 us (46%)
  waiting for transfers between devices  42.1 us (21%)
  local copies, waits for them, and re-layouts  37.8 us (19%)
  starting transfers between devices  26.6 us (13%)
    unnamed x97, local copies, waits for them, and re-layouts  30.3 us
    pallas_call x4, Pallas kernels, conv_call(): pl.pallas_call(functools.partial(conv_kernel, body, len(extra), transpose...  27.5 us
    all_to_all x1, waiting for transfers between devices, local(): lax.all_to_all(send, 'cols', split_axis=0, concat_axis=0, tiled=True)  27.3 us
    pallas_call x1, Pallas kernels, own_grads(): pl.pallas_call(functools.partial(own_grads_kernel, head, picks), name='ow...  18 us
    pallas_call x1, Pallas kernels, attend(): pl.pallas_call(functools.partial(attend_kernel, head, picks), name='atten...  16 us
    pallas_call x1, Pallas kernels, far_grads(): pl.pallas_call(functools.partial(far_grads_kernel, head, picks), name='fa...  14.4 us
    ppermute x4, starting transfers between devices, exchange_edges(): lax.ppermute(farther, 'cols', outer)  13 us
    all_to_all x1, waiting for transfers between devices, local(): lax.all_to_all(send_back, 'cols', split_axis=0, concat_axis=0, tiled=True)  11.4 us
  transfers between devices with their start and end apart: 10, of which 3 were waited for; matrix products, arithmetic and copies ran while one was open for 5% of the time, Pallas kernels for 34%

profile of v3, /device:TPU:13, one launch (start us, length us, event | category | flops | bytes accessed | tf_op | source)
XLA Modules:
  0.0 199.1 jit_solution(7803436161956738069)
XLA Ops:
  0.6 0.8 copy.28.lists_s
  1.4 1.4 copy.41
  2.8 0.7 copy-done.25
  4.9 3.4 %prep.1 = (bf16[7,128,512]{2,1,0:T(8,128)(2,1)S(1)}, bf16[16,128,512]{2,1,0:T(8,128)(2,1)}) custom-call(s32[1]{0:T(128)} %bitcast.own_s, s32[7]{0:T(128)S(1)} %copy-done.30, s32[7,16,2]{2,1,0:T(8,128)S(1)} %copy.28.lists_s, s32[7,16]{1,0:T(8,128)S(1)} %copy-done.25, bf16[4,7,32,512]{3,2,1,0:T(8,128)(2,1)S(1)} %bitcast.34, f32[1,512]{1,0:T(1,128)S(1)} %bitcast.46), custom_call_target="tpu_custom_call" | custom-call | tf_op jit(solution)/shard_map/prep/pallas_call | solution.py:98
  8.3 0.9 copy-done.36
  9.3 6.6 %all-to-all-start = ((bf16[16,128,512]{2,1,0:T(8,128)(2,1)}), bf16[16,128,512]{2,1,0:T(8,128)(2,1)S(1)}, u32[]{:S(2)}, u32[]{:S(2)}) async-start(bf16[16,128,512]{2,1,0:T(8,128)(2,1)} %get-tuple-element.48), calls=%async_computation | async-start | bytes 4194304 | tf_op jit(solution)/shard_map/all_to_all | solution.py:707
  15.8 2.6 %constant_dynamic-slice_fusion = (bf16[7,32,1,512]{3,2,1,0:T(2,128)(2,1)S(1)}, bf16[7,32,1,512]{3,2,1,0:T(2,128)(2,1)S(1)}) fusion(bf16[7,32,4,512]{3,2,1,0:T(4,128)(2,1)} %param.15, s32[]{:T(128)S(6)} %select_n.20, s32[]{:T(128)S(6)} %select_n.19), kind=kLoop, calls=%fused_computation.4 | loop fusion | bytes 917512 | tf_op jit(solution)/shard_map/dynamic-slice.1
  18.4 0.7 copy.36
  19.5 0.7 copy.37
  20.2 3.1 %collective-permute-start.3 = (bf16[224,512]{1,0:T(8,128)(2,1)}, bf16[224,512]{1,0:T(8,128)(2,1)}, u32[]{:S(2)}, u32[]{:S(2)}) collective-permute-start(bf16[224,512]{1,0:T(8,128)(2,1)} %bitcast.17), channel_id=1, source_target_pairs={{1,2},{2,1},{3,4},{4,3},{5,6},{6,5},{7,8},{8,7},{9,10},{10,9},{11,... | collective-permute-start | bytes 688136 | tf_op jit(solution)/shard_map/ppermute | solution.py:666
  23.4 1.0 copy.27
  24.4 2.3 %copy.29 = bf16[4,7,32,512]{3,2,1,0:T(8,128)(2,1)} copy(bf16[4,7,32,512]{3,0,2,1:T(4,128)(2,1)} %bitcast.62) | data formatting | bytes 1835008 | tf_op jit(solution)/shard_map/transpose | solution.py:699
  26.7 1.0 copy-done.15
  27.7 1.0 copy-done.23
  28.8 1.2 copy-done.37
  29.9 6.0 %project.1 = (bf16[896,512]{1,0:T(8,128)(2,1)}, bf16[896,512]{1,0:T(8,128)(2,1)}, bf16[896,512]{1,0:T(8,128)(2,1)}, bf16[7,512,128]{2,1,0:T(8,128)(2,1)}, f32[896,512]{1,0:T(8,128)}, /*index=5*/f32[896,512]{1,0:T(8,128)}) custom-call(bf16[896,512]{1,0:T(8,128)(2,1)S(1)} %bitcast.54, bf16[512,512]{1,0:T(8,128)(2,1)S(1)} %copy-done.23, ...), custom_call_target="tpu_custom_call" | custom-call | flops 1879048192 | bytes 9175040 | tf_op jit(solution)/shard_map/project/pallas_call | solution.py:139
  36.0 27.3 %all-to-all-done.refs_0_ = bf16[16,128,512]{2,1,0:T(8,128)(2,1)S(1)} async-done(((bf16[16,128,512]{2,1,0:T(8,128)(2,1)}), bf16[16,128,512]{2,1,0:T(8,128)(2,1)S(1)}, u32[]{:S(2)}, u32[]{:S(2)}) %all-to-all-start) | async-done | bytes 2097184 | tf_op jit(solution)/shard_map/all_to_all | solution.py:707
  63.3 1.4 copy-done.16
  64.7 1.0 copy-done.22
  65.7 16.0 %attend.1 = (bf16[4,7,32,512]{3,2,1,0:T(8,128)(2,1)S(1)}, bf16[4,7,32,512]{3,2,1,0:T(8,128)(2,1)S(1)}, bf16[7,32,512]{2,1,0:T(8,128)(2,1)S(1)}, bf16[7,32,512]{2...) custom-call(s32[1]{0:T(128)} %bitcast.own_s, ...), custom_call_target="tpu_custom_call" | custom-call | tf_op jit(solution)/shard_map/attend/pallas_call | solution.py:260
  82.1 3.8 %collective-permute-start.1 = (bf16[224,512]{1,0:T(8,128)(2,1)S(1)}, bf16[224,512]{1,0:T(8,128)(2,1)S(1)}, u32[]{:S(2)}, u32[]{:S(2)}) collective-permute-start(bf16[224,512]{1,0:T(8,128)(2,1)S(1)} %bitcast.56), channel_id=1, source_target_pairs={{1,2},{2,1},{3,4},{4,3},{5,6},{6,5},{7,8},{8,7},{9,10},{10,9},{11,... | collective-permute-start | bytes 688136 | tf_op jit(solution)/shard_map/ppermute | solution.py:666
  86.0 2.3 %copy-done.32 = bf16[3,3,512,512]{3,2,1,0:T(8,128)(2,1)S(1)} copy-done((bf16[3,3,512,512]{3,2,1,0:T(8,128)(2,1)S(1)}, bf16[3,3,512,512]{3,2,1,0:T(8,128)(2,1)}, u32[]{:S(2)}) %copy-start.32) | copy-done | bytes 4718616
  88.3 6.5 %grad_two.1.refs_0_ = f32[896,512]{1,0:T(8,128)S(1)} custom-call(s32[1]{0:T(128)} %bitcast.own_s, bf16[896,512]{1,0:T(8,128)(2,1)S(1)} %bitcast.43, bf16[224,512]{1,0:T(8,128)(2,1)S(1)} %collective-permute-done.2.near_ref, bf16[224,512]{1,0:T(8,128)(2,1)} %collective-permute-done.3.farther_ref, bf16[3,3,512,512]{3,2,1,0:T(8,128)(2,1)S(1)} %copy-done.32), custom_call_target="tpu_custom_call" | custom-call | flops 4227858432 | bytes 4718592 | tf_op jit(solution)/shard_map/grad_two/pallas_call | solution.py:358
  94.9 7.3 %conv_one.1 = (bf16[896,512]{1,0:T(8,128)(2,1)S(1)}, bf16[224,512]{1,0:T(8,128)(2,1)S(1)}, bf16[224,512]{1,0:T(8,128)(2,1)S(1)}, bf16[896,512]{1,0:T(8,128)(2,1)...) custom-call(s32[1]{0:T(128)} %bitcast.own_s, bf16[896,512]{1,0:T(8,128)(2,1)S(1)} %bitcast.55, ...), custom_call_target="tpu_custom_call" | custom-call | flops 4227858432 | bytes 4718592 | tf_op jit(solution)/shard_map/conv_one/pallas_call | solution.py:358
  102.2 0.9 copy-done.41
  103.2 3.1 %collective-permute-start.5 = (bf16[224,512]{1,0:T(8,128)(2,1)S(1)}, bf16[224,512]{1,0:T(8,128)(2,1)S(1)}, u32[]{:S(2)}, u32[]{:S(2)}) collective-permute-start(bf16[224,512]{1,0:T(8,128)(2,1)S(1)} %get-tuple-element.67), channel_id=1, source_target_pairs={{1,2},{2,1},{3,4},{4,3},{5,6},{6,5},{7,8},{8,7},{9,10},{10,9},{11,... | collective-permute-start | bytes 688136 | tf_op jit(solution)/shard_map/ppermute | solution.py:666
  106.3 1.8 far_values.1
  108.1 3.4 %collective-permute-done.5.farther_ref = bf16[224,512]{1,0:T(8,128)(2,1)S(1)} collective-permute-done((bf16[224,512]{1,0:T(8,128)(2,1)S(1)}, bf16[224,512]{1,0:T(8,128)(2,1)S(1)}, u32[]{:S(2)}, u32[]{:S(2)}) %collective-permute-start.5) | collective-permute-done | bytes 229408 | tf_op jit(solution)/shard_map/ppermute | solution.py:666
  111.5 8.1 %grad_one.1 = (f32[896,512]{1,0:T(8,128)S(1)}, bf16[896,512]{1,0:T(8,128)(2,1)S(1)}) custom-call(s32[1]{0:T(128)} %bitcast.own_s, bf16[896,512]{1,0:T(8,128)(2,1)S(1)} %get-tuple-element.70.act_ref, bf16[224,512]{1,0:T(8,128)(2,1)S(1)} %collective-permute-done.4.near_ref, bf16[224,512]{1,0:T(8,128)(2,1)S(1)} %collective-permute-done.5.farther_ref, ...), custom_call_target="tpu_custom_call" | custom-call | flops 4227858432 | bytes 4718592 | tf_op jit(solution)/shard_map/grad_one/pallas_call | solution.py:358
  119.6 2.0 %collective-permute-start.6 = (bf16[224,512]{1,0:T(8,128)(2,1)S(1)}, bf16[224,512]{1,0:T(8,128)(2,1)S(1)}, u32[]{:S(2)}, u32[]{:S(2)}) collective-permute-start(bf16[224,512]{1,0:T(8,128)(2,1)S(1)} %get-tuple-element.83), channel_id=1, source_target_pairs={{0,1},{1,0},{2,3},{3,2},{4,5},{5,4},{6,7},{7,6},{8,9},{9,8},{10,11... | collective-permute-start | bytes 688136 | tf_op jit(solution)/shard_map/ppermute | solution.py:666
  121.6 2.9 %collective-permute-start.7 = (bf16[224,512]{1,0:T(8,128)(2,1)S(1)}, bf16[224,512]{1,0:T(8,128)(2,1)S(1)}, u32[]{:S(2)}, u32[]{:S(2)}) collective-permute-start(bf16[224,512]{1,0:T(8,128)(2,1)S(1)} %get-tuple-element.84), channel_id=1, source_target_pairs={{1,2},{2,1},{3,4},{4,3},{5,6},{6,5},{7,8},{8,7},{9,10},{10,9},{11,... | collective-permute-start | bytes 688136 | tf_op jit(solution)/shard_map/ppermute | solution.py:666
  124.6 14.4 %far_grads.1 = bf16[16,128,512]{2,1,0:T(8,128)(2,1)} custom-call(s32[1]{0:T(128)} %bitcast.own_s, s32[7,16,2]{2,1,0:T(8,128)S(1)} %copy.28.lists_s, s32[7,16]{1,0:T(8,128)S(1)} %copy-done.26, bf16[7,128,512]{2,1,0:T(8,128)(2,1)} %bitcast.60, bf16[16,128,512]{2,1,0:T(8,128)(2,1)S(1)} %bitcast.31, bf16[7,4,384,256]{3,2,1,0:T(8,128)(2,1)S(1)} %get-tuple-element.69.e_ref, ...), custom_call_target="tpu_custom_call" | custom-call | tf_op jit(solution)/shard_map/far_grads/pallas_call | solution.py:540
  139.1 0.7 copy-done.38
  139.7 4.4 %all-to-all-start.1 = ((bf16[16,128,512]{2,1,0:T(8,128)(2,1)}), bf16[16,128,512]{2,1,0:T(8,128)(2,1)}, u32[]{:S(2)}, u32[]{:S(2)}) async-start(bf16[16,128,512]{2,1,0:T(8,128)(2,1)} %far_grads.1), calls=%async_computation.1 | async-start | bytes 4194304 | tf_op jit(solution)/shard_map/all_to_all | solution.py:748
  144.3 2.6 %copy-done.1 = bf16[7,4,384,256]{3,2,1,0:T(8,128)(2,1)S(1)} copy-done((bf16[7,4,384,256]{3,2,1,0:T(8,128)(2,1)S(1)}, bf16[7,4,384,256]{3,2,1,0:T(8,128)(2,1)}, u32[]{:S(2)}) %copy-start.1) | copy-done | bytes 5505048
  146.9 1.5 copy-done.8
  148.4 1.2 copy-done.12
  149.5 1.2 copy-done.14
  150.7 1.0 copy-done.20
  151.7 1.0 copy-done.24
  152.8 18.0 %own_grads.1.rows_ref = f32[7,128,512]{2,1,0:T(8,128)} custom-call(s32[1]{0:T(128)} %bitcast.own_s, s32[7,16,2]{2,1,0:T(8,128)S(1)} %copy.28.lists_s, bf16[7,128,512]{2,1,0:T(8,128)(2,1)} %bitcast.61, bf16[7,128,512]{2,1,0:T(8,128)(2,1)} %bitcast.64, bf16[7,128,512]{2,1,0:T(8,128)(2,1)} %bitcast.68, f32[7,128,512]{2,1,0:T(8,128)} %bitcast.65, ...), custom_call_target="tpu_custom_call" | custom-call | flops 4697620480 | bytes 11010048 | tf_op jit(solution)/shard_map/own_grads/pallas_call | solution.py:597
  170.8 2.3 %copy-done.33 = bf16[3,3,512,512]{3,2,1,0:T(8,128)(2,1)S(1)} copy-done((bf16[3,3,512,512]{3,2,1,0:T(8,128)(2,1)S(1)}, bf16[3,3,512,512]{3,2,1,0:T(8,128)(2,1)}, u32[]{:S(2)}) %copy-start.33) | copy-done | bytes 4718616
  173.1 5.6 %conv_two.1 = bf16[896,512]{1,0:T(8,128)(2,1)S(1)} custom-call(s32[1]{0:T(128)} %bitcast.own_s, bf16[896,512]{1,0:T(8,128)(2,1)S(1)} %copy-done.42, bf16[224,512]{1,0:T(8,128)(2,1)S(1)} %collective-permute-done.6.near_ref, bf16[224,512]{1,0:T(8,128)(2,1)S(1)} %copy-done.39, bf16[3,3,512,512]{3,2,1,0:T(8,128)(2,1)S(1)} %copy-done.33, ...), custom_call_target="tpu_custom_call" | custom-call | flops 4227858432 | bytes 4718592 | tf_op jit(solution)/shard_map/conv_two/pallas_call | solution.py:358
  178.7 1.6 copy.40
  180.3 11.4 %all-to-all-done.1.back_ref = bf16[16,128,512]{2,1,0:T(8,128)(2,1)} async-done(((bf16[16,128,512]{2,1,0:T(8,128)(2,1)}), bf16[16,128,512]{2,1,0:T(8,128)(2,1)}, u32[]{:S(2)}, u32[]{:S(2)}) %all-to-all-start.1) | async-done | bytes 2097184 | tf_op jit(solution)/shard_map/all_to_all | solution.py:748
  191.7 1.5 copy-done.18
  193.2 4.3 %final.1 = bf16[4,7,32,512]{3,2,1,0:T(8,128)(2,1)S(1)} custom-call(s32[16]{0:T(128)S(1)} %broadcast_add_fusion.table_s, bf16[16,128,512]{2,1,0:T(8,128)(2,1)} %all-to-all-done.1.back_ref, f32[7,128,512]{2,1,0:T(8,128)S(1)} %copy-done.9, bf16[4,7,32,512]{3,2,1,0:T(8,128)(2,1)S(1)} %bitcast.36, f32[4,7,32,512]{3,2,1,0:T(8,128)S(1)} %bitcast.42, ...), custom_call_target="tpu_custom_call" | custom-call | tf_op jit(solution)/shard_map/final/pallas_call | solution.py:647
  197.5 1.6 copy.35
  (88 shorter events, 2.2 us)
Async XLA Ops:
  2.8 6.4 %copy-start.4 = (bf16[7,32,4,512]{3,1,0,2:T(8,128)(2,1)}, bf16[7,32,4,512]{3,1,0,2:T(8,128)(2,1)S(1)}, u32[]{:S(2)}) copy-start(bf16[7,32,4,512]{3,1,0,2:T(8,128)(2,1)S(1)} %copy.41) | copy-start | bytes 2752516
  9.3 54.0 %all-to-all-start = ((bf16[16,128,512]{2,1,0:T(8,128)(2,1)}), bf16[16,128,512]{2,1,0:T(8,128)(2,1)S(1)}, u32[]{:S(2)}, u32[]{:S(2)}) async-start(bf16[16,128,512]{2,1,0:T(8,128)(2,1)} %get-tuple-element.48), calls=%async_computation | async-start | bytes 4194304 | tf_op jit(solution)/shard_map/all_to_all | solution.py:707
  15.8 7.5 %copy-start.6 = (bf16[512,512]{1,0:T(8,128)(2,1)S(1)}, bf16[512,512]{1,0:T(8,128)(2,1)}, u32[]{:S(2)}) copy-start(bf16[512,512]{1,0:T(8,128)(2,1)} %wv_ref.2) | copy-start | bytes 1572868
  18.4 8.3 %copy-start.10 = (bf16[512,512]{1,0:T(8,128)(2,1)S(1)}, bf16[512,512]{1,0:T(8,128)(2,1)}, u32[]{:S(2)}) copy-start(bf16[512,512]{1,0:T(8,128)(2,1)} %wk_ref.5) | copy-start | bytes 1572868
  19.1 66.8 %collective-permute-start.2 = (bf16[224,512]{1,0:T(8,128)(2,1)}, bf16[224,512]{1,0:T(8,128)(2,1)S(1)}, u32[]{:S(2)}, u32[]{:S(2)}) collective-permute-start(bf16[224,512]{1,0:T(8,128)(2,1)} %bitcast.16), channel_id=1, source_target_pairs={{0,1},{1,0},{2,3},{3,2},{4,5},{5,4},{6,7},{7,6},{8,9},{9,8},{10,11... | collective-permute-start | bytes 688136 | tf_op jit(solution)/shard_map/ppermute | solution.py:666
  20.2 65.7 %collective-permute-start.3 = (bf16[224,512]{1,0:T(8,128)(2,1)}, bf16[224,512]{1,0:T(8,128)(2,1)}, u32[]{:S(2)}, u32[]{:S(2)}) collective-permute-start(bf16[224,512]{1,0:T(8,128)(2,1)} %bitcast.17), channel_id=1, source_target_pairs={{1,2},{2,1},{3,4},{4,3},{5,6},{6,5},{7,8},{8,7},{9,10},{10,9},{11,... | collective-permute-start | bytes 688136 | tf_op jit(solution)/shard_map/ppermute | solution.py:666
  26.7 1.0 copy-start.15
  27.7 1.0 copy-start.23
  28.8 1.2 copy-start.37
  29.9 33.3 %copy-start.26 = (s32[7,16]{1,0:T(8,128)S(1)}, s32[7,16]{1,0:T(8,128)}, u32[]{:S(2)}) copy-start(s32[7,16]{1,0:T(8,128)} %counts_s.5) | copy-start | bytes 1348
  29.9 33.3 %copy-start.29 = (f32[512]{0:T(512)S(1)}, f32[512]{0:T(512)}, u32[]{:S(2)}) copy-start(f32[512]{0:T(512)} %param.21) | copy-start | bytes 6148
  63.3 18.5 %copy-start.2 = (bf16[16,128,512]{2,1,0:T(8,128)(2,1)}, bf16[16,128,512]{2,1,0:T(8,128)(2,1)S(1)}, u32[]{:S(2)}) copy-start(bf16[16,128,512]{2,1,0:T(8,128)(2,1)S(1)} %all-to-all-done.refs_0_) | copy-start | bytes 6291460
  63.3 1.4 copy-start.16
  65.7 20.2 %copy-start.21 = (bf16[4,7,32,512]{3,2,1,0:T(8,128)(2,1)S(1)}, bf16[4,7,32,512]{3,2,1,0:T(8,128)(2,1)}, u32[]{:S(2)}) copy-start(bf16[4,7,32,512]{3,2,1,0:T(8,128)(2,1)} %copy.29) | copy-start | bytes 2752516
  65.7 29.1 %slice-start = ((s8[4718592]{0:T(1024)(128)(4,1)}), s8[4194304]{0:T(1024)(128)(4,1)S(1)}, s32[]{:S(2)}) async-start(s8[4718592]{0:T(1024)(128)(4,1)} %bitcast.50), calls=%async_computation.2 | async-start | bytes 8388608
  81.8 29.7 %copy-start.34 = (bf16[4,7,32,512]{3,2,1,0:T(8,128)(2,1)}, bf16[4,7,32,512]{3,2,1,0:T(8,128)(2,1)S(1)}, u32[]{:S(2)}) copy-start(bf16[4,7,32,512]{3,2,1,0:T(8,128)(2,1)S(1)} %get-tuple-element.73) | copy-start | bytes 2752516
  81.8 42.8 %copy-start = (bf16[7,4,384,256]{3,2,1,0:T(8,128)(2,1)}, bf16[7,4,384,256]{3,2,1,0:T(8,128)(2,1)S(1)}, u32[]{:S(2)}) copy-start(bf16[7,4,384,256]{3,2,1,0:T(8,128)(2,1)S(1)} %get-tuple-element.69.e_ref) | copy-start | bytes 16515076
  81.8 42.8 %copy-start.7 = (bf16[7,256,512]{2,1,0:T(8,128)(2,1)}, bf16[7,256,512]{2,1,0:T(8,128)(2,1)S(1)}, u32[]{:S(2)}) copy-start(bf16[7,256,512]{2,1,0:T(8,128)(2,1)S(1)} %get-tuple-element.81.kf_ref) | copy-start | bytes 5505028
  81.8 42.8 %copy-start.11 = (bf16[7,128,512]{2,1,0:T(8,128)(2,1)}, bf16[7,128,512]{2,1,0:T(8,128)(2,1)S(1)}, u32[]{:S(2)}) copy-start(bf16[7,128,512]{2,1,0:T(8,128)(2,1)S(1)} %get-tuple-element.78.mixed_ref) | copy-start | bytes 2752516
  81.8 42.8 %copy-start.19 = (f32[7,128,128]{2,1,0:T(8,128)}, f32[7,128,128]{2,1,0:T(8,128)S(1)}, u32[]{:S(2)}) copy-start(f32[7,128,128]{2,1,0:T(8,128)S(1)} %get-tuple-element.80.col_ref) | copy-start | bytes 1376260
  81.8 13.0 %collective-permute-start = (bf16[224,512]{1,0:T(8,128)(2,1)S(1)}, bf16[224,512]{1,0:T(8,128)(2,1)S(1)}, u32[]{:S(2)}, u32[]{:S(2)}) collective-permute-start(bf16[224,512]{1,0:T(8,128)(2,1)S(1)} %bitcast.57), channel_id=1, source_target_pairs={{0,1},{1,0},{2,3},{3,2},{4,5},{5,4},{6,7},{7,6},{8,9},{9,8},{10,11... | collective-permute-start | bytes 688136 | tf_op jit(solution)/shard_map/ppermute | solution.py:666
  82.1 12.7 %collective-permute-start.1 = (bf16[224,512]{1,0:T(8,128)(2,1)S(1)}, bf16[224,512]{1,0:T(8,128)(2,1)S(1)}, u32[]{:S(2)}, u32[]{:S(2)}) collective-permute-start(bf16[224,512]{1,0:T(8,128)(2,1)S(1)} %bitcast.56), channel_id=1, source_target_pairs={{1,2},{2,1},{3,4},{4,3},{5,6},{6,5},{7,8},{8,7},{9,10},{10,9},{11,... | collective-permute-start | bytes 688136 | tf_op jit(solution)/shard_map/ppermute | solution.py:666
  86.0 2.3 %copy-start.32 = (bf16[3,3,512,512]{3,2,1,0:T(8,128)(2,1)S(1)}, bf16[3,3,512,512]{3,2,1,0:T(8,128)(2,1)}, u32[]{:S(2)}) copy-start(bf16[3,3,512,512]{3,2,1,0:T(8,128)(2,1)} %w_ref.8) | copy-start | bytes 14155780
  88.3 6.5 %slice-start.1 = ((s8[4718592]{0:T(1024)(128)(4,1)}), s8[524288]{0:T(1024)(128)(4,1)S(1)}, s32[]{:S(2)}) async-start(s8[4718592]{0:T(1024)(128)(4,1)} %bitcast.50), calls=%async_computation.3 | async-start | bytes 1048576
  88.3 6.6 %copy-start.40 = (f32[512]{0:T(512)S(1)}, f32[512]{0:T(512)}, u32[]{:S(2)}) copy-start(f32[512]{0:T(512)} %param.23) | copy-start | bytes 6148
  94.9 11.4 %copy-start.3 = (bf16[16,128,512]{2,1,0:T(8,128)(2,1)S(1)}, bf16[16,128,512]{2,1,0:T(8,128)(2,1)}, u32[]{:S(2)}) copy-start(bf16[16,128,512]{2,1,0:T(8,128)(2,1)} %copy-done.2) | copy-start | bytes 6291460
  103.2 4.9 %collective-permute-start.4 = (bf16[224,512]{1,0:T(8,128)(2,1)S(1)}, bf16[224,512]{1,0:T(8,128)(2,1)S(1)}, u32[]{:S(2)}, u32[]{:S(2)}) collective-permute-start(bf16[224,512]{1,0:T(8,128)(2,1)S(1)} %get-tuple-element.66), channel_id=1, source_target_pairs={{0,1},{1,0},{2,3},{3,2},{4,5},{5,4},{6,7},{7,6},{8,9},{9,8},{10,11... | collective-permute-start | bytes 688136 | tf_op jit(solution)/shard_map/ppermute | solution.py:666
  103.2 8.3 %collective-permute-start.5 = (bf16[224,512]{1,0:T(8,128)(2,1)S(1)}, bf16[224,512]{1,0:T(8,128)(2,1)S(1)}, u32[]{:S(2)}, u32[]{:S(2)}) collective-permute-start(bf16[224,512]{1,0:T(8,128)(2,1)S(1)} %get-tuple-element.67), channel_id=1, source_target_pairs={{1,2},{2,1},{3,4},{4,3},{5,6},{6,5},{7,8},{8,7},{9,10},{10,9},{11,... | collective-permute-start | bytes 688136 | tf_op jit(solution)/shard_map/ppermute | solution.py:666
  119.6 19.4 %copy-start.13 = (bf16[896,512]{1,0:T(8,128)(2,1)}, bf16[896,512]{1,0:T(8,128)(2,1)S(1)}, u32[]{:S(2)}) copy-start(bf16[896,512]{1,0:T(8,128)(2,1)S(1)} %get-tuple-element.77) | copy-start | bytes 2752516
  119.6 19.4 %copy-start.17 = (f32[896,512]{1,0:T(8,128)}, f32[896,512]{1,0:T(8,128)S(1)}, u32[]{:S(2)}) copy-start(f32[896,512]{1,0:T(8,128)S(1)} %get-tuple-element.93) | copy-start | bytes 5505028
  119.6 19.4 %collective-permute-start.6 = (bf16[224,512]{1,0:T(8,128)(2,1)S(1)}, bf16[224,512]{1,0:T(8,128)(2,1)S(1)}, u32[]{:S(2)}, u32[]{:S(2)}) collective-permute-start(bf16[224,512]{1,0:T(8,128)(2,1)S(1)} %get-tuple-element.83), channel_id=1, source_target_pairs={{0,1},{1,0},{2,3},{3,2},{4,5},{5,4},{6,7},{7,6},{8,9},{9,8},{10,11... | collective-permute-start | bytes 688136 | tf_op jit(solution)/shard_map/ppermute | solution.py:666
  121.6 17.4 %collective-permute-start.7 = (bf16[224,512]{1,0:T(8,128)(2,1)S(1)}, bf16[224,512]{1,0:T(8,128)(2,1)S(1)}, u32[]{:S(2)}, u32[]{:S(2)}) collective-permute-start(bf16[224,512]{1,0:T(8,128)(2,1)S(1)} %get-tuple-element.84), channel_id=1, source_target_pairs={{1,2},{2,1},{3,4},{4,3},{5,6},{6,5},{7,8},{8,7},{9,10},{10,9},{11,... | collective-permute-start | bytes 688136 | tf_op jit(solution)/shard_map/ppermute | solution.py:666
  139.0 5.2 %copy-start.31 = (s32[7]{0:T(128)S(1)}, s32[7]{0:T(128)}, u32[]{:S(2)}) copy-start(s32[7]{0:T(128)} %match_s.1) | copy-start | bytes 88
  139.0 5.2 %copy-start.43 = (s32[7,16,2]{1,2,0:T(2,128)S(1)}, s32[7,16,2]{1,2,0:T(2,128)}, u32[]{:S(2)}) copy-start(s32[7,16,2]{1,2,0:T(2,128)} %param.26) | copy-start | bytes 2692
  139.7 52.0 %all-to-all-start.1 = ((bf16[16,128,512]{2,1,0:T(8,128)(2,1)}), bf16[16,128,512]{2,1,0:T(8,128)(2,1)}, u32[]{:S(2)}, u32[]{:S(2)}) async-start(bf16[16,128,512]{2,1,0:T(8,128)(2,1)} %far_grads.1), calls=%async_computation.1 | async-start | bytes 4194304 | tf_op jit(solution)/shard_map/all_to_all | solution.py:748
  144.3 2.6 %copy-start.1 = (bf16[7,4,384,256]{3,2,1,0:T(8,128)(2,1)S(1)}, bf16[7,4,384,256]{3,2,1,0:T(8,128)(2,1)}, u32[]{:S(2)}) copy-start(bf16[7,4,384,256]{3,2,1,0:T(8,128)(2,1)} %copy-done) | copy-start | bytes 16515076
  146.9 1.5 copy-start.8
  148.4 1.2 copy-start.12
  149.5 1.2 copy-start.14
  151.7 1.0 copy-start.24
  152.8 18.0 %copy-start.35 = (bf16[4,7,32,512]{3,2,1,0:T(8,128)(2,1)S(1)}, bf16[4,7,32,512]{3,2,1,0:T(8,128)(2,1)}, u32[]{:S(2)}) copy-start(bf16[4,7,32,512]{3,2,1,0:T(8,128)(2,1)} %copy-done.34) | copy-start | bytes 2752516
  152.8 18.0 %copy-start.39 = (bf16[224,512]{1,0:T(8,128)(2,1)S(1)}, bf16[224,512]{1,0:T(8,128)(2,1)}, u32[]{:S(2)}) copy-start(bf16[224,512]{1,0:T(8,128)(2,1)} %copy-done.38) | copy-start | bytes 688132
  152.8 18.0 %copy-start.42 = (bf16[896,512]{1,0:T(8,128)(2,1)S(1)}, bf16[896,512]{1,0:T(8,128)(2,1)}, u32[]{:S(2)}) copy-start(bf16[896,512]{1,0:T(8,128)(2,1)} %copy-done.41) | copy-start | bytes 2752516
  170.8 2.3 %copy-start.33 = (bf16[3,3,512,512]{3,2,1,0:T(8,128)(2,1)S(1)}, bf16[3,3,512,512]{3,2,1,0:T(8,128)(2,1)}, u32[]{:S(2)}) copy-start(bf16[3,3,512,512]{3,2,1,0:T(8,128)(2,1)} %w_ref.8) | copy-start | bytes 14155780
  173.1 18.6 %copy-start.9 = (f32[7,128,512]{2,1,0:T(8,128)S(1)}, f32[7,128,512]{2,1,0:T(8,128)}, u32[]{:S(2)}) copy-start(f32[7,128,512]{2,1,0:T(8,128)} %own_grads.1.rows_ref) | copy-start | bytes 5505028
  173.1 18.6 %copy-start.28 = (f32[512]{0:T(512)S(1)}, f32[512]{0:T(512)}, u32[]{:S(2)}) copy-start(f32[512]{0:T(512)} %param.16) | copy-start | bytes 6148
  178.7 13.0 %copy-start.5 = (bf16[7,32,4,512]{3,1,0,2:T(8,128)(2,1)S(1)}, bf16[7,32,4,512]{3,1,0,2:T(8,128)(2,1)}, u32[]{:S(2)}) copy-start(bf16[7,32,4,512]{3,1,0,2:T(8,128)(2,1)} %copy-done.4) | copy-start | bytes 2752516
  191.7 1.5 copy-start.18
  (8 other events, 6.7 us)

commit v4 on v3

--- a/solution.py
+++ b/solution.py
@@ -64,7 +64,7 @@
 
 def prep_kernel(n_cols, own_s, match_s, lists_s, counts_s, clip_ref, gain_ref, rows_ref, send_ref, sem):
     cams = match_s.shape[0]
-    picks = lists_s.shape[2]
+    picks = lists_s.shape[1]
     own = own_s[0]
     tw, _, nr, width = clip_ref.shape
     for c in range(cams):
@@ -75,7 +75,7 @@
         cam = jnp.int32(0)
         for c in range(cams):
             for s in range(picks):
-                hit = (lists_s[c, i, s] == own) & (s < counts_s[c, i])
+                hit = (lists_s[c, s, i] == own) & (s < counts_s[c, i])
                 cam = jnp.where(hit, match_s[c], cam)
         pltpu.make_async_copy(rows_ref.at[cam], send_ref.at[i], sem.at[i]).start()
 
@@ -110,7 +110,7 @@
             scratch_shapes=[pltpu.SemaphoreType.DMA((n_cols,))],
         ),
         compiler_params=params(8),
-    )(own, matching, lists, counts, clip_t, gain)
+    )(own, hbm(matching), lists, hbm(counts), clip_t, hbm(gain))
 
 
 def project_kernel(head, blk, rows_ref, wq_ref, wk_ref, wv_ref, wvt_ref, q_ref, k_ref, v_ref, vt_ref, rq_ref, rk_ref):
@@ -183,7 +183,7 @@
         vcat[:, 128:] = jnp.ones((pairs, PAD, keys), BF16)
 
     ones_h = head_ones(half, head)
-    rows = jnp.concatenate([arrived_ref[lists_s[c, own, s]] for s in range(picks)], axis=0)
+    rows = jnp.concatenate([arrived_ref[lists_s[c, s, own]] for s in range(picks)], axis=0)
     kcat[:blk] = k_ref[0]
     vcat[:, :128, :blk] = vt_ref[0].reshape(pairs, 128, blk)
     vcat[:, :128, blk:] = mm_t(wvt_ref[...], rows).astype(BF16).reshape(pairs, 128, keys - blk)
@@ -240,7 +240,7 @@
 def attend(own, lists, counts, arrived, q, k, vt, clip_t, wk, wvt, wo, gain, head):
     tw, cams, nr, width = clip_t.shape
     blk = tw * nr
-    picks = lists.shape[2]
+    picks = lists.shape[1]
     keys = (1 + picks) * blk
     pairs = width // 128
     slab = pl.BlockSpec((tw, 1, nr, width), lambda c, *_: (0, c, 0, 0))
@@ -256,7 +256,7 @@
         pltpu.VMEM((cams, blk, 128), F32),
         pltpu.VMEM((cams, blk, width), BF16),
     )
-    weights = (wk, wvt, wo, gain)
+    weights = (wk, hbm(wvt), hbm(wo), gain)
     return pl.pallas_call(
         functools.partial(attend_kernel, head, picks),
         name="attend",
@@ -442,24 +442,104 @@
     chunks(out.shape[0], one)
 
 
-def grad_one_body(rows_of, even, edge, extra, outs):
-    lifted_ref, cot_ref, gain_ref, wo_ref = extra
-    d_lifted_ref, d_mixed_ref = outs
+def grad_main_kernel(edge, act_ref, w_ref, y_ref, x_ref):
+    step = pl.program_id(0)
+    total, width = act_ref.shape
+
+    @pl.when(step == 0)
+    def _():
+        blank = jnp.zeros((edge, width), BF16)
+        x_ref[:edge, :width] = blank
+        x_ref[edge:, :width] = act_ref[: total - edge]
+        x_ref[:, width : 2 * width] = act_ref[...]
+        x_ref[: total - edge, 2 * width :] = act_ref[edge:]
+        x_ref[total - edge :, 2 * width :] = blank
+
+    conv_step(w_ref, x_ref, y_ref, step, True)
+
+
+def grad_main(act, weights, edge):
+    total, width = act.shape
+    return pl.pallas_call(
+        functools.partial(grad_main_kernel, edge),
+        name="grad_main",
+        out_shape=pltpu.VMEM((3, total, width), F32),
+        grid_spec=pltpu.PrefetchScalarGridSpec(
+            num_scalar_prefetch=0,
+            grid=(3,),
+            in_specs=[
+                whole((total, width)),
+                pl.BlockSpec((1, 3, width, width), lambda p, *_: (p, 0, 0, 0)),
+            ],
+            out_specs=whole((3, total, width)),
+            scratch_shapes=[pltpu.VMEM((total, 3 * width), BF16)],
+        ),
+        compiler_params=params(14),
+        cost_estimate=pl.CostEstimate(
+            flops=18 * total * width * width, bytes_accessed=18 * width * width, transcendentals=0
+        ),
+    )(act, weights)
+
+
+def grad_tail_kernel(nr, own_s, near_ref, farther_ref, w_ref, y_ref, lifted_ref, cot_ref, gain_ref,
+                     wo_ref, d_lifted_ref, d_mixed_ref, z_ref):
+    edge = near_ref.shape[0]
+    total = d_lifted_ref.shape[0]
+    even = lax.rem(own_s[0], 2) == 0
+    near = near_ref[...]
+    farther = farther_ref[...]
+    left = jnp.where(even, farther, near)
+    right = jnp.where(even, near, farther)
+    for p in range(3):
+        z_ref[0, p] = mm_t(left, w_ref[p, 2])
+        z_ref[1, p] = mm_t(right, w_ref[p, 0])
     gain = gain_ref[...]
-    total = d_lifted_ref.shape[0]
-
-    def one(start):
-        rows = pl.ds(start, CHUNK)
-        lifted = lifted_ref[rows, :].astype(F32)
-        r = rms(lifted)
-        hat = lifted * r
-        _, slope = silu_parts(hat * gain)
-        g = rows_of(start, CHUNK) * slope * gain
-        back = r * (g - hat * jnp.mean(g * hat, axis=-1, keepdims=True))
-        d_lifted_ref[rows, :] = cot_ref[rows, :].astype(F32) + back
-
-    chunks(total, one)
+    split = (edge // nr + 1) // 2 * nr
+    for start in range(0, total, edge):
+        for first, last in ((0, split), (split, edge)):
+            size = last - first
+            rows = slice(start + first, start + last)
+            taps = []
+            for p in range(3):
+                tap = y_ref[p, rows]
+                if start == 0:
+                    tap = tap + z_ref[0, p, first:last]
+                if start == total - edge:
+                    tap = tap + z_ref[1, p, first:last]
+                taps.append(tap)
+            place = lax.broadcasted_iota(jnp.int32, (size, 1), 0) % nr
+            conv = (
+                jnp.where(place == 0, 0.0, pltpu.roll(taps[2], 1, 0))
+                + taps[1]
+                + jnp.where(place == nr - 1, 0.0, pltpu.roll(taps[0], size - 1, 0))
+            )
+            lifted = lifted_ref[rows].astype(F32)
+            r = rms(lifted)
+            hat = lifted * r
+            _, slope = silu_parts(hat * gain)
+            g = conv * slope * gain
+            back = r * (g - hat * jnp.mean(g * hat, axis=-1, keepdims=True))
+            d_lifted_ref[rows] = cot_ref[rows].astype(F32) + back
     d_mixed_ref[...] = mm_t(d_lifted_ref[...].astype(BF16), wo_ref[...]).astype(BF16)
+
+
+def grad_tail(own, near, farther, weights, y, lifted, cot, gain, wo, nr):
+    args = (near, farther, weights, y, lifted, cot, gain, wo)
+    edge, width = near.shape
+    outs = (pltpu.VMEM(lifted.shape, F32), pltpu.VMEM(lifted.shape, BF16))
+    return pl.pallas_call(
+        functools.partial(grad_tail_kernel, nr),
+        name="grad_tail",
+        out_shape=outs,
+        grid_spec=pltpu.PrefetchScalarGridSpec(
+            num_scalar_prefetch=1,
+            grid=(1,),
+            in_specs=[whole(x.shape) for x in args],
+            out_specs=[whole(x.shape) for x in outs],
+            scratch_shapes=[pltpu.VMEM((2, 3, edge, width), F32)],
+        ),
+        compiler_params=params(14),
+    )(own, *args)
 
 
 def head_norm_back(grad, hat, r, ones, head):
@@ -497,7 +577,7 @@
     for p in range(width // 128):
         cols = slice(128 * p, 128 * (p + 1))
         q2, dm2, shift = pair_queries(p, q, dm, col, drift, low)
-        far_v = jnp.concatenate([vf_ref[lists_s[c, own, s], :, cols] for s in range(picks)], axis=0)
+        far_v = jnp.concatenate([vf_ref[lists_s[c, s, own], :, cols] for s in range(picks)], axis=0)
         e = e_ref[c, p, blk:]
         d_scaled = (e.astype(F32) * (mm_t(far_v, dm2) - shift)).astype(BF16)
         kgrad[c, :, cols] = mm(d_scaled, q2)
@@ -523,7 +603,7 @@
                 for s in range(picks):
                     pltpu.make_async_copy(
                         shares.at[i, pl.ds(s * blk, blk)],
-                        send_ref.at[lists_s[i, own, s]],
+                        send_ref.at[lists_s[i, s, own]],
                         sems.at[i, s],
                     ).start()
         for i in range(cams):
@@ -535,7 +615,7 @@
 
 def far_grads(own, lists, counts, n_cols, q, vf, e, dm_t, mixed, row, col, kf, rf, wk, wv, head):
     cams, blk, width = mixed.shape
-    picks = lists.shape[2]
+    picks = lists.shape[1]
     args = (vf, e, dm_t, mixed, row, col, kf, rf, wk, wv)
     return pl.pallas_call(
         functools.partial(far_grads_kernel, head, picks),
@@ -569,7 +649,7 @@
     dm = dm_ref[:, c].reshape(blk, width)
     drift = drift_rows(head, dm, mixed_ref[c], row_ref[c])
     col = col_ref[c]
-    listed = [lists_s[c, own, s] for s in range(picks)]
+    listed = [lists_s[c, s, own] for s in range(picks)]
     dq, dk, dv = [], [], []
     for p in range(width // 128):
         cols = slice(128 * p, 128 * (p + 1))
@@ -591,7 +671,7 @@
 
 def own_grads(own, lists, q, k, v, rq, rk, vf, e, dm_t, mixed, row, col, kf, wq, wk, wv, head):
     cams, blk, width = mixed.shape
-    picks = lists.shape[2]
+    picks = lists.shape[1]
     windows = (q, k, v, rq, rk)
     args = (vf, e, dm_t, mixed, row, col, kf, wq, wk, wv)
     return pl.pallas_call(
@@ -691,6 +771,7 @@
     blk = nr * tw
     flat = (total, width)
     slabs = (tw, views, nr, width)
+    block_lists = jnp.transpose(block_lists, (0, 2, 1))
     gain_attn = gain_attn.reshape(1, width)
     gain_first = gain_first.reshape(1, width)
     gain_second = gain_second.reshape(1, width)
@@ -707,9 +788,9 @@
     arrived = lax.all_to_all(send, "cols", split_axis=0, concat_axis=0, tiled=True)
     rows, w_value, lists, live = lax.optimization_barrier((rows, w_value, block_lists, counts))
     w_value_t = w_value.T
-    slots = jnp.arange(lists.shape[2], dtype=jnp.int32)
-    asks = (lists == own_index) & (slots[None, None, :] < live[:, :, None])
-    table = jnp.sum(jnp.where(asks, matching[:, None, None] + 1, 0), axis=(0, 2)) - 1
+    slots = jnp.arange(lists.shape[1], dtype=jnp.int32)
+    asks = (lists == own_index) & (slots[None, :, None] < live[:, None, :])
+    table = jnp.sum(jnp.where(asks, matching[:, None, None] + 1, 0), axis=(0, 1)) - 1
     q, k, v, vt, rq, rk = project(rows.reshape(flat), w_query, w_key, w_value, w_value_t, head, blk)
     q, k, v, rq, rk = (a.reshape(views, blk, width) for a in (q, k, v, rq, rk))
     arrived, q, k, v, vt, rq, rk = lax.optimization_barrier((arrived, q, k, v, vt, rq, rk))
@@ -731,12 +812,11 @@
     )
     d_near, d_far = exchange_edges(d_near, d_far)
     vf = far_values(arrived.reshape(-1, width), w_value)
-    d_near, d_far, vf = lax.optimization_barrier((d_near, d_far, vf))
+    y_grad = grad_main(d_conv, conv_first, views * nr)
+    d_near, d_far, vf, y_grad = lax.optimization_barrier((d_near, d_far, vf, y_grad))
     vf = vf.reshape(arrived.shape)
-    d_lifted, d_mixed = conv_call(
-        "grad_one", grad_one_body, own, d_conv, d_near, d_far, conv_first,
-        (lifted.reshape(flat), cot_t.reshape(flat), gain_first, w_out),
-        (pltpu.VMEM(flat, F32), flat_bf), nr, True,
+    d_lifted, d_mixed = grad_tail(
+        own, d_near, d_far, conv_first, y_grad, lifted.reshape(flat), cot_t.reshape(flat), gain_first, w_out, nr
     )
     d_mixed, act_near, act_far = lax.optimization_barrier((d_mixed, act_near, act_far))
     d_mixed = d_mixed.reshape(slabs)

time: 200 us -> 193 us (0.965)
  local copies, waits for them, and re-layouts: 37.8 us -> 34.5 us
  waiting for transfers between devices: 42.1 us -> 39.7 us
    pallas_call x0 -> x2, Pallas kernels: none -> 8.24 us  [the longest x1 5.06 us: grad_main(): pl.pallas_call(functools.partial(grad_main_kernel, edge), name='grad_main...]
    pallas_call x4 -> x3, Pallas kernels: 27.5 us -> 19.5 us  [conv_call(): pl.pallas_call(functools.partial(conv_kernel, body, len(extra), transpose...]
    unnamed x97 -> x90, local copies, waits for them, and re-layouts: 30.3 us -> 27 us
    ppermute x4, waiting for transfers between devices: 3.4 us -> 0.12 us  [exchange_edges(): lax.ppermute(farther, 'cols', outer)]
  transfers between devices with their start and end apart: 10 -> 10, of which waited for: 3 -> 3; matrix products, arithmetic and copies ran while one was open for 5% -> 5% of each run, Pallas kernels for 34% -> 38%
where the time goes in v4:
time: 193 us; the launch traced here: 192 us
  Pallas kernels  90.4 us (47%)
  waiting for transfers between devices  39.7 us (21%)
  local copies, waits for them, and re-layouts  34.5 us (18%)
  starting transfers between devices  26.5 us (14%)
    all_to_all x1, waiting for transfers between devices, local(): lax.all_to_all(send, 'cols', split_axis=0, concat_axis=0, tiled=True)  27.3 us
    unnamed x90, local copies, waits for them, and re-layouts  27 us
    pallas_call x3, Pallas kernels, conv_call(): pl.pallas_call(functools.partial(conv_kernel, body, len(extra), transpose...  19.5 us
    pallas_call x1, Pallas kernels, own_grads(): pl.pallas_call(functools.partial(own_grads_kernel, head, picks), name='ow...  17.1 us
    pallas_call x1, Pallas kernels, attend(): pl.pallas_call(functools.partial(attend_kernel, head, picks), name='atten...  16.6 us
    pallas_call x1, Pallas kernels, far_grads(): pl.pallas_call(functools.partial(far_grads_kernel, head, picks), name='fa...  13.6 us
    ppermute x4, starting transfers between devices, exchange_edges(): lax.ppermute(farther, 'cols', outer)  13 us
    all_to_all x1, waiting for transfers between devices, local(): lax.all_to_all(send_back, 'cols', split_axis=0, concat_axis=0, tiled=True)  12.2 us
  transfers between devices with their start and end apart: 10, of which 3 were waited for; matrix products, arithmetic and copies ran while one was open for 5% of the time, Pallas kernels for 38%

profile of v4, /device:TPU:13, one launch (start us, length us, event | category | flops | bytes accessed | tf_op | source)
XLA Modules:
  0.0 192.3 jit_solution(9086322882101560234)
XLA Ops:
  0.6 1.4 copy.33
  2.0 0.7 copy-done.26
  2.7 3.4 %prep.1 = (bf16[7,128,512]{2,1,0:T(8,128)(2,1)S(1)}, bf16[16,128,512]{2,1,0:T(8,128)(2,1)}) custom-call(s32[1]{0:T(128)} %bitcast.own_s, s32[7]{0:T(128)} %match_s.1, s32[7,2,16]{2,1,0:T(2,128)S(1)} %bitcast.51, s32[7,16]{1,0:T(8,128)} %counts_s.5, bf16[4,7,32,512]{3,2,1,0:T(8,128)(2,1)S(1)} %bitcast.35, f32[1,512]{1,0:T(1,128)} %bitcast.56), custom_call_target="tpu_custom_call" | custom-call | tf_op jit(solution)/shard_map/prep/pallas_call | solution.py:98
  6.2 0.9 copy-done.33
  7.1 6.6 %all-to-all-start = ((bf16[16,128,512]{2,1,0:T(8,128)(2,1)}), bf16[16,128,512]{2,1,0:T(8,128)(2,1)S(1)}, u32[]{:S(2)}, u32[]{:S(2)}) async-start(bf16[16,128,512]{2,1,0:T(8,128)(2,1)} %get-tuple-element.49), calls=%async_computation | async-start | bytes 4194304 | tf_op jit(solution)/shard_map/all_to_all | solution.py:788
  13.7 2.6 %constant_dynamic-slice_fusion = (bf16[7,32,1,512]{3,2,1,0:T(2,128)(2,1)S(1)}, bf16[7,32,1,512]{3,2,1,0:T(2,128)(2,1)S(1)}) fusion(bf16[7,32,4,512]{3,2,1,0:T(4,128)(2,1)} %param.15, s32[]{:T(128)S(6)} %select_n.20, s32[]{:T(128)S(6)} %select_n.19), kind=kLoop, calls=%fused_computation.4 | loop fusion | bytes 917512 | tf_op jit(solution)/shard_map/dynamic-slice.1
  16.3 0.7 copy.28
  17.0 0.4 collective-permute-start.2
  17.4 0.7 copy.29
  18.1 3.1 %collective-permute-start.3 = (bf16[224,512]{1,0:T(8,128)(2,1)}, bf16[224,512]{1,0:T(8,128)(2,1)}, u32[]{:S(2)}, u32[]{:S(2)}) collective-permute-start(bf16[224,512]{1,0:T(8,128)(2,1)} %bitcast.18), channel_id=1, source_target_pairs={{1,2},{2,1},{3,4},{4,3},{5,6},{6,5},{7,8},{8,7},{9,10},{10,9},{11,... | collective-permute-start | bytes 688136 | tf_op jit(solution)/shard_map/ppermute | solution.py:746
  21.2 1.0 copy.22
  22.2 2.3 %copy.23 = bf16[4,7,32,512]{3,2,1,0:T(8,128)(2,1)} copy(bf16[4,7,32,512]{3,0,2,1:T(4,128)(2,1)} %bitcast.68) | data formatting | bytes 1835008 | tf_op jit(solution)/shard_map/transpose | solution.py:780
  24.5 1.0 copy-done.17
  25.6 1.0 copy-done.24
  26.6 1.2 copy-done.34
  27.8 6.0 %project.1 = (bf16[896,512]{1,0:T(8,128)(2,1)}, bf16[896,512]{1,0:T(8,128)(2,1)}, bf16[896,512]{1,0:T(8,128)(2,1)}, bf16[7,512,128]{2,1,0:T(8,128)(2,1)}, f32[896,512]{1,0:T(8,128)}, /*index=5*/f32[896,512]{1,0:T(8,128)}) custom-call(bf16[896,512]{1,0:T(8,128)(2,1)S(1)} %bitcast.60, bf16[512,512]{1,0:T(8,128)(2,1)S(1)} %copy-done.24, ...), custom_call_target="tpu_custom_call" | custom-call | flops 1879048192 | bytes 9175040 | tf_op jit(solution)/shard_map/project/pallas_call | solution.py:139
  33.8 27.3 %all-to-all-done.refs_0_ = bf16[16,128,512]{2,1,0:T(8,128)(2,1)S(1)} async-done(((bf16[16,128,512]{2,1,0:T(8,128)(2,1)}), bf16[16,128,512]{2,1,0:T(8,128)(2,1)S(1)}, u32[]{:S(2)}, u32[]{:S(2)}) %all-to-all-start) | async-done | bytes 2097184 | tf_op jit(solution)/shard_map/all_to_all | solution.py:788
  61.2 16.6 %attend.1 = (bf16[4,7,32,512]{3,2,1,0:T(8,128)(2,1)S(1)}, bf16[4,7,32,512]{3,2,1,0:T(8,128)(2,1)S(1)}, bf16[7,32,512]{2,1,0:T(8,128)(2,1)S(1)}, bf16[7,32,512]{2...) custom-call(s32[1]{0:T(128)} %bitcast.own_s, ...), custom_call_target="tpu_custom_call" | custom-call | tf_op jit(solution)/shard_map/attend/pallas_call | solution.py:260
  77.9 0.3 collective-permute-start
  78.1 3.8 %collective-permute-start.1 = (bf16[224,512]{1,0:T(8,128)(2,1)S(1)}, bf16[224,512]{1,0:T(8,128)(2,1)S(1)}, u32[]{:S(2)}, u32[]{:S(2)}) collective-permute-start(bf16[224,512]{1,0:T(8,128)(2,1)S(1)} %bitcast.62), channel_id=1, source_target_pairs={{1,2},{2,1},{3,4},{4,3},{5,6},{6,5},{7,8},{8,7},{9,10},{10,9},{11,... | collective-permute-start | bytes 688136 | tf_op jit(solution)/shard_map/ppermute | solution.py:746
  82.0 2.3 %copy-done.31 = bf16[3,3,512,512]{3,2,1,0:T(8,128)(2,1)S(1)} copy-done((bf16[3,3,512,512]{3,2,1,0:T(8,128)(2,1)S(1)}, bf16[3,3,512,512]{3,2,1,0:T(8,128)(2,1)}, u32[]{:S(2)}) %copy-start.31) | copy-done | bytes 4718616
  84.3 6.6 %grad_two.1.refs_0_ = f32[896,512]{1,0:T(8,128)S(1)} custom-call(s32[1]{0:T(128)} %bitcast.own_s, bf16[896,512]{1,0:T(8,128)(2,1)S(1)} %bitcast.40, bf16[224,512]{1,0:T(8,128)(2,1)S(1)} %collective-permute-done.2.near_ref, bf16[224,512]{1,0:T(8,128)(2,1)} %collective-permute-done.3.farther_ref, bf16[3,3,512,512]{3,2,1,0:T(8,128)(2,1)S(1)} %copy-done.31), custom_call_target="tpu_custom_call" | custom-call | flops 4227858432 | bytes 4718592 | tf_op jit(solution)/shard_map/grad_two/pallas_call | solution.py:358
  90.9 1.8 far_values.1
  92.8 7.3 %conv_one.1 = (bf16[896,512]{1,0:T(8,128)(2,1)S(1)}, bf16[224,512]{1,0:T(8,128)(2,1)S(1)}, bf16[224,512]{1,0:T(8,128)(2,1)S(1)}, bf16[896,512]{1,0:T(8,128)(2,1)...) custom-call(s32[1]{0:T(128)} %bitcast.own_s, bf16[896,512]{1,0:T(8,128)(2,1)S(1)} %bitcast.61, ...), custom_call_target="tpu_custom_call" | custom-call | flops 4227858432 | bytes 4718592 | tf_op jit(solution)/shard_map/conv_one/pallas_call | solution.py:358
  100.1 0.9 copy-done.38
  101.0 3.1 %collective-permute-start.5 = (bf16[224,512]{1,0:T(8,128)(2,1)S(1)}, bf16[224,512]{1,0:T(8,128)(2,1)S(1)}, u32[]{:S(2)}, u32[]{:S(2)}) collective-permute-start(bf16[224,512]{1,0:T(8,128)(2,1)S(1)} %get-tuple-element.68), channel_id=1, source_target_pairs={{1,2},{2,1},{3,4},{4,3},{5,6},{6,5},{7,8},{8,7},{9,10},{10,9},{11,... | collective-permute-start | bytes 688136 | tf_op jit(solution)/shard_map/ppermute | solution.py:746
  104.2 5.1 %grad_main.1.y_ref = f32[3,896,512]{2,1,0:T(8,128)S(1)} custom-call(bf16[896,512]{1,0:T(8,128)(2,1)S(1)} %get-tuple-element.69.act_ref, bf16[3,3,512,512]{3,2,1,0:T(8,128)(2,1)S(1)} %bitcast.39), custom_call_target="tpu_custom_call" | custom-call | flops 4227858432 | bytes 4718592 | tf_op jit(solution)/shard_map/grad_main/pallas_call | solution.py:463
  109.4 3.2 %grad_tail.1 = (f32[896,512]{1,0:T(8,128)S(1)}, bf16[896,512]{1,0:T(8,128)(2,1)S(1)}) custom-call(s32[1]{0:T(128)} %bitcast.own_s, bf16[224,512]{1,0:T(8,128)(2,1)S(1)} %collective-permute-done.4.near_ref, bf16[224,512]{1,0:T(8,128)(2,1)S(1)} %collective-permute-done.5.farther_ref, bf16[3,3,512,512]{3,2,1,0:T(8,128)(2,1)S(1)} %bitcast.39, ...), custom_call_target="tpu_custom_call" | custom-call | tf_op jit(solution)/shard_map/grad_tail/pallas_call | solution.py:530
  112.6 1.2 copy-done.18
  113.8 2.0 %collective-permute-start.6 = (bf16[224,512]{1,0:T(8,128)(2,1)S(1)}, bf16[224,512]{1,0:T(8,128)(2,1)S(1)}, u32[]{:S(2)}, u32[]{:S(2)}) collective-permute-start(bf16[224,512]{1,0:T(8,128)(2,1)S(1)} %get-tuple-element.85), channel_id=1, source_target_pairs={{0,1},{1,0},{2,3},{3,2},{4,5},{5,4},{6,7},{7,6},{8,9},{9,8},{10,11... | collective-permute-start | bytes 688136 | tf_op jit(solution)/shard_map/ppermute | solution.py:746
  115.8 2.9 %collective-permute-start.7 = (bf16[224,512]{1,0:T(8,128)(2,1)S(1)}, bf16[224,512]{1,0:T(8,128)(2,1)S(1)}, u32[]{:S(2)}, u32[]{:S(2)}) collective-permute-start(bf16[224,512]{1,0:T(8,128)(2,1)S(1)} %get-tuple-element.86), channel_id=1, source_target_pairs={{1,2},{2,1},{3,4},{4,3},{5,6},{6,5},{7,8},{8,7},{9,10},{10,9},{11,... | collective-permute-start | bytes 688136 | tf_op jit(solution)/shard_map/ppermute | solution.py:746
  118.8 13.6 %far_grads.1 = bf16[16,128,512]{2,1,0:T(8,128)(2,1)} custom-call(s32[1]{0:T(128)} %bitcast.own_s, s32[7,2,16]{2,1,0:T(2,128)S(1)} %bitcast.53, s32[7,16]{1,0:T(8,128)S(1)} %copy-done.28, bf16[7,128,512]{2,1,0:T(8,128)(2,1)} %bitcast.66, bf16[16,128,512]{2,1,0:T(8,128)(2,1)S(1)} %bitcast.32, bf16[7,4,384,256]{3,2,1,0:T(8,128)(2,1)S(1)} %get-tuple-element.71.e_ref, ...), custom_call_target="tpu_custom_call" | custom-call | tf_op jit(solution)/shard_map/far_grads/pallas_call | solution.py:620
  132.4 0.7 copy-done.35
  133.1 4.4 %all-to-all-start.1 = ((bf16[16,128,512]{2,1,0:T(8,128)(2,1)}), bf16[16,128,512]{2,1,0:T(8,128)(2,1)}, u32[]{:S(2)}, u32[]{:S(2)}) async-start(bf16[16,128,512]{2,1,0:T(8,128)(2,1)} %far_grads.1), calls=%async_computation.1 | async-start | bytes 4194304 | tf_op jit(solution)/shard_map/all_to_all | solution.py:828
  137.6 2.6 %copy-done.1 = bf16[7,4,384,256]{3,2,1,0:T(8,128)(2,1)S(1)} copy-done((bf16[7,4,384,256]{3,2,1,0:T(8,128)(2,1)S(1)}, bf16[7,4,384,256]{3,2,1,0:T(8,128)(2,1)}, u32[]{:S(2)}) %copy-start.1) | copy-done | bytes 5505048
  140.2 1.5 copy-done.8
  141.7 1.2 copy-done.13
  142.8 1.2 copy-done.15
  144.0 1.0 copy-done.21
  145.0 1.0 copy-done.25
  146.1 17.1 %own_grads.1.rows_ref = f32[7,128,512]{2,1,0:T(8,128)} custom-call(s32[1]{0:T(128)} %bitcast.own_s, s32[7,2,16]{2,1,0:T(2,128)S(1)} %bitcast.55, bf16[7,128,512]{2,1,0:T(8,128)(2,1)} %bitcast.67, bf16[7,128,512]{2,1,0:T(8,128)(2,1)} %bitcast.70, bf16[7,128,512]{2,1,0:T(8,128)(2,1)} %bitcast.74, f32[7,128,512]{2,1,0:T(8,128)} %bitcast.71, ...), custom_call_target="tpu_custom_call" | custom-call | flops 4697620480 | bytes 11010048 | tf_op jit(solution)/shard_map/own_grads/pallas_call | solution.py:677
  163.2 2.3 %copy-done.32 = bf16[3,3,512,512]{3,2,1,0:T(8,128)(2,1)S(1)} copy-done((bf16[3,3,512,512]{3,2,1,0:T(8,128)(2,1)S(1)}, bf16[3,3,512,512]{3,2,1,0:T(8,128)(2,1)}, u32[]{:S(2)}) %copy-start.32) | copy-done | bytes 4718616
  165.5 5.6 %conv_two.1 = bf16[896,512]{1,0:T(8,128)(2,1)S(1)} custom-call(s32[1]{0:T(128)} %bitcast.own_s, bf16[896,512]{1,0:T(8,128)(2,1)S(1)} %copy-done.39, bf16[224,512]{1,0:T(8,128)(2,1)S(1)} %collective-permute-done.6.near_ref, bf16[224,512]{1,0:T(8,128)(2,1)S(1)} %copy-done.36, bf16[3,3,512,512]{3,2,1,0:T(8,128)(2,1)S(1)} %copy-done.32, ...), custom_call_target="tpu_custom_call" | custom-call | flops 4227858432 | bytes 4718592 | tf_op jit(solution)/shard_map/conv_two/pallas_call | solution.py:358
  171.1 1.6 copy.32
  172.8 12.2 %all-to-all-done.1.back_ref = bf16[16,128,512]{2,1,0:T(8,128)(2,1)} async-done(((bf16[16,128,512]{2,1,0:T(8,128)(2,1)}), bf16[16,128,512]{2,1,0:T(8,128)(2,1)}, u32[]{:S(2)}, u32[]{:S(2)}) %all-to-all-start.1) | async-done | bytes 2097184 | tf_op jit(solution)/shard_map/all_to_all | solution.py:828
  185.0 1.5 copy-done.19
  186.5 4.2 %final.1 = bf16[4,7,32,512]{3,2,1,0:T(8,128)(2,1)S(1)} custom-call(s32[16]{0:T(128)S(1)} %broadcast_add_fusion.table_s, bf16[16,128,512]{2,1,0:T(8,128)(2,1)} %all-to-all-done.1.back_ref, f32[7,128,512]{2,1,0:T(8,128)S(1)} %copy-done.9, bf16[4,7,32,512]{3,2,1,0:T(8,128)(2,1)S(1)} %bitcast.37, f32[4,7,32,512]{3,2,1,0:T(8,128)S(1)} %bitcast.47, ...), custom_call_target="tpu_custom_call" | custom-call | tf_op jit(solution)/shard_map/final/pallas_call | solution.py:727
  190.7 1.6 copy.27
  (82 shorter events, 0.4 us)
Async XLA Ops:
  2.0 5.1 %copy-start.4 = (bf16[7,32,4,512]{3,1,0,2:T(8,128)(2,1)}, bf16[7,32,4,512]{3,1,0,2:T(8,128)(2,1)S(1)}, u32[]{:S(2)}) copy-start(bf16[7,32,4,512]{3,1,0,2:T(8,128)(2,1)S(1)} %copy.33) | copy-start | bytes 2752516
  7.1 54.0 %all-to-all-start = ((bf16[16,128,512]{2,1,0:T(8,128)(2,1)}), bf16[16,128,512]{2,1,0:T(8,128)(2,1)S(1)}, u32[]{:S(2)}, u32[]{:S(2)}) async-start(bf16[16,128,512]{2,1,0:T(8,128)(2,1)} %get-tuple-element.49), calls=%async_computation | async-start | bytes 4194304 | tf_op jit(solution)/shard_map/all_to_all | solution.py:788
  13.7 7.6 %copy-start.6 = (bf16[512,512]{1,0:T(8,128)(2,1)S(1)}, bf16[512,512]{1,0:T(8,128)(2,1)}, u32[]{:S(2)}) copy-start(bf16[512,512]{1,0:T(8,128)(2,1)} %wv_ref.2) | copy-start | bytes 1572868
  16.3 8.3 %copy-start.10 = (bf16[512,512]{1,0:T(8,128)(2,1)S(1)}, bf16[512,512]{1,0:T(8,128)(2,1)}, u32[]{:S(2)}) copy-start(bf16[512,512]{1,0:T(8,128)(2,1)} %wk_ref.5) | copy-start | bytes 1572868
  17.0 64.9 %collective-permute-start.2 = (bf16[224,512]{1,0:T(8,128)(2,1)}, bf16[224,512]{1,0:T(8,128)(2,1)S(1)}, u32[]{:S(2)}, u32[]{:S(2)}) collective-permute-start(bf16[224,512]{1,0:T(8,128)(2,1)} %bitcast.17), channel_id=1, source_target_pairs={{0,1},{1,0},{2,3},{3,2},{4,5},{5,4},{6,7},{7,6},{8,9},{9,8},{10,11... | collective-permute-start | bytes 688136 | tf_op jit(solution)/shard_map/ppermute | solution.py:746
  18.1 63.9 %collective-permute-start.3 = (bf16[224,512]{1,0:T(8,128)(2,1)}, bf16[224,512]{1,0:T(8,128)(2,1)}, u32[]{:S(2)}, u32[]{:S(2)}) collective-permute-start(bf16[224,512]{1,0:T(8,128)(2,1)} %bitcast.18), channel_id=1, source_target_pairs={{1,2},{2,1},{3,4},{4,3},{5,6},{6,5},{7,8},{8,7},{9,10},{10,9},{11,... | collective-permute-start | bytes 688136 | tf_op jit(solution)/shard_map/ppermute | solution.py:746
  24.5 1.0 copy-start.17
  25.6 1.0 copy-start.24
  26.6 1.2 copy-start.34
  27.8 33.3 %copy-start.27 = (s32[7,16,2]{1,2,0:T(2,128)S(1)}, s32[7,16,2]{1,2,0:T(2,128)}, u32[]{:S(2)}) copy-start(s32[7,16,2]{1,2,0:T(2,128)} %param.26) | copy-start | bytes 2692
  27.8 33.3 %copy-start.28 = (s32[7,16]{1,0:T(8,128)S(1)}, s32[7,16]{1,0:T(8,128)}, u32[]{:S(2)}) copy-start(s32[7,16]{1,0:T(8,128)} %counts_s.5) | copy-start | bytes 1348
  27.8 33.3 %copy-start.30 = (f32[512]{0:T(512)S(1)}, f32[512]{0:T(512)}, u32[]{:S(2)}) copy-start(f32[512]{0:T(512)} %param.21) | copy-start | bytes 6148
  61.1 16.7 %copy-start.2 = (bf16[16,128,512]{2,1,0:T(8,128)(2,1)}, bf16[16,128,512]{2,1,0:T(8,128)(2,1)S(1)}, u32[]{:S(2)}) copy-start(bf16[16,128,512]{2,1,0:T(8,128)(2,1)S(1)} %all-to-all-done.refs_0_) | copy-start | bytes 6291460
  61.1 20.8 %copy-start.11 = (bf16[4,7,32,512]{3,2,1,0:T(8,128)(2,1)S(1)}, bf16[4,7,32,512]{3,2,1,0:T(8,128)(2,1)}, u32[]{:S(2)}) copy-start(bf16[4,7,32,512]{3,2,1,0:T(8,128)(2,1)} %copy.23) | copy-start | bytes 2752516
  61.1 31.6 %slice-start = ((s8[4718592]{0:T(1024)(128)(4,1)}), s8[4194304]{0:T(1024)(128)(4,1)S(1)}, s32[]{:S(2)}) async-start(s8[4718592]{0:T(1024)(128)(4,1)} %bitcast.38), calls=%async_computation.2 | async-start | bytes 8388608
  77.8 31.6 %copy-start.22 = (bf16[4,7,32,512]{3,2,1,0:T(8,128)(2,1)}, bf16[4,7,32,512]{3,2,1,0:T(8,128)(2,1)S(1)}, u32[]{:S(2)}) copy-start(bf16[4,7,32,512]{3,2,1,0:T(8,128)(2,1)S(1)} %get-tuple-element.75) | copy-start | bytes 2752516
  77.8 40.9 %copy-start = (bf16[7,4,384,256]{3,2,1,0:T(8,128)(2,1)}, bf16[7,4,384,256]{3,2,1,0:T(8,128)(2,1)S(1)}, u32[]{:S(2)}) copy-start(bf16[7,4,384,256]{3,2,1,0:T(8,128)(2,1)S(1)} %get-tuple-element.71.e_ref) | copy-start | bytes 16515076
  77.8 40.9 %copy-start.7 = (bf16[7,256,512]{2,1,0:T(8,128)(2,1)}, bf16[7,256,512]{2,1,0:T(8,128)(2,1)S(1)}, u32[]{:S(2)}) copy-start(bf16[7,256,512]{2,1,0:T(8,128)(2,1)S(1)} %get-tuple-element.83.kf_ref) | copy-start | bytes 5505028
  77.8 40.9 %copy-start.12 = (bf16[7,128,512]{2,1,0:T(8,128)(2,1)}, bf16[7,128,512]{2,1,0:T(8,128)(2,1)S(1)}, u32[]{:S(2)}) copy-start(bf16[7,128,512]{2,1,0:T(8,128)(2,1)S(1)} %get-tuple-element.80.mixed_ref) | copy-start | bytes 2752516
  77.8 40.9 %copy-start.20 = (f32[7,128,128]{2,1,0:T(8,128)}, f32[7,128,128]{2,1,0:T(8,128)S(1)}, u32[]{:S(2)}) copy-start(f32[7,128,128]{2,1,0:T(8,128)S(1)} %get-tuple-element.82.col_ref) | copy-start | bytes 1376260
  77.9 14.9 %collective-permute-start = (bf16[224,512]{1,0:T(8,128)(2,1)S(1)}, bf16[224,512]{1,0:T(8,128)(2,1)S(1)}, u32[]{:S(2)}, u32[]{:S(2)}) collective-permute-start(bf16[224,512]{1,0:T(8,128)(2,1)S(1)} %bitcast.63), channel_id=1, source_target_pairs={{0,1},{1,0},{2,3},{3,2},{4,5},{5,4},{6,7},{7,6},{8,9},{9,8},{10,11... | collective-permute-start | bytes 688136 | tf_op jit(solution)/shard_map/ppermute | solution.py:746
  78.1 14.6 %collective-permute-start.1 = (bf16[224,512]{1,0:T(8,128)(2,1)S(1)}, bf16[224,512]{1,0:T(8,128)(2,1)S(1)}, u32[]{:S(2)}, u32[]{:S(2)}) collective-permute-start(bf16[224,512]{1,0:T(8,128)(2,1)S(1)} %bitcast.62), channel_id=1, source_target_pairs={{1,2},{2,1},{3,4},{4,3},{5,6},{6,5},{7,8},{8,7},{9,10},{10,9},{11,... | collective-permute-start | bytes 688136 | tf_op jit(solution)/shard_map/ppermute | solution.py:746
  82.0 2.3 %copy-start.31 = (bf16[3,3,512,512]{3,2,1,0:T(8,128)(2,1)S(1)}, bf16[3,3,512,512]{3,2,1,0:T(8,128)(2,1)}, u32[]{:S(2)}) copy-start(bf16[3,3,512,512]{3,2,1,0:T(8,128)(2,1)} %w_ref.10) | copy-start | bytes 14155780
  84.3 6.6 %copy-start.3 = (bf16[16,128,512]{2,1,0:T(8,128)(2,1)S(1)}, bf16[16,128,512]{2,1,0:T(8,128)(2,1)}, u32[]{:S(2)}) copy-start(bf16[16,128,512]{2,1,0:T(8,128)(2,1)} %copy-done.2) | copy-start | bytes 6291460
  84.3 8.4 %slice-start.1 = ((s8[4718592]{0:T(1024)(128)(4,1)}), s8[524288]{0:T(1024)(128)(4,1)S(1)}, s32[]{:S(2)}) async-start(s8[4718592]{0:T(1024)(128)(4,1)} %bitcast.38), calls=%async_computation.3 | async-start | bytes 1048576
  90.9 1.8 copy-start.37
  101.0 8.2 %collective-permute-start.4 = (bf16[224,512]{1,0:T(8,128)(2,1)S(1)}, bf16[224,512]{1,0:T(8,128)(2,1)S(1)}, u32[]{:S(2)}, u32[]{:S(2)}) collective-permute-start(bf16[224,512]{1,0:T(8,128)(2,1)S(1)} %get-tuple-element.67), channel_id=1, source_target_pairs={{0,1},{1,0},{2,3},{3,2},{4,5},{5,4},{6,7},{7,6},{8,9},{9,8},{10,11... | collective-permute-start | bytes 688136 | tf_op jit(solution)/shard_map/ppermute | solution.py:746
  101.0 8.3 %collective-permute-start.5 = (bf16[224,512]{1,0:T(8,128)(2,1)S(1)}, bf16[224,512]{1,0:T(8,128)(2,1)S(1)}, u32[]{:S(2)}, u32[]{:S(2)}) collective-permute-start(bf16[224,512]{1,0:T(8,128)(2,1)S(1)} %get-tuple-element.68), channel_id=1, source_target_pairs={{1,2},{2,1},{3,4},{4,3},{5,6},{6,5},{7,8},{8,7},{9,10},{10,9},{11,... | collective-permute-start | bytes 688136 | tf_op jit(solution)/shard_map/ppermute | solution.py:746
  104.2 5.2 %copy-start.16 = (bf16[512,512]{1,0:T(8,128)(2,1)S(1)}, bf16[512,512]{1,0:T(8,128)(2,1)}, u32[]{:S(2)}) copy-start(bf16[512,512]{1,0:T(8,128)(2,1)} %wo_ref.1) | copy-start | bytes 1572868
  112.6 1.3 copy-start.18
  113.8 18.5 %copy-start.14 = (bf16[896,512]{1,0:T(8,128)(2,1)}, bf16[896,512]{1,0:T(8,128)(2,1)S(1)}, u32[]{:S(2)}) copy-start(bf16[896,512]{1,0:T(8,128)(2,1)S(1)} %get-tuple-element.79) | copy-start | bytes 2752516
  113.8 18.6 %collective-permute-start.6 = (bf16[224,512]{1,0:T(8,128)(2,1)S(1)}, bf16[224,512]{1,0:T(8,128)(2,1)S(1)}, u32[]{:S(2)}, u32[]{:S(2)}) collective-permute-start(bf16[224,512]{1,0:T(8,128)(2,1)S(1)} %get-tuple-element.85), channel_id=1, source_target_pairs={{0,1},{1,0},{2,3},{3,2},{4,5},{5,4},{6,7},{7,6},{8,9},{9,8},{10,11... | collective-permute-start | bytes 688136 | tf_op jit(solution)/shard_map/ppermute | solution.py:746
  115.8 16.6 %collective-permute-start.7 = (bf16[224,512]{1,0:T(8,128)(2,1)S(1)}, bf16[224,512]{1,0:T(8,128)(2,1)S(1)}, u32[]{:S(2)}, u32[]{:S(2)}) collective-permute-start(bf16[224,512]{1,0:T(8,128)(2,1)S(1)} %get-tuple-element.86), channel_id=1, source_target_pairs={{1,2},{2,1},{3,4},{4,3},{5,6},{6,5},{7,8},{8,7},{9,10},{10,9},{11,... | collective-permute-start | bytes 688136 | tf_op jit(solution)/shard_map/ppermute | solution.py:746
  132.4 5.1 %copy-start.40 = (s32[7]{0:T(128)S(1)}, s32[7]{0:T(128)}, u32[]{:S(2)}) copy-start(s32[7]{0:T(128)} %match_s.1) | copy-start | bytes 88
  133.1 51.9 %all-to-all-start.1 = ((bf16[16,128,512]{2,1,0:T(8,128)(2,1)}), bf16[16,128,512]{2,1,0:T(8,128)(2,1)}, u32[]{:S(2)}, u32[]{:S(2)}) async-start(bf16[16,128,512]{2,1,0:T(8,128)(2,1)} %far_grads.1), calls=%async_computation.1 | async-start | bytes 4194304 | tf_op jit(solution)/shard_map/all_to_all | solution.py:828
  137.6 2.6 %copy-start.1 = (bf16[7,4,384,256]{3,2,1,0:T(8,128)(2,1)S(1)}, bf16[7,4,384,256]{3,2,1,0:T(8,128)(2,1)}, u32[]{:S(2)}) copy-start(bf16[7,4,384,256]{3,2,1,0:T(8,128)(2,1)} %copy-done) | copy-start | bytes 16515076
  140.2 1.5 copy-start.8
  141.7 1.2 copy-start.13
  142.8 1.2 copy-start.15
  145.0 1.0 copy-start.25
  146.1 17.1 %copy-start.23 = (bf16[4,7,32,512]{3,2,1,0:T(8,128)(2,1)S(1)}, bf16[4,7,32,512]{3,2,1,0:T(8,128)(2,1)}, u32[]{:S(2)}) copy-start(bf16[4,7,32,512]{3,2,1,0:T(8,128)(2,1)} %copy-done.22) | copy-start | bytes 2752516
  146.1 17.1 %copy-start.36 = (bf16[224,512]{1,0:T(8,128)(2,1)S(1)}, bf16[224,512]{1,0:T(8,128)(2,1)}, u32[]{:S(2)}) copy-start(bf16[224,512]{1,0:T(8,128)(2,1)} %copy-done.35) | copy-start | bytes 688132
  146.1 17.1 %copy-start.39 = (bf16[896,512]{1,0:T(8,128)(2,1)S(1)}, bf16[896,512]{1,0:T(8,128)(2,1)}, u32[]{:S(2)}) copy-start(bf16[896,512]{1,0:T(8,128)(2,1)} %copy-done.38) | copy-start | bytes 2752516
  163.2 2.3 %copy-start.32 = (bf16[3,3,512,512]{3,2,1,0:T(8,128)(2,1)S(1)}, bf16[3,3,512,512]{3,2,1,0:T(8,128)(2,1)}, u32[]{:S(2)}) copy-start(bf16[3,3,512,512]{3,2,1,0:T(8,128)(2,1)} %w_ref.10) | copy-start | bytes 14155780
  165.5 19.5 %copy-start.9 = (f32[7,128,512]{2,1,0:T(8,128)S(1)}, f32[7,128,512]{2,1,0:T(8,128)}, u32[]{:S(2)}) copy-start(f32[7,128,512]{2,1,0:T(8,128)} %own_grads.1.rows_ref) | copy-start | bytes 5505028
  165.5 19.5 %copy-start.29 = (f32[512]{0:T(512)S(1)}, f32[512]{0:T(512)}, u32[]{:S(2)}) copy-start(f32[512]{0:T(512)} %param.16) | copy-start | bytes 6148
  171.1 13.9 %copy-start.5 = (bf16[7,32,4,512]{3,1,0,2:T(8,128)(2,1)S(1)}, bf16[7,32,4,512]{3,1,0,2:T(8,128)(2,1)}, u32[]{:S(2)}) copy-start(bf16[7,32,4,512]{3,1,0,2:T(8,128)(2,1)} %copy-done.4) | copy-start | bytes 2752516
  185.0 1.5 copy-start.19
  (5 other events, 4.3 us)

commit v5 on v4

--- a/solution.py
+++ b/solution.py
@@ -811,7 +811,8 @@
         (flat_bf, edge_bf, edge_bf, flat_bf, edge_bf, edge_bf), nr, False,
     )
     d_near, d_far = exchange_edges(d_near, d_far)
-    vf = far_values(arrived.reshape(-1, width), w_value)
+    d_conv, fetched = lax.optimization_barrier((d_conv, arrived))
+    vf = far_values(fetched.reshape(-1, width), w_value)
     y_grad = grad_main(d_conv, conv_first, views * nr)
     d_near, d_far, vf, y_grad = lax.optimization_barrier((d_near, d_far, vf, y_grad))
     vf = vf.reshape(arrived.shape)

time: 193 us -> 192 us (level)
  transfers between devices with their start and end apart: 10 -> 10, of which waited for: 3 -> 2; matrix products, arithmetic and copies ran while one was open for 5% -> 5% of each run, Pallas kernels for 38% -> 38%
where the time goes in v5:
time: 192 us; the launch traced here: 191 us
  Pallas kernels  90.7 us (47%)
  waiting for transfers between devices  39.5 us (21%)
  local copies, waits for them, and re-layouts  33.6 us (18%)
  starting transfers between devices  25.6 us (13%)
    all_to_all x1, waiting for transfers between devices, local(): lax.all_to_all(send, 'cols', split_axis=0, concat_axis=0, tiled=True)  27.3 us
    unnamed x90, local copies, waits for them, and re-layouts  26 us
    pallas_call x3, Pallas kernels, conv_call(): pl.pallas_call(functools.partial(conv_kernel, body, len(extra), transpose...  19.4 us
    pallas_call x1, Pallas kernels, own_grads(): pl.pallas_call(functools.partial(own_grads_kernel, head, picks), name='ow...  17.2 us
    pallas_call x1, Pallas kernels, attend(): pl.pallas_call(functools.partial(attend_kernel, head, picks), name='atten...  16.6 us
    pallas_call x1, Pallas kernels, far_grads(): pl.pallas_call(functools.partial(far_grads_kernel, head, picks), name='fa...  13.6 us
    ppermute x4, starting transfers between devices, exchange_edges(): lax.ppermute(farther, 'cols', outer)  13.4 us
    all_to_all x1, waiting for transfers between devices, local(): lax.all_to_all(send_back, 'cols', split_axis=0, concat_axis=0, tiled=True)  12.1 us
  transfers between devices with their start and end apart: 10, of which 2 were waited for; matrix products, arithmetic and copies ran while one was open for 5% of the time, Pallas kernels for 38%

profile of v5, /device:TPU:13, one launch (start us, length us, event | category | flops | bytes accessed | tf_op | source)
XLA Modules:
  0.0 190.7 jit_solution(10029601442613332356)
XLA Ops:
  0.6 1.4 copy.33
  2.0 0.7 copy-done.26
  2.7 3.4 %prep.1 = (bf16[7,128,512]{2,1,0:T(8,128)(2,1)S(1)}, bf16[16,128,512]{2,1,0:T(8,128)(2,1)}) custom-call(s32[1]{0:T(128)} %bitcast.own_s, s32[7]{0:T(128)} %match_s.1, s32[7,2,16]{2,1,0:T(2,128)S(1)} %bitcast.51, s32[7,16]{1,0:T(8,128)} %counts_s.5, bf16[4,7,32,512]{3,2,1,0:T(8,128)(2,1)S(1)} %bitcast.35, f32[1,512]{1,0:T(1,128)} %bitcast.56), custom_call_target="tpu_custom_call" | custom-call | tf_op jit(solution)/shard_map/prep/pallas_call | solution.py:98
  6.2 0.9 copy-done.33
  7.1 6.6 %all-to-all-start = ((bf16[16,128,512]{2,1,0:T(8,128)(2,1)}), bf16[16,128,512]{2,1,0:T(8,128)(2,1)S(1)}, u32[]{:S(2)}, u32[]{:S(2)}) async-start(bf16[16,128,512]{2,1,0:T(8,128)(2,1)} %get-tuple-element.51), calls=%async_computation | async-start | bytes 4194304 | tf_op jit(solution)/shard_map/all_to_all | solution.py:788
  13.7 2.6 %constant_dynamic-slice_fusion = (bf16[7,32,1,512]{3,2,1,0:T(2,128)(2,1)S(1)}, bf16[7,32,1,512]{3,2,1,0:T(2,128)(2,1)S(1)}) fusion(bf16[7,32,4,512]{3,2,1,0:T(4,128)(2,1)} %param.15, s32[]{:T(128)S(6)} %select_n.20, s32[]{:T(128)S(6)} %select_n.19), kind=kLoop, calls=%fused_computation.4 | loop fusion | bytes 917512 | tf_op jit(solution)/shard_map/dynamic-slice.1
  16.3 0.7 copy.28
  17.0 0.4 collective-permute-start.2
  17.4 0.7 copy.29
  18.1 3.1 %collective-permute-start.3 = (bf16[224,512]{1,0:T(8,128)(2,1)}, bf16[224,512]{1,0:T(8,128)(2,1)}, u32[]{:S(2)}, u32[]{:S(2)}) collective-permute-start(bf16[224,512]{1,0:T(8,128)(2,1)} %bitcast.18), channel_id=1, source_target_pairs={{1,2},{2,1},{3,4},{4,3},{5,6},{6,5},{7,8},{8,7},{9,10},{10,9},{11,... | collective-permute-start | bytes 688136 | tf_op jit(solution)/shard_map/ppermute | solution.py:746
  21.2 1.0 copy.22
  22.2 2.3 %copy.23 = bf16[4,7,32,512]{3,2,1,0:T(8,128)(2,1)} copy(bf16[4,7,32,512]{3,0,2,1:T(4,128)(2,1)} %bitcast.68) | data formatting | bytes 1835008 | tf_op jit(solution)/shard_map/transpose | solution.py:780
  24.5 1.0 copy-done.17
  25.6 1.0 copy-done.24
  26.6 1.2 copy-done.34
  27.8 6.0 %project.1 = (bf16[896,512]{1,0:T(8,128)(2,1)}, bf16[896,512]{1,0:T(8,128)(2,1)}, bf16[896,512]{1,0:T(8,128)(2,1)}, bf16[7,512,128]{2,1,0:T(8,128)(2,1)}, f32[896,512]{1,0:T(8,128)}, /*index=5*/f32[896,512]{1,0:T(8,128)}) custom-call(bf16[896,512]{1,0:T(8,128)(2,1)S(1)} %bitcast.60, bf16[512,512]{1,0:T(8,128)(2,1)S(1)} %copy-done.24, ...), custom_call_target="tpu_custom_call" | custom-call | flops 1879048192 | bytes 9175040 | tf_op jit(solution)/shard_map/project/pallas_call | solution.py:139
  33.8 27.3 %all-to-all-done.refs_0_ = bf16[16,128,512]{2,1,0:T(8,128)(2,1)S(1)} async-done(((bf16[16,128,512]{2,1,0:T(8,128)(2,1)}), bf16[16,128,512]{2,1,0:T(8,128)(2,1)S(1)}, u32[]{:S(2)}, u32[]{:S(2)}) %all-to-all-start) | async-done | bytes 2097184 | tf_op jit(solution)/shard_map/all_to_all | solution.py:788
  61.2 16.6 %attend.1 = (bf16[4,7,32,512]{3,2,1,0:T(8,128)(2,1)S(1)}, bf16[4,7,32,512]{3,2,1,0:T(8,128)(2,1)S(1)}, bf16[7,32,512]{2,1,0:T(8,128)(2,1)S(1)}, bf16[7,32,512]{2...) custom-call(s32[1]{0:T(128)} %bitcast.own_s, ...), custom_call_target="tpu_custom_call" | custom-call | tf_op jit(solution)/shard_map/attend/pallas_call | solution.py:260
  77.9 0.3 collective-permute-start
  78.1 3.8 %collective-permute-start.1 = (bf16[224,512]{1,0:T(8,128)(2,1)S(1)}, bf16[224,512]{1,0:T(8,128)(2,1)S(1)}, u32[]{:S(2)}, u32[]{:S(2)}) collective-permute-start(bf16[224,512]{1,0:T(8,128)(2,1)S(1)} %bitcast.62), channel_id=1, source_target_pairs={{1,2},{2,1},{3,4},{4,3},{5,6},{6,5},{7,8},{8,7},{9,10},{10,9},{11,... | collective-permute-start | bytes 688136 | tf_op jit(solution)/shard_map/ppermute | solution.py:746
  82.0 2.3 %copy-done.31 = bf16[3,3,512,512]{3,2,1,0:T(8,128)(2,1)S(1)} copy-done((bf16[3,3,512,512]{3,2,1,0:T(8,128)(2,1)S(1)}, bf16[3,3,512,512]{3,2,1,0:T(8,128)(2,1)}, u32[]{:S(2)}) %copy-start.31) | copy-done | bytes 4718616
  84.3 6.5 %grad_two.1.refs_0_ = f32[896,512]{1,0:T(8,128)S(1)} custom-call(s32[1]{0:T(128)} %bitcast.own_s, bf16[896,512]{1,0:T(8,128)(2,1)S(1)} %bitcast.40, bf16[224,512]{1,0:T(8,128)(2,1)S(1)} %collective-permute-done.2.near_ref, bf16[224,512]{1,0:T(8,128)(2,1)} %collective-permute-done.3.farther_ref, bf16[3,3,512,512]{3,2,1,0:T(8,128)(2,1)S(1)} %copy-done.31), custom_call_target="tpu_custom_call" | custom-call | flops 4227858432 | bytes 4718592 | tf_op jit(solution)/shard_map/grad_two/pallas_call | solution.py:358
  90.9 7.3 %conv_one.1 = (bf16[896,512]{1,0:T(8,128)(2,1)S(1)}, bf16[224,512]{1,0:T(8,128)(2,1)S(1)}, bf16[224,512]{1,0:T(8,128)(2,1)S(1)}, bf16[896,512]{1,0:T(8,128)(2,1)...) custom-call(s32[1]{0:T(128)} %bitcast.own_s, bf16[896,512]{1,0:T(8,128)(2,1)S(1)} %bitcast.61, ...), custom_call_target="tpu_custom_call" | custom-call | flops 4227858432 | bytes 4718592 | tf_op jit(solution)/shard_map/conv_one/pallas_call | solution.py:358
  98.3 3.1 %collective-permute-start.5 = (bf16[224,512]{1,0:T(8,128)(2,1)S(1)}, bf16[224,512]{1,0:T(8,128)(2,1)S(1)}, u32[]{:S(2)}, u32[]{:S(2)}) collective-permute-start(bf16[224,512]{1,0:T(8,128)(2,1)S(1)} %get-tuple-element.70), channel_id=1, source_target_pairs={{1,2},{2,1},{3,4},{4,3},{5,6},{6,5},{7,8},{8,7},{9,10},{10,9},{11,... | collective-permute-start | bytes 688136 | tf_op jit(solution)/shard_map/ppermute | solution.py:746
  101.5 5.1 %grad_main.1.y_ref = f32[3,896,512]{2,1,0:T(8,128)S(1)} custom-call(bf16[896,512]{1,0:T(8,128)(2,1)S(1)} %get-tuple-element.73.act_ref, bf16[3,3,512,512]{3,2,1,0:T(8,128)(2,1)S(1)} %bitcast.39), custom_call_target="tpu_custom_call" | custom-call | flops 4227858432 | bytes 4718592 | tf_op jit(solution)/shard_map/grad_main/pallas_call | solution.py:463
  106.6 1.8 far_values.1
  108.4 3.4 %grad_tail.1 = (f32[896,512]{1,0:T(8,128)S(1)}, bf16[896,512]{1,0:T(8,128)(2,1)S(1)}) custom-call(s32[1]{0:T(128)} %bitcast.own_s, bf16[224,512]{1,0:T(8,128)(2,1)S(1)} %collective-permute-done.4.near_ref, bf16[224,512]{1,0:T(8,128)(2,1)S(1)} %collective-permute-done.5.farther_ref, bf16[3,3,512,512]{3,2,1,0:T(8,128)(2,1)S(1)} %bitcast.39, ...), custom_call_target="tpu_custom_call" | custom-call | tf_op jit(solution)/shard_map/grad_tail/pallas_call | solution.py:530
  111.8 1.2 copy-done.18
  113.0 0.2 collective-permute-start.6
  113.2 3.3 %collective-permute-start.7 = (bf16[224,512]{1,0:T(8,128)(2,1)S(1)}, bf16[224,512]{1,0:T(8,128)(2,1)S(1)}, u32[]{:S(2)}, u32[]{:S(2)}) collective-permute-start(bf16[224,512]{1,0:T(8,128)(2,1)S(1)} %get-tuple-element.90), channel_id=1, source_target_pairs={{1,2},{2,1},{3,4},{4,3},{5,6},{6,5},{7,8},{8,7},{9,10},{10,9},{11,... | collective-permute-start | bytes 688136 | tf_op jit(solution)/shard_map/ppermute | solution.py:746
  116.6 13.6 %far_grads.1 = bf16[16,128,512]{2,1,0:T(8,128)(2,1)} custom-call(s32[1]{0:T(128)} %bitcast.own_s, s32[7,2,16]{2,1,0:T(2,128)S(1)} %bitcast.53, s32[7,16]{1,0:T(8,128)S(1)} %copy-done.28, bf16[7,128,512]{2,1,0:T(8,128)(2,1)} %bitcast.66, bf16[16,128,512]{2,1,0:T(8,128)(2,1)S(1)} %bitcast.32, bf16[7,4,384,256]{3,2,1,0:T(8,128)(2,1)S(1)} %get-tuple-element.75.e_ref, ...), custom_call_target="tpu_custom_call" | custom-call | tf_op jit(solution)/shard_map/far_grads/pallas_call | solution.py:620
  130.2 0.7 copy-done.35
  130.9 4.8 %all-to-all-start.1 = ((bf16[16,128,512]{2,1,0:T(8,128)(2,1)}), bf16[16,128,512]{2,1,0:T(8,128)(2,1)}, u32[]{:S(2)}, u32[]{:S(2)}) async-start(bf16[16,128,512]{2,1,0:T(8,128)(2,1)} %far_grads.1), calls=%async_computation.1 | async-start | bytes 4194304 | tf_op jit(solution)/shard_map/all_to_all | solution.py:829
  135.8 0.1 fusion
  135.9 2.6 %copy-done.1 = bf16[7,4,384,256]{3,2,1,0:T(8,128)(2,1)S(1)} copy-done((bf16[7,4,384,256]{3,2,1,0:T(8,128)(2,1)S(1)}, bf16[7,4,384,256]{3,2,1,0:T(8,128)(2,1)}, u32[]{:S(2)}) %copy-start.1) | copy-done | bytes 5505048
  138.4 1.5 copy-done.8
  139.9 1.2 copy-done.13
  141.1 1.2 copy-done.15
  142.3 1.0 copy-done.21
  143.3 1.0 copy-done.25
  144.4 17.2 %own_grads.1.rows_ref = f32[7,128,512]{2,1,0:T(8,128)} custom-call(s32[1]{0:T(128)} %bitcast.own_s, s32[7,2,16]{2,1,0:T(2,128)S(1)} %bitcast.55, bf16[7,128,512]{2,1,0:T(8,128)(2,1)} %bitcast.67, bf16[7,128,512]{2,1,0:T(8,128)(2,1)} %bitcast.70, bf16[7,128,512]{2,1,0:T(8,128)(2,1)} %bitcast.74, f32[7,128,512]{2,1,0:T(8,128)} %bitcast.71, ...), custom_call_target="tpu_custom_call" | custom-call | flops 4697620480 | bytes 11010048 | tf_op jit(solution)/shard_map/own_grads/pallas_call | solution.py:677
  161.6 2.3 %copy-done.32 = bf16[3,3,512,512]{3,2,1,0:T(8,128)(2,1)S(1)} copy-done((bf16[3,3,512,512]{3,2,1,0:T(8,128)(2,1)S(1)}, bf16[3,3,512,512]{3,2,1,0:T(8,128)(2,1)}, u32[]{:S(2)}) %copy-start.32) | copy-done | bytes 4718616
  163.9 5.6 %conv_two.1 = bf16[896,512]{1,0:T(8,128)(2,1)S(1)} custom-call(s32[1]{0:T(128)} %bitcast.own_s, bf16[896,512]{1,0:T(8,128)(2,1)S(1)} %copy-done.39, bf16[224,512]{1,0:T(8,128)(2,1)S(1)} %collective-permute-done.6.near_ref, bf16[224,512]{1,0:T(8,128)(2,1)S(1)} %copy-done.36, bf16[3,3,512,512]{3,2,1,0:T(8,128)(2,1)S(1)} %copy-done.32, ...), custom_call_target="tpu_custom_call" | custom-call | flops 4227858432 | bytes 4718592 | tf_op jit(solution)/shard_map/conv_two/pallas_call | solution.py:358
  169.5 1.6 copy.32
  171.1 12.1 %all-to-all-done.1.back_ref = bf16[16,128,512]{2,1,0:T(8,128)(2,1)} async-done(((bf16[16,128,512]{2,1,0:T(8,128)(2,1)}), bf16[16,128,512]{2,1,0:T(8,128)(2,1)}, u32[]{:S(2)}, u32[]{:S(2)}) %all-to-all-start.1) | async-done | bytes 2097184 | tf_op jit(solution)/shard_map/all_to_all | solution.py:829
  183.3 1.5 copy-done.19
  184.8 4.3 %final.1 = bf16[4,7,32,512]{3,2,1,0:T(8,128)(2,1)S(1)} custom-call(s32[16]{0:T(128)S(1)} %broadcast_add_fusion.table_s, bf16[16,128,512]{2,1,0:T(8,128)(2,1)} %all-to-all-done.1.back_ref, f32[7,128,512]{2,1,0:T(8,128)S(1)} %copy-done.9, bf16[4,7,32,512]{3,2,1,0:T(8,128)(2,1)S(1)} %bitcast.37, f32[4,7,32,512]{3,2,1,0:T(8,128)S(1)} %bitcast.47, ...), custom_call_target="tpu_custom_call" | custom-call | tf_op jit(solution)/shard_map/final/pallas_call | solution.py:727
  189.1 1.6 copy.27
  (82 shorter events, 0.3 us)
Async XLA Ops:
  2.0 5.1 %copy-start.4 = (bf16[7,32,4,512]{3,1,0,2:T(8,128)(2,1)}, bf16[7,32,4,512]{3,1,0,2:T(8,128)(2,1)S(1)}, u32[]{:S(2)}) copy-start(bf16[7,32,4,512]{3,1,0,2:T(8,128)(2,1)S(1)} %copy.33) | copy-start | bytes 2752516
  7.1 54.0 %all-to-all-start = ((bf16[16,128,512]{2,1,0:T(8,128)(2,1)}), bf16[16,128,512]{2,1,0:T(8,128)(2,1)S(1)}, u32[]{:S(2)}, u32[]{:S(2)}) async-start(bf16[16,128,512]{2,1,0:T(8,128)(2,1)} %get-tuple-element.51), calls=%async_computation | async-start | bytes 4194304 | tf_op jit(solution)/shard_map/all_to_all | solution.py:788
  13.7 7.6 %copy-start.6 = (bf16[512,512]{1,0:T(8,128)(2,1)S(1)}, bf16[512,512]{1,0:T(8,128)(2,1)}, u32[]{:S(2)}) copy-start(bf16[512,512]{1,0:T(8,128)(2,1)} %wv_ref.2) | copy-start | bytes 1572868
  16.3 8.3 %copy-start.10 = (bf16[512,512]{1,0:T(8,128)(2,1)S(1)}, bf16[512,512]{1,0:T(8,128)(2,1)}, u32[]{:S(2)}) copy-start(bf16[512,512]{1,0:T(8,128)(2,1)} %wk_ref.5) | copy-start | bytes 1572868
  17.0 64.9 %collective-permute-start.2 = (bf16[224,512]{1,0:T(8,128)(2,1)}, bf16[224,512]{1,0:T(8,128)(2,1)S(1)}, u32[]{:S(2)}, u32[]{:S(2)}) collective-permute-start(bf16[224,512]{1,0:T(8,128)(2,1)} %bitcast.17), channel_id=1, source_target_pairs={{0,1},{1,0},{2,3},{3,2},{4,5},{5,4},{6,7},{7,6},{8,9},{9,8},{10,11... | collective-permute-start | bytes 688136 | tf_op jit(solution)/shard_map/ppermute | solution.py:746
  18.1 63.9 %collective-permute-start.3 = (bf16[224,512]{1,0:T(8,128)(2,1)}, bf16[224,512]{1,0:T(8,128)(2,1)}, u32[]{:S(2)}, u32[]{:S(2)}) collective-permute-start(bf16[224,512]{1,0:T(8,128)(2,1)} %bitcast.18), channel_id=1, source_target_pairs={{1,2},{2,1},{3,4},{4,3},{5,6},{6,5},{7,8},{8,7},{9,10},{10,9},{11,... | collective-permute-start | bytes 688136 | tf_op jit(solution)/shard_map/ppermute | solution.py:746
  24.5 1.0 copy-start.17
  25.6 1.0 copy-start.24
  26.6 1.2 copy-start.34
  27.8 33.3 %copy-start.27 = (s32[7,16,2]{1,2,0:T(2,128)S(1)}, s32[7,16,2]{1,2,0:T(2,128)}, u32[]{:S(2)}) copy-start(s32[7,16,2]{1,2,0:T(2,128)} %param.26) | copy-start | bytes 2692
  27.8 33.3 %copy-start.28 = (s32[7,16]{1,0:T(8,128)S(1)}, s32[7,16]{1,0:T(8,128)}, u32[]{:S(2)}) copy-start(s32[7,16]{1,0:T(8,128)} %counts_s.5) | copy-start | bytes 1348
  27.8 33.3 %copy-start.30 = (f32[512]{0:T(512)S(1)}, f32[512]{0:T(512)}, u32[]{:S(2)}) copy-start(f32[512]{0:T(512)} %param.21) | copy-start | bytes 6148
  61.1 16.7 %copy-start.2 = (bf16[16,128,512]{2,1,0:T(8,128)(2,1)}, bf16[16,128,512]{2,1,0:T(8,128)(2,1)S(1)}, u32[]{:S(2)}) copy-start(bf16[16,128,512]{2,1,0:T(8,128)(2,1)S(1)} %all-to-all-done.refs_0_) | copy-start | bytes 6291460
  61.1 20.8 %copy-start.11 = (bf16[4,7,32,512]{3,2,1,0:T(8,128)(2,1)S(1)}, bf16[4,7,32,512]{3,2,1,0:T(8,128)(2,1)}, u32[]{:S(2)}) copy-start(bf16[4,7,32,512]{3,2,1,0:T(8,128)(2,1)} %copy.23) | copy-start | bytes 2752516
  61.1 29.7 %slice-start = ((s8[4718592]{0:T(1024)(128)(4,1)}), s8[4194304]{0:T(1024)(128)(4,1)S(1)}, s32[]{:S(2)}) async-start(s8[4718592]{0:T(1024)(128)(4,1)} %bitcast.38), calls=%async_computation.2 | async-start | bytes 8388608
  77.8 30.6 %copy-start.22 = (bf16[4,7,32,512]{3,2,1,0:T(8,128)(2,1)}, bf16[4,7,32,512]{3,2,1,0:T(8,128)(2,1)S(1)}, u32[]{:S(2)}) copy-start(bf16[4,7,32,512]{3,2,1,0:T(8,128)(2,1)S(1)} %get-tuple-element.79) | copy-start | bytes 2752516
  77.8 38.7 %copy-start = (bf16[7,4,384,256]{3,2,1,0:T(8,128)(2,1)}, bf16[7,4,384,256]{3,2,1,0:T(8,128)(2,1)S(1)}, u32[]{:S(2)}) copy-start(bf16[7,4,384,256]{3,2,1,0:T(8,128)(2,1)S(1)} %get-tuple-element.75.e_ref) | copy-start | bytes 16515076
  77.8 38.7 %copy-start.7 = (bf16[7,256,512]{2,1,0:T(8,128)(2,1)}, bf16[7,256,512]{2,1,0:T(8,128)(2,1)S(1)}, u32[]{:S(2)}) copy-start(bf16[7,256,512]{2,1,0:T(8,128)(2,1)S(1)} %get-tuple-element.87.kf_ref) | copy-start | bytes 5505028
  77.8 38.7 %copy-start.12 = (bf16[7,128,512]{2,1,0:T(8,128)(2,1)}, bf16[7,128,512]{2,1,0:T(8,128)(2,1)S(1)}, u32[]{:S(2)}) copy-start(bf16[7,128,512]{2,1,0:T(8,128)(2,1)S(1)} %get-tuple-element.84.mixed_ref) | copy-start | bytes 2752516
  77.8 38.7 %copy-start.20 = (f32[7,128,128]{2,1,0:T(8,128)}, f32[7,128,128]{2,1,0:T(8,128)S(1)}, u32[]{:S(2)}) copy-start(f32[7,128,128]{2,1,0:T(8,128)S(1)} %get-tuple-element.86.col_ref) | copy-start | bytes 1376260
  77.9 13.0 %collective-permute-start = (bf16[224,512]{1,0:T(8,128)(2,1)S(1)}, bf16[224,512]{1,0:T(8,128)(2,1)S(1)}, u32[]{:S(2)}, u32[]{:S(2)}) collective-permute-start(bf16[224,512]{1,0:T(8,128)(2,1)S(1)} %bitcast.63), channel_id=1, source_target_pairs={{0,1},{1,0},{2,3},{3,2},{4,5},{5,4},{6,7},{7,6},{8,9},{9,8},{10,11... | collective-permute-start | bytes 688136 | tf_op jit(solution)/shard_map/ppermute | solution.py:746
  78.1 12.7 %collective-permute-start.1 = (bf16[224,512]{1,0:T(8,128)(2,1)S(1)}, bf16[224,512]{1,0:T(8,128)(2,1)S(1)}, u32[]{:S(2)}, u32[]{:S(2)}) collective-permute-start(bf16[224,512]{1,0:T(8,128)(2,1)S(1)} %bitcast.62), channel_id=1, source_target_pairs={{1,2},{2,1},{3,4},{4,3},{5,6},{6,5},{7,8},{8,7},{9,10},{10,9},{11,... | collective-permute-start | bytes 688136 | tf_op jit(solution)/shard_map/ppermute | solution.py:746
  82.0 2.3 %copy-start.31 = (bf16[3,3,512,512]{3,2,1,0:T(8,128)(2,1)S(1)}, bf16[3,3,512,512]{3,2,1,0:T(8,128)(2,1)}, u32[]{:S(2)}) copy-start(bf16[3,3,512,512]{3,2,1,0:T(8,128)(2,1)} %w_ref.10) | copy-start | bytes 14155780
  84.3 6.6 %slice-start.1 = ((s8[4718592]{0:T(1024)(128)(4,1)}), s8[524288]{0:T(1024)(128)(4,1)S(1)}, s32[]{:S(2)}) async-start(s8[4718592]{0:T(1024)(128)(4,1)} %bitcast.38), calls=%async_computation.3 | async-start | bytes 1048576
  84.3 6.6 %copy-start.37 = (f32[512]{0:T(512)S(1)}, f32[512]{0:T(512)}, u32[]{:S(2)}) copy-start(f32[512]{0:T(512)} %param.23) | copy-start | bytes 6148
  98.2 8.3 %copy-start.38 = (bf16[896,512]{1,0:T(8,128)(2,1)}, bf16[896,512]{1,0:T(8,128)(2,1)S(1)}, u32[]{:S(2)}) copy-start(bf16[896,512]{1,0:T(8,128)(2,1)S(1)} %get-tuple-element.68.act_ref) | copy-start | bytes 2752516
  98.2 10.1 %collective-permute-start.4 = (bf16[224,512]{1,0:T(8,128)(2,1)S(1)}, bf16[224,512]{1,0:T(8,128)(2,1)S(1)}, u32[]{:S(2)}, u32[]{:S(2)}) collective-permute-start(bf16[224,512]{1,0:T(8,128)(2,1)S(1)} %get-tuple-element.69), channel_id=1, source_target_pairs={{0,1},{1,0},{2,3},{3,2},{4,5},{5,4},{6,7},{7,6},{8,9},{9,8},{10,11... | collective-permute-start | bytes 688136 | tf_op jit(solution)/shard_map/ppermute | solution.py:746
  98.3 10.1 %collective-permute-start.5 = (bf16[224,512]{1,0:T(8,128)(2,1)S(1)}, bf16[224,512]{1,0:T(8,128)(2,1)S(1)}, u32[]{:S(2)}, u32[]{:S(2)}) collective-permute-start(bf16[224,512]{1,0:T(8,128)(2,1)S(1)} %get-tuple-element.70), channel_id=1, source_target_pairs={{1,2},{2,1},{3,4},{4,3},{5,6},{6,5},{7,8},{8,7},{9,10},{10,9},{11,... | collective-permute-start | bytes 688136 | tf_op jit(solution)/shard_map/ppermute | solution.py:746
  101.5 5.1 %copy-start.3 = (bf16[16,128,512]{2,1,0:T(8,128)(2,1)S(1)}, bf16[16,128,512]{2,1,0:T(8,128)(2,1)}, u32[]{:S(2)}) copy-start(bf16[16,128,512]{2,1,0:T(8,128)(2,1)} %copy-done.2) | copy-start | bytes 6291460
  106.6 1.8 copy-start.16
  111.8 1.3 copy-start.18
  113.0 17.2 %copy-start.14 = (bf16[896,512]{1,0:T(8,128)(2,1)}, bf16[896,512]{1,0:T(8,128)(2,1)S(1)}, u32[]{:S(2)}) copy-start(bf16[896,512]{1,0:T(8,128)(2,1)S(1)} %get-tuple-element.83) | copy-start | bytes 2752516
  113.0 17.2 %collective-permute-start.6 = (bf16[224,512]{1,0:T(8,128)(2,1)S(1)}, bf16[224,512]{1,0:T(8,128)(2,1)S(1)}, u32[]{:S(2)}, u32[]{:S(2)}) collective-permute-start(bf16[224,512]{1,0:T(8,128)(2,1)S(1)} %get-tuple-element.89), channel_id=1, source_target_pairs={{0,1},{1,0},{2,3},{3,2},{4,5},{5,4},{6,7},{7,6},{8,9},{9,8},{10,11... | collective-permute-start | bytes 688136 | tf_op jit(solution)/shard_map/ppermute | solution.py:746
  113.2 17.0 %collective-permute-start.7 = (bf16[224,512]{1,0:T(8,128)(2,1)S(1)}, bf16[224,512]{1,0:T(8,128)(2,1)S(1)}, u32[]{:S(2)}, u32[]{:S(2)}) collective-permute-start(bf16[224,512]{1,0:T(8,128)(2,1)S(1)} %get-tuple-element.90), channel_id=1, source_target_pairs={{1,2},{2,1},{3,4},{4,3},{5,6},{6,5},{7,8},{8,7},{9,10},{10,9},{11,... | collective-permute-start | bytes 688136 | tf_op jit(solution)/shard_map/ppermute | solution.py:746
  130.2 5.6 %copy-start.40 = (s32[7]{0:T(128)S(1)}, s32[7]{0:T(128)}, u32[]{:S(2)}) copy-start(s32[7]{0:T(128)} %match_s.1) | copy-start | bytes 88
  130.9 52.3 %all-to-all-start.1 = ((bf16[16,128,512]{2,1,0:T(8,128)(2,1)}), bf16[16,128,512]{2,1,0:T(8,128)(2,1)}, u32[]{:S(2)}, u32[]{:S(2)}) async-start(bf16[16,128,512]{2,1,0:T(8,128)(2,1)} %far_grads.1), calls=%async_computation.1 | async-start | bytes 4194304 | tf_op jit(solution)/shard_map/all_to_all | solution.py:829
  135.9 2.6 %copy-start.1 = (bf16[7,4,384,256]{3,2,1,0:T(8,128)(2,1)S(1)}, bf16[7,4,384,256]{3,2,1,0:T(8,128)(2,1)}, u32[]{:S(2)}) copy-start(bf16[7,4,384,256]{3,2,1,0:T(8,128)(2,1)} %copy-done) | copy-start | bytes 16515076
  138.4 1.5 copy-start.8
  139.9 1.2 copy-start.13
  141.1 1.2 copy-start.15
  144.4 17.2 %copy-start.23 = (bf16[4,7,32,512]{3,2,1,0:T(8,128)(2,1)S(1)}, bf16[4,7,32,512]{3,2,1,0:T(8,128)(2,1)}, u32[]{:S(2)}) copy-start(bf16[4,7,32,512]{3,2,1,0:T(8,128)(2,1)} %copy-done.22) | copy-start | bytes 2752516
  144.4 17.2 %copy-start.36 = (bf16[224,512]{1,0:T(8,128)(2,1)S(1)}, bf16[224,512]{1,0:T(8,128)(2,1)}, u32[]{:S(2)}) copy-start(bf16[224,512]{1,0:T(8,128)(2,1)} %copy-done.35) | copy-start | bytes 688132
  144.4 17.2 %copy-start.39 = (bf16[896,512]{1,0:T(8,128)(2,1)S(1)}, bf16[896,512]{1,0:T(8,128)(2,1)}, u32[]{:S(2)}) copy-start(bf16[896,512]{1,0:T(8,128)(2,1)} %copy-done.38) | copy-start | bytes 2752516
  161.5 2.3 %copy-start.32 = (bf16[3,3,512,512]{3,2,1,0:T(8,128)(2,1)S(1)}, bf16[3,3,512,512]{3,2,1,0:T(8,128)(2,1)}, u32[]{:S(2)}) copy-start(bf16[3,3,512,512]{3,2,1,0:T(8,128)(2,1)} %w_ref.10) | copy-start | bytes 14155780
  163.9 19.4 %copy-start.9 = (f32[7,128,512]{2,1,0:T(8,128)S(1)}, f32[7,128,512]{2,1,0:T(8,128)}, u32[]{:S(2)}) copy-start(f32[7,128,512]{2,1,0:T(8,128)} %own_grads.1.rows_ref) | copy-start | bytes 5505028
  163.9 19.4 %copy-start.29 = (f32[512]{0:T(512)S(1)}, f32[512]{0:T(512)}, u32[]{:S(2)}) copy-start(f32[512]{0:T(512)} %param.16) | copy-start | bytes 6148
  169.5 13.8 %copy-start.5 = (bf16[7,32,4,512]{3,1,0,2:T(8,128)(2,1)S(1)}, bf16[7,32,4,512]{3,1,0,2:T(8,128)(2,1)}, u32[]{:S(2)}) copy-start(bf16[7,32,4,512]{3,1,0,2:T(8,128)(2,1)} %copy-done.4) | copy-start | bytes 2752516
  183.3 1.5 copy-start.19
  (5 other events, 4.4 us)

commit v6 on v5

--- a/solution.py
+++ b/solution.py
@@ -800,7 +800,7 @@
     edge = (views * nr, width)
     near, farther = exchange_edges(near.reshape(edge), farther.reshape(edge))
     (d_act_two,) = conv_call(
-        "grad_two", grad_two_body, own, cot_t.reshape(flat), cot_near, cot_far, conv_second,
+        "grad_two", grad_two_body, own, cot_t.reshape(flat), cot_near, cot_far, hbm(conv_second),
         (), (pltpu.VMEM(flat, F32),), nr, True,
     )
     flat_bf = pltpu.VMEM(flat, BF16)

time: 192 us -> 190 us (0.990)
  local copies, waits for them, and re-layouts: 33.6 us -> 31.3 us
    unnamed x90 -> x88, local copies, waits for them, and re-layouts: 26 us -> 23.7 us
  transfers between devices with their start and end apart: 10 -> 10, of which waited for: 2 -> 2; matrix products, arithmetic and copies ran while one was open for 5% -> 5% of each run, Pallas kernels for 38% -> 39%
where the time goes in v6:
time: 190 us; the launch traced here: 189 us
  Pallas kernels  91.2 us (48%)
  waiting for transfers between devices  39.4 us (21%)
  local copies, waits for them, and re-layouts  31.3 us (16%)
  starting transfers between devices  25.7 us (14%)
    all_to_all x1, waiting for transfers between devices, local(): lax.all_to_all(send, 'cols', split_axis=0, concat_axis=0, tiled=True)  27.3 us
    unnamed x88, local copies, waits for them, and re-layouts  23.7 us
    pallas_call x3, Pallas kernels, conv_call(): pl.pallas_call(functools.partial(conv_kernel, body, len(extra), transpose...  19.9 us
    pallas_call x1, Pallas kernels, own_grads(): pl.pallas_call(functools.partial(own_grads_kernel, head, picks), name='ow...  17.1 us
    pallas_call x1, Pallas kernels, attend(): pl.pallas_call(functools.partial(attend_kernel, head, picks), name='atten...  16.6 us
    pallas_call x1, Pallas kernels, far_grads(): pl.pallas_call(functools.partial(far_grads_kernel, head, picks), name='fa...  13.6 us
    ppermute x4, starting transfers between devices, exchange_edges(): lax.ppermute(farther, 'cols', outer)  13.5 us
    all_to_all x1, waiting for transfers between devices, local(): lax.all_to_all(send_back, 'cols', split_axis=0, concat_axis=0, tiled=True)  12.2 us
  transfers between devices with their start and end apart: 10, of which 2 were waited for; matrix products, arithmetic and copies ran while one was open for 5% of the time, Pallas kernels for 39%

profile of v6, /device:TPU:13, one launch (start us, length us, event | category | flops | bytes accessed | tf_op | source)
XLA Modules:
  0.0 188.9 jit_solution(3990439728568073594)
XLA Ops:
  0.6 1.4 copy.33
  2.0 0.7 copy-done.26
  2.7 3.4 %prep.1 = (bf16[7,128,512]{2,1,0:T(8,128)(2,1)S(1)}, bf16[16,128,512]{2,1,0:T(8,128)(2,1)}) custom-call(s32[1]{0:T(128)} %bitcast.own_s, s32[7]{0:T(128)} %match_s.1, s32[7,2,16]{2,1,0:T(2,128)S(1)} %bitcast.51, s32[7,16]{1,0:T(8,128)} %counts_s.5, bf16[4,7,32,512]{3,2,1,0:T(8,128)(2,1)S(1)} %bitcast.35, f32[1,512]{1,0:T(1,128)} %bitcast.56), custom_call_target="tpu_custom_call" | custom-call | tf_op jit(solution)/shard_map/prep/pallas_call | solution.py:98
  6.2 0.9 copy-done.32
  7.1 6.6 %all-to-all-start = ((bf16[16,128,512]{2,1,0:T(8,128)(2,1)}), bf16[16,128,512]{2,1,0:T(8,128)(2,1)S(1)}, u32[]{:S(2)}, u32[]{:S(2)}) async-start(bf16[16,128,512]{2,1,0:T(8,128)(2,1)} %get-tuple-element.51), calls=%async_computation | async-start | bytes 4194304 | tf_op jit(solution)/shard_map/all_to_all | solution.py:788
  13.7 2.6 %constant_dynamic-slice_fusion = (bf16[7,32,1,512]{3,2,1,0:T(2,128)(2,1)S(1)}, bf16[7,32,1,512]{3,2,1,0:T(2,128)(2,1)S(1)}) fusion(bf16[7,32,4,512]{3,2,1,0:T(4,128)(2,1)} %param.15, s32[]{:T(128)S(6)} %select_n.20, s32[]{:T(128)S(6)} %select_n.19), kind=kLoop, calls=%fused_computation.4 | loop fusion | bytes 917512 | tf_op jit(solution)/shard_map/dynamic-slice.1
  16.3 0.7 copy.28
  17.0 0.4 collective-permute-start.2
  17.4 0.7 copy.29
  18.1 3.1 %collective-permute-start.3 = (bf16[224,512]{1,0:T(8,128)(2,1)}, bf16[224,512]{1,0:T(8,128)(2,1)}, u32[]{:S(2)}, u32[]{:S(2)}) collective-permute-start(bf16[224,512]{1,0:T(8,128)(2,1)} %bitcast.18), channel_id=1, source_target_pairs={{1,2},{2,1},{3,4},{4,3},{5,6},{6,5},{7,8},{8,7},{9,10},{10,9},{11,... | collective-permute-start | bytes 688136 | tf_op jit(solution)/shard_map/ppermute | solution.py:746
  21.3 1.0 copy.22
  22.2 2.3 %copy.23 = bf16[4,7,32,512]{3,2,1,0:T(8,128)(2,1)} copy(bf16[4,7,32,512]{3,0,2,1:T(4,128)(2,1)} %bitcast.68) | data formatting | bytes 1835008 | tf_op jit(solution)/shard_map/transpose | solution.py:780
  24.6 1.0 copy-done.17
  25.6 1.0 copy-done.24
  26.7 1.2 copy-done.33
  27.8 6.0 %project.1 = (bf16[896,512]{1,0:T(8,128)(2,1)}, bf16[896,512]{1,0:T(8,128)(2,1)}, bf16[896,512]{1,0:T(8,128)(2,1)}, bf16[7,512,128]{2,1,0:T(8,128)(2,1)}, f32[896,512]{1,0:T(8,128)}, /*index=5*/f32[896,512]{1,0:T(8,128)}) custom-call(bf16[896,512]{1,0:T(8,128)(2,1)S(1)} %bitcast.60, bf16[512,512]{1,0:T(8,128)(2,1)S(1)} %copy-done.24, ...), custom_call_target="tpu_custom_call" | custom-call | flops 1879048192 | bytes 9175040 | tf_op jit(solution)/shard_map/project/pallas_call | solution.py:139
  33.9 27.3 %all-to-all-done.refs_0_ = bf16[16,128,512]{2,1,0:T(8,128)(2,1)S(1)} async-done(((bf16[16,128,512]{2,1,0:T(8,128)(2,1)}), bf16[16,128,512]{2,1,0:T(8,128)(2,1)S(1)}, u32[]{:S(2)}, u32[]{:S(2)}) %all-to-all-start) | async-done | bytes 2097184 | tf_op jit(solution)/shard_map/all_to_all | solution.py:788
  61.2 16.6 %attend.1 = (bf16[4,7,32,512]{3,2,1,0:T(8,128)(2,1)S(1)}, bf16[4,7,32,512]{3,2,1,0:T(8,128)(2,1)S(1)}, bf16[7,32,512]{2,1,0:T(8,128)(2,1)S(1)}, bf16[7,32,512]{2...) custom-call(s32[1]{0:T(128)} %bitcast.own_s, ...), custom_call_target="tpu_custom_call" | custom-call | tf_op jit(solution)/shard_map/attend/pallas_call | solution.py:260
  77.9 0.3 collective-permute-start
  78.1 3.8 %collective-permute-start.1 = (bf16[224,512]{1,0:T(8,128)(2,1)S(1)}, bf16[224,512]{1,0:T(8,128)(2,1)S(1)}, u32[]{:S(2)}, u32[]{:S(2)}) collective-permute-start(bf16[224,512]{1,0:T(8,128)(2,1)S(1)} %bitcast.62), channel_id=1, source_target_pairs={{1,2},{2,1},{3,4},{4,3},{5,6},{6,5},{7,8},{8,7},{9,10},{10,9},{11,... | collective-permute-start | bytes 688136 | tf_op jit(solution)/shard_map/ppermute | solution.py:746
  82.0 7.0 %grad_two.1.refs_0_ = f32[896,512]{1,0:T(8,128)S(1)} custom-call(s32[1]{0:T(128)} %bitcast.own_s, bf16[896,512]{1,0:T(8,128)(2,1)S(1)} %bitcast.40, bf16[224,512]{1,0:T(8,128)(2,1)S(1)} %collective-permute-done.2.near_ref, bf16[224,512]{1,0:T(8,128)(2,1)} %collective-permute-done.3.farther_ref, bf16[3,3,512,512]{3,2,1,0:T(8,128)(2,1)} %w_ref.10), custom_call_target="tpu_custom_call" | custom-call | flops 4227858432 | bytes 4718592 | tf_op jit(solution)/shard_map/grad_two/pallas_call | solution.py:358
  89.1 7.3 %conv_one.1 = (bf16[896,512]{1,0:T(8,128)(2,1)S(1)}, bf16[224,512]{1,0:T(8,128)(2,1)S(1)}, bf16[224,512]{1,0:T(8,128)(2,1)S(1)}, bf16[896,512]{1,0:T(8,128)(2,1)...) custom-call(s32[1]{0:T(128)} %bitcast.own_s, bf16[896,512]{1,0:T(8,128)(2,1)S(1)} %bitcast.61, ...), custom_call_target="tpu_custom_call" | custom-call | flops 4227858432 | bytes 4718592 | tf_op jit(solution)/shard_map/conv_one/pallas_call | solution.py:358
  96.4 0.1 collective-permute-start.4
  96.5 3.3 %collective-permute-start.5 = (bf16[224,512]{1,0:T(8,128)(2,1)S(1)}, bf16[224,512]{1,0:T(8,128)(2,1)S(1)}, u32[]{:S(2)}, u32[]{:S(2)}) collective-permute-start(bf16[224,512]{1,0:T(8,128)(2,1)S(1)} %get-tuple-element.70), channel_id=1, source_target_pairs={{1,2},{2,1},{3,4},{4,3},{5,6},{6,5},{7,8},{8,7},{9,10},{10,9},{11,... | collective-permute-start | bytes 688136 | tf_op jit(solution)/shard_map/ppermute | solution.py:746
  99.8 5.1 %grad_main.1.y_ref = f32[3,896,512]{2,1,0:T(8,128)S(1)} custom-call(bf16[896,512]{1,0:T(8,128)(2,1)S(1)} %get-tuple-element.73.act_ref, bf16[3,3,512,512]{3,2,1,0:T(8,128)(2,1)S(1)} %bitcast.39), custom_call_target="tpu_custom_call" | custom-call | flops 4227858432 | bytes 4718592 | tf_op jit(solution)/shard_map/grad_main/pallas_call | solution.py:463
  104.9 1.8 far_values.1
  106.8 3.4 %grad_tail.1 = (f32[896,512]{1,0:T(8,128)S(1)}, bf16[896,512]{1,0:T(8,128)(2,1)S(1)}) custom-call(s32[1]{0:T(128)} %bitcast.own_s, bf16[224,512]{1,0:T(8,128)(2,1)S(1)} %collective-permute-done.4.near_ref, bf16[224,512]{1,0:T(8,128)(2,1)S(1)} %collective-permute-done.5.farther_ref, bf16[3,3,512,512]{3,2,1,0:T(8,128)(2,1)S(1)} %bitcast.39, ...), custom_call_target="tpu_custom_call" | custom-call | tf_op jit(solution)/shard_map/grad_tail/pallas_call | solution.py:530
  110.1 1.2 copy-done.18
  111.4 0.0 collective-permute-start.6
  111.4 3.3 %collective-permute-start.7 = (bf16[224,512]{1,0:T(8,128)(2,1)S(1)}, bf16[224,512]{1,0:T(8,128)(2,1)S(1)}, u32[]{:S(2)}, u32[]{:S(2)}) collective-permute-start(bf16[224,512]{1,0:T(8,128)(2,1)S(1)} %get-tuple-element.90), channel_id=1, source_target_pairs={{1,2},{2,1},{3,4},{4,3},{5,6},{6,5},{7,8},{8,7},{9,10},{10,9},{11,... | collective-permute-start | bytes 688136 | tf_op jit(solution)/shard_map/ppermute | solution.py:746
  114.7 13.6 %far_grads.1 = bf16[16,128,512]{2,1,0:T(8,128)(2,1)} custom-call(s32[1]{0:T(128)} %bitcast.own_s, s32[7,2,16]{2,1,0:T(2,128)S(1)} %bitcast.53, s32[7,16]{1,0:T(8,128)S(1)} %copy-done.28, bf16[7,128,512]{2,1,0:T(8,128)(2,1)} %bitcast.66, bf16[16,128,512]{2,1,0:T(8,128)(2,1)S(1)} %bitcast.32, bf16[7,4,384,256]{3,2,1,0:T(8,128)(2,1)S(1)} %get-tuple-element.75.e_ref, ...), custom_call_target="tpu_custom_call" | custom-call | tf_op jit(solution)/shard_map/far_grads/pallas_call | solution.py:620
  128.4 0.7 copy-done.34
  129.1 4.9 %all-to-all-start.1 = ((bf16[16,128,512]{2,1,0:T(8,128)(2,1)}), bf16[16,128,512]{2,1,0:T(8,128)(2,1)}, u32[]{:S(2)}, u32[]{:S(2)}) async-start(bf16[16,128,512]{2,1,0:T(8,128)(2,1)} %far_grads.1), calls=%async_computation.1 | async-start | bytes 4194304 | tf_op jit(solution)/shard_map/all_to_all | solution.py:829
  133.9 0.1 fusion
  134.1 2.6 %copy-done.1 = bf16[7,4,384,256]{3,2,1,0:T(8,128)(2,1)S(1)} copy-done((bf16[7,4,384,256]{3,2,1,0:T(8,128)(2,1)S(1)}, bf16[7,4,384,256]{3,2,1,0:T(8,128)(2,1)}, u32[]{:S(2)}) %copy-start.1) | copy-done | bytes 5505048
  136.6 1.5 copy-done.8
  138.1 1.2 copy-done.13
  139.3 1.2 copy-done.15
  140.5 1.0 copy-done.21
  141.5 1.0 copy-done.25
  142.5 17.1 %own_grads.1.rows_ref = f32[7,128,512]{2,1,0:T(8,128)} custom-call(s32[1]{0:T(128)} %bitcast.own_s, s32[7,2,16]{2,1,0:T(2,128)S(1)} %bitcast.55, bf16[7,128,512]{2,1,0:T(8,128)(2,1)} %bitcast.67, bf16[7,128,512]{2,1,0:T(8,128)(2,1)} %bitcast.70, bf16[7,128,512]{2,1,0:T(8,128)(2,1)} %bitcast.74, f32[7,128,512]{2,1,0:T(8,128)} %bitcast.71, ...), custom_call_target="tpu_custom_call" | custom-call | flops 4697620480 | bytes 11010048 | tf_op jit(solution)/shard_map/own_grads/pallas_call | solution.py:677
  159.7 2.3 %copy-done.31 = bf16[3,3,512,512]{3,2,1,0:T(8,128)(2,1)S(1)} copy-done((bf16[3,3,512,512]{3,2,1,0:T(8,128)(2,1)S(1)}, bf16[3,3,512,512]{3,2,1,0:T(8,128)(2,1)}, u32[]{:S(2)}) %copy-start.31) | copy-done | bytes 4718616
  162.0 5.6 %conv_two.1 = bf16[896,512]{1,0:T(8,128)(2,1)S(1)} custom-call(s32[1]{0:T(128)} %bitcast.own_s, bf16[896,512]{1,0:T(8,128)(2,1)S(1)} %copy-done.38, bf16[224,512]{1,0:T(8,128)(2,1)S(1)} %collective-permute-done.6.near_ref, bf16[224,512]{1,0:T(8,128)(2,1)S(1)} %copy-done.35, bf16[3,3,512,512]{3,2,1,0:T(8,128)(2,1)S(1)} %copy-done.31, ...), custom_call_target="tpu_custom_call" | custom-call | flops 4227858432 | bytes 4718592 | tf_op jit(solution)/shard_map/conv_two/pallas_call | solution.py:358
  167.7 1.6 copy.32
  169.3 12.2 %all-to-all-done.1.back_ref = bf16[16,128,512]{2,1,0:T(8,128)(2,1)} async-done(((bf16[16,128,512]{2,1,0:T(8,128)(2,1)}), bf16[16,128,512]{2,1,0:T(8,128)(2,1)}, u32[]{:S(2)}, u32[]{:S(2)}) %all-to-all-start.1) | async-done | bytes 2097184 | tf_op jit(solution)/shard_map/all_to_all | solution.py:829
  181.5 1.5 copy-done.19
  183.0 4.3 %final.1 = bf16[4,7,32,512]{3,2,1,0:T(8,128)(2,1)S(1)} custom-call(s32[16]{0:T(128)S(1)} %broadcast_add_fusion.table_s, bf16[16,128,512]{2,1,0:T(8,128)(2,1)} %all-to-all-done.1.back_ref, f32[7,128,512]{2,1,0:T(8,128)S(1)} %copy-done.9, bf16[4,7,32,512]{3,2,1,0:T(8,128)(2,1)S(1)} %bitcast.37, f32[4,7,32,512]{3,2,1,0:T(8,128)S(1)} %bitcast.47, ...), custom_call_target="tpu_custom_call" | custom-call | tf_op jit(solution)/shard_map/final/pallas_call | solution.py:727
  187.2 1.6 copy.27
  (80 shorter events, 0.2 us)
Async XLA Ops:
  2.0 5.1 %copy-start.4 = (bf16[7,32,4,512]{3,1,0,2:T(8,128)(2,1)}, bf16[7,32,4,512]{3,1,0,2:T(8,128)(2,1)S(1)}, u32[]{:S(2)}) copy-start(bf16[7,32,4,512]{3,1,0,2:T(8,128)(2,1)S(1)} %copy.33) | copy-start | bytes 2752516
  7.1 54.0 %all-to-all-start = ((bf16[16,128,512]{2,1,0:T(8,128)(2,1)}), bf16[16,128,512]{2,1,0:T(8,128)(2,1)S(1)}, u32[]{:S(2)}, u32[]{:S(2)}) async-start(bf16[16,128,512]{2,1,0:T(8,128)(2,1)} %get-tuple-element.51), calls=%async_computation | async-start | bytes 4194304 | tf_op jit(solution)/shard_map/all_to_all | solution.py:788
  13.7 7.6 %copy-start.6 = (bf16[512,512]{1,0:T(8,128)(2,1)S(1)}, bf16[512,512]{1,0:T(8,128)(2,1)}, u32[]{:S(2)}) copy-start(bf16[512,512]{1,0:T(8,128)(2,1)} %wv_ref.2) | copy-start | bytes 1572868
  16.3 8.3 %copy-start.10 = (bf16[512,512]{1,0:T(8,128)(2,1)S(1)}, bf16[512,512]{1,0:T(8,128)(2,1)}, u32[]{:S(2)}) copy-start(bf16[512,512]{1,0:T(8,128)(2,1)} %wk_ref.5) | copy-start | bytes 1572868
  17.0 64.9 %collective-permute-start.2 = (bf16[224,512]{1,0:T(8,128)(2,1)}, bf16[224,512]{1,0:T(8,128)(2,1)S(1)}, u32[]{:S(2)}, u32[]{:S(2)}) collective-permute-start(bf16[224,512]{1,0:T(8,128)(2,1)} %bitcast.17), channel_id=1, source_target_pairs={{0,1},{1,0},{2,3},{3,2},{4,5},{5,4},{6,7},{7,6},{8,9},{9,8},{10,11... | collective-permute-start | bytes 688136 | tf_op jit(solution)/shard_map/ppermute | solution.py:746
  18.1 63.8 %collective-permute-start.3 = (bf16[224,512]{1,0:T(8,128)(2,1)}, bf16[224,512]{1,0:T(8,128)(2,1)}, u32[]{:S(2)}, u32[]{:S(2)}) collective-permute-start(bf16[224,512]{1,0:T(8,128)(2,1)} %bitcast.18), channel_id=1, source_target_pairs={{1,2},{2,1},{3,4},{4,3},{5,6},{6,5},{7,8},{8,7},{9,10},{10,9},{11,... | collective-permute-start | bytes 688136 | tf_op jit(solution)/shard_map/ppermute | solution.py:746
  24.6 1.0 copy-start.17
  25.6 1.0 copy-start.24
  26.6 1.2 copy-start.33
  27.8 33.3 %copy-start.27 = (s32[7,16,2]{1,2,0:T(2,128)S(1)}, s32[7,16,2]{1,2,0:T(2,128)}, u32[]{:S(2)}) copy-start(s32[7,16,2]{1,2,0:T(2,128)} %param.26) | copy-start | bytes 2692
  27.8 33.3 %copy-start.28 = (s32[7,16]{1,0:T(8,128)S(1)}, s32[7,16]{1,0:T(8,128)}, u32[]{:S(2)}) copy-start(s32[7,16]{1,0:T(8,128)} %counts_s.5) | copy-start | bytes 1348
  27.8 33.3 %copy-start.30 = (f32[512]{0:T(512)S(1)}, f32[512]{0:T(512)}, u32[]{:S(2)}) copy-start(f32[512]{0:T(512)} %param.21) | copy-start | bytes 6148
  61.1 16.7 %copy-start.2 = (bf16[16,128,512]{2,1,0:T(8,128)(2,1)}, bf16[16,128,512]{2,1,0:T(8,128)(2,1)S(1)}, u32[]{:S(2)}) copy-start(bf16[16,128,512]{2,1,0:T(8,128)(2,1)S(1)} %all-to-all-done.refs_0_) | copy-start | bytes 6291460
  61.1 20.8 %copy-start.11 = (bf16[4,7,32,512]{3,2,1,0:T(8,128)(2,1)S(1)}, bf16[4,7,32,512]{3,2,1,0:T(8,128)(2,1)}, u32[]{:S(2)}) copy-start(bf16[4,7,32,512]{3,2,1,0:T(8,128)(2,1)} %copy.23) | copy-start | bytes 2752516
  61.1 27.9 %slice-start = ((s8[4718592]{0:T(1024)(128)(4,1)}), s8[4194304]{0:T(1024)(128)(4,1)S(1)}, s32[]{:S(2)}) async-start(s8[4718592]{0:T(1024)(128)(4,1)} %bitcast.38), calls=%async_computation.2 | async-start | bytes 8388608
  77.8 28.9 %copy-start.22 = (bf16[4,7,32,512]{3,2,1,0:T(8,128)(2,1)}, bf16[4,7,32,512]{3,2,1,0:T(8,128)(2,1)S(1)}, u32[]{:S(2)}) copy-start(bf16[4,7,32,512]{3,2,1,0:T(8,128)(2,1)S(1)} %get-tuple-element.79) | copy-start | bytes 2752516
  77.8 36.9 %copy-start = (bf16[7,4,384,256]{3,2,1,0:T(8,128)(2,1)}, bf16[7,4,384,256]{3,2,1,0:T(8,128)(2,1)S(1)}, u32[]{:S(2)}) copy-start(bf16[7,4,384,256]{3,2,1,0:T(8,128)(2,1)S(1)} %get-tuple-element.75.e_ref) | copy-start | bytes 16515076
  77.8 36.9 %copy-start.7 = (bf16[7,256,512]{2,1,0:T(8,128)(2,1)}, bf16[7,256,512]{2,1,0:T(8,128)(2,1)S(1)}, u32[]{:S(2)}) copy-start(bf16[7,256,512]{2,1,0:T(8,128)(2,1)S(1)} %get-tuple-element.87.kf_ref) | copy-start | bytes 5505028
  77.8 36.9 %copy-start.12 = (bf16[7,128,512]{2,1,0:T(8,128)(2,1)}, bf16[7,128,512]{2,1,0:T(8,128)(2,1)S(1)}, u32[]{:S(2)}) copy-start(bf16[7,128,512]{2,1,0:T(8,128)(2,1)S(1)} %get-tuple-element.84.mixed_ref) | copy-start | bytes 2752516
  77.8 36.9 %copy-start.20 = (f32[7,128,128]{2,1,0:T(8,128)}, f32[7,128,128]{2,1,0:T(8,128)S(1)}, u32[]{:S(2)}) copy-start(f32[7,128,128]{2,1,0:T(8,128)S(1)} %get-tuple-element.86.col_ref) | copy-start | bytes 1376260
  77.9 11.2 %collective-permute-start = (bf16[224,512]{1,0:T(8,128)(2,1)S(1)}, bf16[224,512]{1,0:T(8,128)(2,1)S(1)}, u32[]{:S(2)}, u32[]{:S(2)}) collective-permute-start(bf16[224,512]{1,0:T(8,128)(2,1)S(1)} %bitcast.63), channel_id=1, source_target_pairs={{0,1},{1,0},{2,3},{3,2},{4,5},{5,4},{6,7},{7,6},{8,9},{9,8},{10,11... | collective-permute-start | bytes 688136 | tf_op jit(solution)/shard_map/ppermute | solution.py:746
  78.1 10.9 %collective-permute-start.1 = (bf16[224,512]{1,0:T(8,128)(2,1)S(1)}, bf16[224,512]{1,0:T(8,128)(2,1)S(1)}, u32[]{:S(2)}, u32[]{:S(2)}) collective-permute-start(bf16[224,512]{1,0:T(8,128)(2,1)S(1)} %bitcast.62), channel_id=1, source_target_pairs={{1,2},{2,1},{3,4},{4,3},{5,6},{6,5},{7,8},{8,7},{9,10},{10,9},{11,... | collective-permute-start | bytes 688136 | tf_op jit(solution)/shard_map/ppermute | solution.py:746
  82.0 7.1 %slice-start.1 = ((s8[4718592]{0:T(1024)(128)(4,1)}), s8[524288]{0:T(1024)(128)(4,1)S(1)}, s32[]{:S(2)}) async-start(s8[4718592]{0:T(1024)(128)(4,1)} %bitcast.38), calls=%async_computation.3 | async-start | bytes 1048576
  82.0 7.1 %copy-start.36 = (f32[512]{0:T(512)S(1)}, f32[512]{0:T(512)}, u32[]{:S(2)}) copy-start(f32[512]{0:T(512)} %param.23) | copy-start | bytes 6148
  96.4 8.5 %copy-start.37 = (bf16[896,512]{1,0:T(8,128)(2,1)}, bf16[896,512]{1,0:T(8,128)(2,1)S(1)}, u32[]{:S(2)}) copy-start(bf16[896,512]{1,0:T(8,128)(2,1)S(1)} %get-tuple-element.68.act_ref) | copy-start | bytes 2752516
  96.4 10.3 %collective-permute-start.4 = (bf16[224,512]{1,0:T(8,128)(2,1)S(1)}, bf16[224,512]{1,0:T(8,128)(2,1)S(1)}, u32[]{:S(2)}, u32[]{:S(2)}) collective-permute-start(bf16[224,512]{1,0:T(8,128)(2,1)S(1)} %get-tuple-element.69), channel_id=1, source_target_pairs={{0,1},{1,0},{2,3},{3,2},{4,5},{5,4},{6,7},{7,6},{8,9},{9,8},{10,11... | collective-permute-start | bytes 688136 | tf_op jit(solution)/shard_map/ppermute | solution.py:746
  96.5 10.2 %collective-permute-start.5 = (bf16[224,512]{1,0:T(8,128)(2,1)S(1)}, bf16[224,512]{1,0:T(8,128)(2,1)S(1)}, u32[]{:S(2)}, u32[]{:S(2)}) collective-permute-start(bf16[224,512]{1,0:T(8,128)(2,1)S(1)} %get-tuple-element.70), channel_id=1, source_target_pairs={{1,2},{2,1},{3,4},{4,3},{5,6},{6,5},{7,8},{8,7},{9,10},{10,9},{11,... | collective-permute-start | bytes 688136 | tf_op jit(solution)/shard_map/ppermute | solution.py:746
  99.8 5.1 %copy-start.3 = (bf16[16,128,512]{2,1,0:T(8,128)(2,1)S(1)}, bf16[16,128,512]{2,1,0:T(8,128)(2,1)}, u32[]{:S(2)}) copy-start(bf16[16,128,512]{2,1,0:T(8,128)(2,1)} %copy-done.2) | copy-start | bytes 6291460
  104.9 1.8 copy-start.16
  110.1 1.3 copy-start.18
  111.4 17.0 %copy-start.14 = (bf16[896,512]{1,0:T(8,128)(2,1)}, bf16[896,512]{1,0:T(8,128)(2,1)S(1)}, u32[]{:S(2)}) copy-start(bf16[896,512]{1,0:T(8,128)(2,1)S(1)} %get-tuple-element.83) | copy-start | bytes 2752516
  111.4 17.0 %collective-permute-start.6 = (bf16[224,512]{1,0:T(8,128)(2,1)S(1)}, bf16[224,512]{1,0:T(8,128)(2,1)S(1)}, u32[]{:S(2)}, u32[]{:S(2)}) collective-permute-start(bf16[224,512]{1,0:T(8,128)(2,1)S(1)} %get-tuple-element.89), channel_id=1, source_target_pairs={{0,1},{1,0},{2,3},{3,2},{4,5},{5,4},{6,7},{7,6},{8,9},{9,8},{10,11... | collective-permute-start | bytes 688136 | tf_op jit(solution)/shard_map/ppermute | solution.py:746
  111.4 17.0 %collective-permute-start.7 = (bf16[224,512]{1,0:T(8,128)(2,1)S(1)}, bf16[224,512]{1,0:T(8,128)(2,1)S(1)}, u32[]{:S(2)}, u32[]{:S(2)}) collective-permute-start(bf16[224,512]{1,0:T(8,128)(2,1)S(1)} %get-tuple-element.90), channel_id=1, source_target_pairs={{1,2},{2,1},{3,4},{4,3},{5,6},{6,5},{7,8},{8,7},{9,10},{10,9},{11,... | collective-permute-start | bytes 688136 | tf_op jit(solution)/shard_map/ppermute | solution.py:746
  128.3 5.6 %copy-start.39 = (s32[7]{0:T(128)S(1)}, s32[7]{0:T(128)}, u32[]{:S(2)}) copy-start(s32[7]{0:T(128)} %match_s.1) | copy-start | bytes 88
  129.1 52.4 %all-to-all-start.1 = ((bf16[16,128,512]{2,1,0:T(8,128)(2,1)}), bf16[16,128,512]{2,1,0:T(8,128)(2,1)}, u32[]{:S(2)}, u32[]{:S(2)}) async-start(bf16[16,128,512]{2,1,0:T(8,128)(2,1)} %far_grads.1), calls=%async_computation.1 | async-start | bytes 4194304 | tf_op jit(solution)/shard_map/all_to_all | solution.py:829
  134.0 2.6 %copy-start.1 = (bf16[7,4,384,256]{3,2,1,0:T(8,128)(2,1)S(1)}, bf16[7,4,384,256]{3,2,1,0:T(8,128)(2,1)}, u32[]{:S(2)}) copy-start(bf16[7,4,384,256]{3,2,1,0:T(8,128)(2,1)} %copy-done) | copy-start | bytes 16515076
  136.6 1.5 copy-start.8
  138.1 1.2 copy-start.13
  139.3 1.2 copy-start.15
  141.5 1.0 copy-start.25
  142.5 17.2 %copy-start.23 = (bf16[4,7,32,512]{3,2,1,0:T(8,128)(2,1)S(1)}, bf16[4,7,32,512]{3,2,1,0:T(8,128)(2,1)}, u32[]{:S(2)}) copy-start(bf16[4,7,32,512]{3,2,1,0:T(8,128)(2,1)} %copy-done.22) | copy-start | bytes 2752516
  142.5 17.2 %copy-start.35 = (bf16[224,512]{1,0:T(8,128)(2,1)S(1)}, bf16[224,512]{1,0:T(8,128)(2,1)}, u32[]{:S(2)}) copy-start(bf16[224,512]{1,0:T(8,128)(2,1)} %copy-done.34) | copy-start | bytes 688132
  142.5 17.2 %copy-start.38 = (bf16[896,512]{1,0:T(8,128)(2,1)S(1)}, bf16[896,512]{1,0:T(8,128)(2,1)}, u32[]{:S(2)}) copy-start(bf16[896,512]{1,0:T(8,128)(2,1)} %copy-done.37) | copy-start | bytes 2752516
  159.7 2.3 %copy-start.31 = (bf16[3,3,512,512]{3,2,1,0:T(8,128)(2,1)S(1)}, bf16[3,3,512,512]{3,2,1,0:T(8,128)(2,1)}, u32[]{:S(2)}) copy-start(bf16[3,3,512,512]{3,2,1,0:T(8,128)(2,1)} %w_ref.10) | copy-start | bytes 14155780
  162.0 19.4 %copy-start.9 = (f32[7,128,512]{2,1,0:T(8,128)S(1)}, f32[7,128,512]{2,1,0:T(8,128)}, u32[]{:S(2)}) copy-start(f32[7,128,512]{2,1,0:T(8,128)} %own_grads.1.rows_ref) | copy-start | bytes 5505028
  162.0 19.4 %copy-start.29 = (f32[512]{0:T(512)S(1)}, f32[512]{0:T(512)}, u32[]{:S(2)}) copy-start(f32[512]{0:T(512)} %param.16) | copy-start | bytes 6148
  167.7 13.8 %copy-start.5 = (bf16[7,32,4,512]{3,1,0,2:T(8,128)(2,1)S(1)}, bf16[7,32,4,512]{3,1,0,2:T(8,128)(2,1)}, u32[]{:S(2)}) copy-start(bf16[7,32,4,512]{3,1,0,2:T(8,128)(2,1)} %copy-done.4) | copy-start | bytes 2752516
  181.5 1.5 copy-start.19
  (4 other events, 3.4 us)
